TPU v7x, 32 devices: a whole 2x2x4 slice. The times are simulated.
32 devices in a mesh: parts: 2 (over x), gz: 8 (over z, y), gx: 2 (over core).
Axes of the slice: x: 2, y: 2, z: 4, core: 2. Of those that a mesh axis runs over, the one named last changes fastest.
Arguments:
- noise: float32 [512, 2, 16, 2048], P(('parts', 'gz'), None, None, 'gx'), parts along dimension 0, may hold values from -6 to 6
- scale_index: int32 [512, 2], P(('parts', 'gz')), parts along dimension 0, may hold values from 0 to 15
- rates: float32 [16], replicated, may hold values from 0.000390625 to 0.5
- facies_code: int32 [32, 2048], P('parts', 'gx'), parts along dimension 0, may hold values from 0 to 7
- thresholds: float32 [8], replicated, may hold values from -1 to 1
Outputs:
- latent: float32 [512, 2, 16, 2048], P(('parts', 'gz'), None, None, 'gx'), parts along dimension 0
- facies_soft: float32 [512, 16, 2048], P(('parts', 'gz'), None, 'gx'), parts along dimension 0
There are 2 independent parts, one for each index of `parts`. A program takes and returns all parts, laid end to end along the dimension named above; an argument that names none is the same for every part. Nothing has to cross between parts.
All inputs are finite; a program needn't handle non-finite values.
Results may differ from a plain program's by a relative error of at most 0.00021.
Values sent between devices are 32-bit elements; how exact they have to be, the bound alone decides.
No kernel may reach another device: no remote copies, remote signals or barrier semaphores. Data moves between devices by JAX's collectives and lax.ppermute only.
A program may use at most 64 MiB of HBM per device.

v0:
```python
import jax
import jax.numpy as jnp
from jax import lax
from jax.sharding import PartitionSpec as P

SWEEPS = 4


def shifted(value, axis, by):
    length = lax.axis_size(axis)
    pairs = [(i, i + by) for i in range(length) if 0 <= i + by < length]
    return lax.ppermute(value, axis, pairs)


def padded_2(value, sides, width):
    for axis, dim in sides:
        size, length = (lax.axis_size(axis), value.shape[dim])
        up = [(i, (i + 1) % size) for i in range(size - 1)]
        down = [(j, i) for i, j in up]
        last = lax.slice_in_dim(value, length - width, length, axis=dim)
        leading = lax.slice_in_dim(value, 0, width, axis=dim)
        before = lax.ppermute(last, axis, up)
        after = lax.ppermute(leading, axis, down)
        value = jnp.concatenate([before, value, after], axis=dim)
    return value


def lookup(codes, table):
    slots = jnp.arange(table.shape[0], dtype=jnp.int32)
    hits = (codes[..., None] == slots).astype(jnp.float32)
    return jnp.sum(hits * table, axis=-1)


def sweep_once(field, padded):
    rowpad = jnp.pad(field, ((0, 0), (0, 0), (1, 1), (0, 0)))
    lap = padded[..., 2:] + padded[..., :-2] + rowpad[:, :, 2:] + rowpad[:, :, :-2] - 4.0 * field
    return field + 0.2 * lap


def shards(noise, scale_index, rates, facies_code, thresholds):
    alpha = jnp.exp(-lookup(scale_index, rates))
    fwd_gain = jnp.sqrt(1.0 - alpha * alpha)
    bwd_gain = 1.0 - alpha
    start = jnp.zeros(noise.shape[1:], jnp.float32)

    def forward(state, inputs):
        level_alpha, level_gain, level_noise = inputs
        state = level_alpha[:, None, None] * state + level_gain[:, None, None] * level_noise
        return (state, state)

    _, local_fwd = lax.scan(forward, start, (alpha, fwd_gain, noise))
    fwd_factor = jnp.cumprod(alpha, axis=0)
    fwd_total = fwd_factor[-1][:, None, None]
    fwd_last = local_fwd[-1]

    def fwd_step(turn, entering):
        return shifted(fwd_total * entering + fwd_last, "gz", 1)

    fwd_in = lax.fori_loop(0, lax.axis_size("gz") - 1, fwd_step, start)
    filtered = local_fwd + fwd_factor[:, :, None, None] * fwd_in[None]

    def backward(state, inputs):
        level_alpha, level_gain, level_field = inputs
        state = level_alpha[:, None, None] * state + level_gain[:, None, None] * level_field
        return (state, state)

    _, local_bwd = lax.scan(backward, start, (alpha, bwd_gain, filtered), reverse=True)
    bwd_factor = jnp.flip(jnp.cumprod(jnp.flip(alpha, axis=0), axis=0), axis=0)
    bwd_total = bwd_factor[0][:, None, None]
    bwd_first = local_bwd[0]

    def bwd_step(turn, entering):
        return shifted(bwd_total * entering + bwd_first, "gz", -1)

    bwd_in = lax.fori_loop(0, lax.axis_size("gz") - 1, bwd_step, start)
    field = local_bwd + bwd_factor[:, :, None, None] * bwd_in[None]
    for sweep in range(SWEEPS):
        padded = padded_2(field, (("gx", 3),), 1)
        field = sweep_once(field, padded)
    depth_level = lookup(facies_code, thresholds)
    facies_soft = jax.nn.sigmoid(3.0 * (field[:, 0] - depth_level[None])) * jax.nn.sigmoid(
        3.0 * field[:, 1]
    )
    return (field, facies_soft)


def solution(mesh):
    return jax.shard_map(
        shards,
        mesh=mesh,
        in_specs=(
            P(("parts", "gz"), None, None, "gx"),
            P(("parts", "gz"), None),
            P(),
            P("parts", "gx"),
            P(),
        ),
        out_specs=(P(("parts", "gz"), None, None, "gx"), P(("parts", "gz"), None, "gx")),
        check_vma=False,
    )
```

profile of v0, /device:TPU:0, one launch (start us, length us, event | category | flops | bytes accessed | tf_op | source)
XLA Modules:
  0.0 274.3 jit_solution(18082910668739778176)
XLA Ops:
  4.5 53.0 %while.52 = (s32[]{:T(128)}, f32[2,16,1024]{2,1,0:T(8,128)S(1)}, f32[32,2,16,1024]{3,2,1,0:T(8,128)}, f32[32,2]{1,0:T(8,128)S(1)}, f32[32,2]{1,0:T(8,128)S(1)}, ...) while((s32[]{:T(128)}, f32[2,16,1024]{2,1,0:T(8,128)S(1)}, f32[32,2,16,1024]{3,2,1,0:T(8,128)}, ...), condition=%wide.region_2.3_spmd.clone, body=%wide.region_1.2_spmd.clone.sunk | while | flops 131075 | bytes 524947 | solution.py:51
  58.4 54.4 %while.50 = (s32[]{:T(128)}, f32[2,16,1024]{2,1,0:T(8,128)S(1)}, f32[2,1,1]{0,2,1:T(1,128)S(1)}, f32[2,16,1024]{2,1,0:T(8,128)S(1)}, s32[]{:T(128)}) while((s32[]{:T(128)}, f32[2,16,1024]{2,1,0:T(8,128)S(1)}, f32[2,1,1]{0,2,1:T(1,128)S(1)}, f32[2,16,1024]{2,1,0:T(8,128)S(1)}, s32[]{:T(128)}) %tuple.108), condition=%wide.region_5.6_spmd, body=%wide.region_4.5_spmd.sunk | while | flops 65538 | bytes 917613 | solution.py:59
  58.5 4.9 %collective-permute-start = (f32[2,16,1024]{2,1,0:T(8,128)S(1)}, f32[2,16,1024]{2,1,0:T(8,128)S(1)}, u32[]{:S(2)}, u32[]{:S(2)}) collective-permute-start(f32[2,16,1024]{2,1,0:T(8,128)S(1)} %multiply_add_fusion.6), channel_id=1, source_target_pairs={{0,2},{2,4},{4,6},{6,8},{8,10},{10,12},{12,14},{1,3},{3,5},{5,7},{... | collective-permute-start | bytes 393224 | tf_op jit(solution)/shard_map/while/body/eval_jaxpr/ppermute | solution.py:12
  66.2 4.4 %collective-permute-start = (f32[2,16,1024]{2,1,0:T(8,128)S(1)}, f32[2,16,1024]{2,1,0:T(8,128)S(1)}, u32[]{:S(2)}, u32[]{:S(2)}) collective-permute-start(f32[2,16,1024]{2,1,0:T(8,128)S(1)} %multiply_add_fusion.6), channel_id=1, source_target_pairs={{0,2},{2,4},{4,6},{6,8},{8,10},{10,12},{12,14},{1,3},{3,5},{5,7},{... | collective-permute-start | bytes 393224 | tf_op jit(solution)/shard_map/while/body/eval_jaxpr/ppermute | solution.py:12
  73.2 4.4 %collective-permute-start = (f32[2,16,1024]{2,1,0:T(8,128)S(1)}, f32[2,16,1024]{2,1,0:T(8,128)S(1)}, u32[]{:S(2)}, u32[]{:S(2)}) collective-permute-start(f32[2,16,1024]{2,1,0:T(8,128)S(1)} %multiply_add_fusion.6), channel_id=1, source_target_pairs={{0,2},{2,4},{4,6},{6,8},{8,10},{10,12},{12,14},{1,3},{3,5},{5,7},{... | collective-permute-start | bytes 393224 | tf_op jit(solution)/shard_map/while/body/eval_jaxpr/ppermute | solution.py:12
  80.1 5.2 %collective-permute-start = (f32[2,16,1024]{2,1,0:T(8,128)S(1)}, f32[2,16,1024]{2,1,0:T(8,128)S(1)}, u32[]{:S(2)}, u32[]{:S(2)}) collective-permute-start(f32[2,16,1024]{2,1,0:T(8,128)S(1)} %multiply_add_fusion.6), channel_id=1, source_target_pairs={{0,2},{2,4},{4,6},{6,8},{8,10},{10,12},{12,14},{1,3},{3,5},{5,7},{... | collective-permute-start | bytes 393224 | tf_op jit(solution)/shard_map/while/body/eval_jaxpr/ppermute | solution.py:12
  88.0 5.3 %collective-permute-start = (f32[2,16,1024]{2,1,0:T(8,128)S(1)}, f32[2,16,1024]{2,1,0:T(8,128)S(1)}, u32[]{:S(2)}, u32[]{:S(2)}) collective-permute-start(f32[2,16,1024]{2,1,0:T(8,128)S(1)} %multiply_add_fusion.6), channel_id=1, source_target_pairs={{0,2},{2,4},{4,6},{6,8},{8,10},{10,12},{12,14},{1,3},{3,5},{5,7},{... | collective-permute-start | bytes 393224 | tf_op jit(solution)/shard_map/while/body/eval_jaxpr/ppermute | solution.py:12
  95.8 5.3 %collective-permute-start = (f32[2,16,1024]{2,1,0:T(8,128)S(1)}, f32[2,16,1024]{2,1,0:T(8,128)S(1)}, u32[]{:S(2)}, u32[]{:S(2)}) collective-permute-start(f32[2,16,1024]{2,1,0:T(8,128)S(1)} %multiply_add_fusion.6), channel_id=1, source_target_pairs={{0,2},{2,4},{4,6},{6,8},{8,10},{10,12},{12,14},{1,3},{3,5},{5,7},{... | collective-permute-start | bytes 393224 | tf_op jit(solution)/shard_map/while/body/eval_jaxpr/ppermute | solution.py:12
  101.2 3.5 %collective-permute-done = f32[2,16,1024]{2,1,0:T(8,128)S(1)} collective-permute-done((f32[2,16,1024]{2,1,0:T(8,128)S(1)}, f32[2,16,1024]{2,1,0:T(8,128)S(1)}, u32[]{:S(2)}, u32[]{:S(2)}) %collective-permute-start) | collective-permute-done | bytes 131104 | tf_op jit(solution)/shard_map/while/body/eval_jaxpr/ppermute | solution.py:12
  104.8 5.5 %collective-permute-start = (f32[2,16,1024]{2,1,0:T(8,128)S(1)}, f32[2,16,1024]{2,1,0:T(8,128)S(1)}, u32[]{:S(2)}, u32[]{:S(2)}) collective-permute-start(f32[2,16,1024]{2,1,0:T(8,128)S(1)} %multiply_add_fusion.6), channel_id=1, source_target_pairs={{0,2},{2,4},{4,6},{6,8},{8,10},{10,12},{12,14},{1,3},{3,5},{5,7},{... | collective-permute-start | bytes 393224 | tf_op jit(solution)/shard_map/while/body/eval_jaxpr/ppermute | solution.py:12
  112.8 4.5 %multiply_add_fusion.3 = f32[32,2,16,1024]{3,2,1,0:T(8,128)} fusion(f32[32,2,16,1024]{3,2,1,0:T(8,128)} %get-tuple-element.200, f32[2,16,1024]{2,1,0:T(8,128)S(1)} %get-tuple-element.201, f32[32,2]{1,0:T(8,128)S(1)} %reduce_window.14), kind=kLoop, calls=%fused_computation.59 | loop fusion | flops 2097152 | bytes 8519936 | tf_op jit(solution)/shard_map/add | solution.py:60
  119.9 53.0 %while.53 = (s32[]{:T(128)}, f32[2,16,1024]{2,1,0:T(8,128)S(1)}, f32[32,2,16,1024]{3,2,1,0:T(8,128)}, f32[32,2]{1,0:T(8,128)S(1)}, f32[32,2]{1,0:T(8,128)S(1)}, ...) while((s32[]{:T(128)}, f32[2,16,1024]{2,1,0:T(8,128)S(1)}, ...), condition=%wide.region_7.8_spmd.clone, body=%wide.region_6.7_spmd.clone.sunk | while | flops 131076 | bytes 524459 | solution.py:67
  173.9 56.9 %while.51 = (s32[]{:T(128)}, f32[2,16,1024]{2,1,0:T(8,128)S(1)}, f32[2,1,1]{0,2,1:T(1,128)S(1)}, f32[2,16,1024]{2,1,0:T(8,128)S(1)}, s32[]{:T(128)}) while((s32[]{:T(128)}, f32[2,16,1024]{2,1,0:T(8,128)S(1)}, f32[2,1,1]{0,2,1:T(1,128)S(1)}, f32[2,16,1024]{2,1,0:T(8,128)S(1)}, s32[]{:T(128)}) %tuple.114), condition=%wide.region_10.11_spmd, body=%wide.region_9.10_spmd.sunk | while | flops 65538 | bytes 917613 | solution.py:75
  175.3 7.3 %collective-permute-done.1 = f32[2,16,1024]{2,1,0:T(8,128)S(1)} collective-permute-done((f32[2,16,1024]{2,1,0:T(8,128)S(1)}, f32[2,16,1024]{2,1,0:T(8,128)S(1)}, u32[]{:S(2)}, u32[]{:S(2)}) %collective-permute-start.1) | collective-permute-done | bytes 131104 | tf_op jit(solution)/shard_map/while/body/eval_jaxpr/ppermute | solution.py:12
  184.0 6.5 %collective-permute-done.1 = f32[2,16,1024]{2,1,0:T(8,128)S(1)} collective-permute-done((f32[2,16,1024]{2,1,0:T(8,128)S(1)}, f32[2,16,1024]{2,1,0:T(8,128)S(1)}, u32[]{:S(2)}, u32[]{:S(2)}) %collective-permute-start.1) | collective-permute-done | bytes 131104 | tf_op jit(solution)/shard_map/while/body/eval_jaxpr/ppermute | solution.py:12
  191.9 6.5 %collective-permute-done.1 = f32[2,16,1024]{2,1,0:T(8,128)S(1)} collective-permute-done((f32[2,16,1024]{2,1,0:T(8,128)S(1)}, f32[2,16,1024]{2,1,0:T(8,128)S(1)}, u32[]{:S(2)}, u32[]{:S(2)}) %collective-permute-start.1) | collective-permute-done | bytes 131104 | tf_op jit(solution)/shard_map/while/body/eval_jaxpr/ppermute | solution.py:12
  199.7 6.5 %collective-permute-done.1 = f32[2,16,1024]{2,1,0:T(8,128)S(1)} collective-permute-done((f32[2,16,1024]{2,1,0:T(8,128)S(1)}, f32[2,16,1024]{2,1,0:T(8,128)S(1)}, u32[]{:S(2)}, u32[]{:S(2)}) %collective-permute-start.1) | collective-permute-done | bytes 131104 | tf_op jit(solution)/shard_map/while/body/eval_jaxpr/ppermute | solution.py:12
  207.5 7.3 %collective-permute-done.1 = f32[2,16,1024]{2,1,0:T(8,128)S(1)} collective-permute-done((f32[2,16,1024]{2,1,0:T(8,128)S(1)}, f32[2,16,1024]{2,1,0:T(8,128)S(1)}, u32[]{:S(2)}, u32[]{:S(2)}) %collective-permute-start.1) | collective-permute-done | bytes 131104 | tf_op jit(solution)/shard_map/while/body/eval_jaxpr/ppermute | solution.py:12
  216.2 6.8 %collective-permute-done.1 = f32[2,16,1024]{2,1,0:T(8,128)S(1)} collective-permute-done((f32[2,16,1024]{2,1,0:T(8,128)S(1)}, f32[2,16,1024]{2,1,0:T(8,128)S(1)}, u32[]{:S(2)}, u32[]{:S(2)}) %collective-permute-start.1) | collective-permute-done | bytes 131104 | tf_op jit(solution)/shard_map/while/body/eval_jaxpr/ppermute | solution.py:12
  224.3 6.5 %collective-permute-done.1 = f32[2,16,1024]{2,1,0:T(8,128)S(1)} collective-permute-done((f32[2,16,1024]{2,1,0:T(8,128)S(1)}, f32[2,16,1024]{2,1,0:T(8,128)S(1)}, u32[]{:S(2)}, u32[]{:S(2)}) %collective-permute-start.1) | collective-permute-done | bytes 131104 | tf_op jit(solution)/shard_map/while/body/eval_jaxpr/ppermute | solution.py:12
  239.5 3.4 %fusion.10 = f32[32,2,16,1024]{3,2,1,0:T(8,128)S(1)} fusion(f32[32,2,16,1024]{3,2,1,0:T(8,128)S(1)} %multiply_add_fusion.2, f32[32,2,16,1]{3,2,1,0:T(8,128)S(1)} %collective-permute-done.3, f32[32,2,16,1]{3,2,1,0:T(8,128)S(1)} %collective-permute-done.2), kind=kLoop, calls=%fused_computation.30 | loop fusion | flops 9437184 | bytes 8396800 | tf_op jit(solution)/shard_map/add | solution.py:37
  249.0 3.4 %fusion.15 = f32[32,2,16,1024]{3,2,1,0:T(8,128)S(1)} fusion(f32[32,2,16,1024]{3,2,1,0:T(8,128)S(1)} %fusion.10, f32[32,2,16,1]{3,2,1,0:T(8,128)S(1)} %collective-permute-done.5, f32[32,2,16,1]{3,2,1,0:T(8,128)S(1)} %collective-permute-done.4), kind=kLoop, calls=%fused_computation.35 | loop fusion | flops 9437184 | bytes 8396800 | tf_op jit(solution)/shard_map/add | solution.py:37
  258.7 3.4 %fusion.20 = f32[32,2,16,1024]{3,2,1,0:T(8,128)S(1)} fusion(f32[32,2,16,1024]{3,2,1,0:T(8,128)S(1)} %fusion.15, f32[32,2,16,1]{3,2,1,0:T(8,128)S(1)} %collective-permute-done.7, f32[32,2,16,1]{3,2,1,0:T(8,128)S(1)} %collective-permute-done.6), kind=kLoop, calls=%fused_computation.40 | loop fusion | flops 9437184 | bytes 8396800 | tf_op jit(solution)/shard_map/add | solution.py:37
  268.2 3.4 %fusion.25 = f32[32,2,16,1024]{3,2,1,0:T(8,128)S(1)} fusion(f32[32,2,16,1024]{3,2,1,0:T(8,128)S(1)} %fusion.20, f32[32,2,16,1]{3,2,1,0:T(8,128)S(1)} %collective-permute-done.9, f32[32,2,16,1]{3,2,1,0:T(8,128)S(1)} %collective-permute-done.8), kind=kLoop, calls=%fused_computation.45 | loop fusion | flops 9437184 | bytes 8396800 | tf_op jit(solution)/shard_map/add | solution.py:37
  (204 shorter events, 169.3 us)
Async XLA Ops:
  58.5 7.6 %collective-permute-start = (f32[2,16,1024]{2,1,0:T(8,128)S(1)}, f32[2,16,1024]{2,1,0:T(8,128)S(1)}, u32[]{:S(2)}, u32[]{:S(2)}) collective-permute-start(f32[2,16,1024]{2,1,0:T(8,128)S(1)} %multiply_add_fusion.6), channel_id=1, source_target_pairs={{0,2},{2,4},{4,6},{6,8},{8,10},{10,12},{12,14},{1,3},{3,5},{5,7},{... | collective-permute-start | bytes 393224 | tf_op jit(solution)/shard_map/while/body/eval_jaxpr/ppermute | solution.py:12
  66.2 6.9 %collective-permute-start = (f32[2,16,1024]{2,1,0:T(8,128)S(1)}, f32[2,16,1024]{2,1,0:T(8,128)S(1)}, u32[]{:S(2)}, u32[]{:S(2)}) collective-permute-start(f32[2,16,1024]{2,1,0:T(8,128)S(1)} %multiply_add_fusion.6), channel_id=1, source_target_pairs={{0,2},{2,4},{4,6},{6,8},{8,10},{10,12},{12,14},{1,3},{3,5},{5,7},{... | collective-permute-start | bytes 393224 | tf_op jit(solution)/shard_map/while/body/eval_jaxpr/ppermute | solution.py:12
  73.2 6.9 %collective-permute-start = (f32[2,16,1024]{2,1,0:T(8,128)S(1)}, f32[2,16,1024]{2,1,0:T(8,128)S(1)}, u32[]{:S(2)}, u32[]{:S(2)}) collective-permute-start(f32[2,16,1024]{2,1,0:T(8,128)S(1)} %multiply_add_fusion.6), channel_id=1, source_target_pairs={{0,2},{2,4},{4,6},{6,8},{8,10},{10,12},{12,14},{1,3},{3,5},{5,7},{... | collective-permute-start | bytes 393224 | tf_op jit(solution)/shard_map/while/body/eval_jaxpr/ppermute | solution.py:12
  80.1 7.7 %collective-permute-start = (f32[2,16,1024]{2,1,0:T(8,128)S(1)}, f32[2,16,1024]{2,1,0:T(8,128)S(1)}, u32[]{:S(2)}, u32[]{:S(2)}) collective-permute-start(f32[2,16,1024]{2,1,0:T(8,128)S(1)} %multiply_add_fusion.6), channel_id=1, source_target_pairs={{0,2},{2,4},{4,6},{6,8},{8,10},{10,12},{12,14},{1,3},{3,5},{5,7},{... | collective-permute-start | bytes 393224 | tf_op jit(solution)/shard_map/while/body/eval_jaxpr/ppermute | solution.py:12
  88.0 7.8 %collective-permute-start = (f32[2,16,1024]{2,1,0:T(8,128)S(1)}, f32[2,16,1024]{2,1,0:T(8,128)S(1)}, u32[]{:S(2)}, u32[]{:S(2)}) collective-permute-start(f32[2,16,1024]{2,1,0:T(8,128)S(1)} %multiply_add_fusion.6), channel_id=1, source_target_pairs={{0,2},{2,4},{4,6},{6,8},{8,10},{10,12},{12,14},{1,3},{3,5},{5,7},{... | collective-permute-start | bytes 393224 | tf_op jit(solution)/shard_map/while/body/eval_jaxpr/ppermute | solution.py:12
  95.8 8.9 %collective-permute-start = (f32[2,16,1024]{2,1,0:T(8,128)S(1)}, f32[2,16,1024]{2,1,0:T(8,128)S(1)}, u32[]{:S(2)}, u32[]{:S(2)}) collective-permute-start(f32[2,16,1024]{2,1,0:T(8,128)S(1)} %multiply_add_fusion.6), channel_id=1, source_target_pairs={{0,2},{2,4},{4,6},{6,8},{8,10},{10,12},{12,14},{1,3},{3,5},{5,7},{... | collective-permute-start | bytes 393224 | tf_op jit(solution)/shard_map/while/body/eval_jaxpr/ppermute | solution.py:12
  104.8 8.0 %collective-permute-start = (f32[2,16,1024]{2,1,0:T(8,128)S(1)}, f32[2,16,1024]{2,1,0:T(8,128)S(1)}, u32[]{:S(2)}, u32[]{:S(2)}) collective-permute-start(f32[2,16,1024]{2,1,0:T(8,128)S(1)} %multiply_add_fusion.6), channel_id=1, source_target_pairs={{0,2},{2,4},{4,6},{6,8},{8,10},{10,12},{12,14},{1,3},{3,5},{5,7},{... | collective-permute-start | bytes 393224 | tf_op jit(solution)/shard_map/while/body/eval_jaxpr/ppermute | solution.py:12
  174.0 8.6 %collective-permute-start.1 = (f32[2,16,1024]{2,1,0:T(8,128)S(1)}, f32[2,16,1024]{2,1,0:T(8,128)S(1)}, u32[]{:S(2)}, u32[]{:S(2)}) collective-permute-start(f32[2,16,1024]{2,1,0:T(8,128)S(1)} %multiply_add_fusion.7), channel_id=1, source_target_pairs={{2,0},{4,2},{6,4},{8,6},{10,8},{12,10},{14,12},{3,1},{5,3},{7,5},{... | collective-permute-start | bytes 393224 | tf_op jit(solution)/shard_map/while/body/eval_jaxpr/ppermute | solution.py:12
  182.7 7.8 %collective-permute-start.1 = (f32[2,16,1024]{2,1,0:T(8,128)S(1)}, f32[2,16,1024]{2,1,0:T(8,128)S(1)}, u32[]{:S(2)}, u32[]{:S(2)}) collective-permute-start(f32[2,16,1024]{2,1,0:T(8,128)S(1)} %multiply_add_fusion.7), channel_id=1, source_target_pairs={{2,0},{4,2},{6,4},{8,6},{10,8},{12,10},{14,12},{3,1},{5,3},{7,5},{... | collective-permute-start | bytes 393224 | tf_op jit(solution)/shard_map/while/body/eval_jaxpr/ppermute | solution.py:12
  190.5 7.8 %collective-permute-start.1 = (f32[2,16,1024]{2,1,0:T(8,128)S(1)}, f32[2,16,1024]{2,1,0:T(8,128)S(1)}, u32[]{:S(2)}, u32[]{:S(2)}) collective-permute-start(f32[2,16,1024]{2,1,0:T(8,128)S(1)} %multiply_add_fusion.7), channel_id=1, source_target_pairs={{2,0},{4,2},{6,4},{8,6},{10,8},{12,10},{14,12},{3,1},{5,3},{7,5},{... | collective-permute-start | bytes 393224 | tf_op jit(solution)/shard_map/while/body/eval_jaxpr/ppermute | solution.py:12
  198.4 7.8 %collective-permute-start.1 = (f32[2,16,1024]{2,1,0:T(8,128)S(1)}, f32[2,16,1024]{2,1,0:T(8,128)S(1)}, u32[]{:S(2)}, u32[]{:S(2)}) collective-permute-start(f32[2,16,1024]{2,1,0:T(8,128)S(1)} %multiply_add_fusion.7), channel_id=1, source_target_pairs={{2,0},{4,2},{6,4},{8,6},{10,8},{12,10},{14,12},{3,1},{5,3},{7,5},{... | collective-permute-start | bytes 393224 | tf_op jit(solution)/shard_map/while/body/eval_jaxpr/ppermute | solution.py:12
  206.2 8.6 %collective-permute-start.1 = (f32[2,16,1024]{2,1,0:T(8,128)S(1)}, f32[2,16,1024]{2,1,0:T(8,128)S(1)}, u32[]{:S(2)}, u32[]{:S(2)}) collective-permute-start(f32[2,16,1024]{2,1,0:T(8,128)S(1)} %multiply_add_fusion.7), channel_id=1, source_target_pairs={{2,0},{4,2},{6,4},{8,6},{10,8},{12,10},{14,12},{3,1},{5,3},{7,5},{... | collective-permute-start | bytes 393224 | tf_op jit(solution)/shard_map/while/body/eval_jaxpr/ppermute | solution.py:12
  214.9 8.1 %collective-permute-start.1 = (f32[2,16,1024]{2,1,0:T(8,128)S(1)}, f32[2,16,1024]{2,1,0:T(8,128)S(1)}, u32[]{:S(2)}, u32[]{:S(2)}) collective-permute-start(f32[2,16,1024]{2,1,0:T(8,128)S(1)} %multiply_add_fusion.7), channel_id=1, source_target_pairs={{2,0},{4,2},{6,4},{8,6},{10,8},{12,10},{14,12},{3,1},{5,3},{7,5},{... | collective-permute-start | bytes 393224 | tf_op jit(solution)/shard_map/while/body/eval_jaxpr/ppermute | solution.py:12
  223.0 7.8 %collective-permute-start.1 = (f32[2,16,1024]{2,1,0:T(8,128)S(1)}, f32[2,16,1024]{2,1,0:T(8,128)S(1)}, u32[]{:S(2)}, u32[]{:S(2)}) collective-permute-start(f32[2,16,1024]{2,1,0:T(8,128)S(1)} %multiply_add_fusion.7), channel_id=1, source_target_pairs={{2,0},{4,2},{6,4},{8,6},{10,8},{12,10},{14,12},{3,1},{5,3},{7,5},{... | collective-permute-start | bytes 393224 | tf_op jit(solution)/shard_map/while/body/eval_jaxpr/ppermute | solution.py:12
  233.6 4.4 %collective-permute-start.2 = (f32[32,2,16,1]{3,2,1,0:T(8,128)S(1)}, f32[32,2,16,1]{3,2,1,0:T(8,128)S(1)}, u32[]{:S(2)}, u32[]{:S(2)}) collective-permute-start(f32[32,2,16,1]{3,2,1,0:T(8,128)S(1)} %get-tuple-element.312), channel_id=1, source_target_pairs={{1,0},{3,2},{5,4},{7,6},{9,8},{11,10},{13,12},{15,14},{17,16},{19,... | collective-permute-start | bytes 12296 | tf_op jit(solution)/shard_map/ppermute | solution.py:23
  234.9 4.6 %collective-permute-start.3 = (f32[32,2,16,1]{3,2,1,0:T(8,128)S(1)}, f32[32,2,16,1]{3,2,1,0:T(8,128)S(1)}, u32[]{:S(2)}, u32[]{:S(2)}) collective-permute-start(f32[32,2,16,1]{3,2,1,0:T(8,128)S(1)} %get-tuple-element.313), channel_id=1, source_target_pairs={{0,1},{2,3},{4,5},{6,7},{8,9},{10,11},{12,13},{14,15},{16,17},{18,... | collective-permute-start | bytes 12296 | tf_op jit(solution)/shard_map/ppermute | solution.py:22
  243.1 4.4 %collective-permute-start.4 = (f32[32,2,16,1]{3,2,1,0:T(8,128)S(1)}, f32[32,2,16,1]{3,2,1,0:T(8,128)S(1)}, u32[]{:S(2)}, u32[]{:S(2)}) collective-permute-start(f32[32,2,16,1]{3,2,1,0:T(8,128)S(1)} %get-tuple-element.310), channel_id=1, source_target_pairs={{1,0},{3,2},{5,4},{7,6},{9,8},{11,10},{13,12},{15,14},{17,16},{19,... | collective-permute-start | bytes 12296 | tf_op jit(solution)/shard_map/ppermute | solution.py:23
  244.4 4.6 %collective-permute-start.5 = (f32[32,2,16,1]{3,2,1,0:T(8,128)S(1)}, f32[32,2,16,1]{3,2,1,0:T(8,128)S(1)}, u32[]{:S(2)}, u32[]{:S(2)}) collective-permute-start(f32[32,2,16,1]{3,2,1,0:T(8,128)S(1)} %get-tuple-element.311), channel_id=1, source_target_pairs={{0,1},{2,3},{4,5},{6,7},{8,9},{10,11},{12,13},{14,15},{16,17},{18,... | collective-permute-start | bytes 12296 | tf_op jit(solution)/shard_map/ppermute | solution.py:22
  252.7 4.6 %collective-permute-start.6 = (f32[32,2,16,1]{3,2,1,0:T(8,128)S(1)}, f32[32,2,16,1]{3,2,1,0:T(8,128)S(1)}, u32[]{:S(2)}, u32[]{:S(2)}) collective-permute-start(f32[32,2,16,1]{3,2,1,0:T(8,128)S(1)} %get-tuple-element.308), channel_id=1, source_target_pairs={{1,0},{3,2},{5,4},{7,6},{9,8},{11,10},{13,12},{15,14},{17,16},{19,... | collective-permute-start | bytes 12296 | tf_op jit(solution)/shard_map/ppermute | solution.py:23
  254.0 12.8 %copy-start.1 = (s32[16,1024]{1,0:T(8,128)S(1)}, s32[16,1024]{1,0:T(8,128)}, u32[]{:S(2)}) copy-start(s32[16,1024]{1,0:T(8,128)} %param.16) | copy-start | bytes 196612
  254.0 12.8 %copy-start.2 = (f32[8]{0:T(128)S(1)}, f32[8]{0:T(128)}, u32[]{:S(2)}) copy-start(f32[8]{0:T(128)} %param.17) | copy-start | bytes 100
  254.0 4.7 %collective-permute-start.7 = (f32[32,2,16,1]{3,2,1,0:T(8,128)S(1)}, f32[32,2,16,1]{3,2,1,0:T(8,128)S(1)}, u32[]{:S(2)}, u32[]{:S(2)}) collective-permute-start(f32[32,2,16,1]{3,2,1,0:T(8,128)S(1)} %get-tuple-element.309), channel_id=1, source_target_pairs={{0,1},{2,3},{4,5},{6,7},{8,9},{10,11},{12,13},{14,15},{16,17},{18,... | collective-permute-start | bytes 12296 | tf_op jit(solution)/shard_map/ppermute | solution.py:22
  262.3 4.7 %collective-permute-start.8 = (f32[32,2,16,1]{3,2,1,0:T(8,128)S(1)}, f32[32,2,16,1]{3,2,1,0:T(8,128)S(1)}, u32[]{:S(2)}, u32[]{:S(2)}) collective-permute-start(f32[32,2,16,1]{3,2,1,0:T(8,128)S(1)} %get-tuple-element.306), channel_id=1, source_target_pairs={{1,0},{3,2},{5,4},{7,6},{9,8},{11,10},{13,12},{15,14},{17,16},{19,... | collective-permute-start | bytes 12296 | tf_op jit(solution)/shard_map/ppermute | solution.py:23
  263.6 4.6 %collective-permute-start.9 = (f32[32,2,16,1]{3,2,1,0:T(8,128)S(1)}, f32[32,2,16,1]{3,2,1,0:T(8,128)S(1)}, u32[]{:S(2)}, u32[]{:S(2)}) collective-permute-start(f32[32,2,16,1]{3,2,1,0:T(8,128)S(1)} %get-tuple-element.307), channel_id=1, source_target_pairs={{0,1},{2,3},{4,5},{6,7},{8,9},{10,11},{12,13},{14,15},{16,17},{18,... | collective-permute-start | bytes 12296 | tf_op jit(solution)/shard_map/ppermute | solution.py:22
  (1 other events, 2.7 us)
where the time goes:
time: 277 us; the launch traced here: 274 us
  other arithmetic  131 us (47%)
  waiting for transfers between devices  71.6 us (26%)
  starting transfers between devices  61.7 us (22%)
  local copies, waits for them, and re-layouts  8.68 us (3%)
    dynamic_update_slice x64, other arithmetic, shards(): _, local_fwd = lax.scan(forward, start, (alpha, fwd_gain, noise))  105 us
    ppermute x14, waiting for transfers between devices, shifted(): return lax.ppermute(value, axis, pairs)  65.9 us
    ppermute x14, starting transfers between devices, shifted(): return lax.ppermute(value, axis, pairs)  44 us
    add x4, other arithmetic, sweep_once(): return field + 0.2 * lap  13.6 us
    ppermute x4, starting transfers between devices, padded_2(): before = lax.ppermute(last, axis, up)  12.5 us
    ppermute x4, waiting for transfers between devices, padded_2(): before = lax.ppermute(last, axis, up)  5.64 us
  transfers between devices with their start and end apart: 22, of which 18 were waited for; matrix products, arithmetic and copies ran while one was open for 0% of the time, Pallas kernels for 0%

commit v1 on v0

v1 whole, which is shorter than its diff:
```python
import functools

import jax
import jax.numpy as jnp
from jax import lax
from jax.experimental import pallas as pl
from jax.experimental.pallas import tpu as pltpu
from jax.sharding import PartitionSpec as P

SWEEPS = 4
GROUP = 4
TILE = 128
EDGE = SWEEPS
F32 = jnp.float32
SMEM = pl.BlockSpec(memory_space=pltpu.SMEM)
ANY = pl.BlockSpec(memory_space=pl.ANY)
VMEM = pl.BlockSpec(memory_space=pltpu.VMEM)
HBM = pl.BlockSpec(memory_space=pltpu.HBM)


def splat(value):
    return jnp.full((8, TILE), value, F32)


def row(ref, *at):
    return jnp.broadcast_to(ref[(*at[:-1], pl.ds(at[-1], 1), slice(None))], (8, TILE))


def fill_tables(rates_ref, table):
    for i in range(rates_ref.shape[0]):
        alpha = jnp.exp(-splat(rates_ref[i]))
        table[0, i] = alpha
        table[1, i] = jnp.sqrt(1.0 - alpha * alpha)


def position():
    return lax.rem(lax.axis_index("gz"), GROUP)


def carries(idx_hbm, rates_hbm, noise_hbm, out0, out1, out2, out3, coef, packed, table, pre, wts, tiled, idx, rates, sems):
    outs = (out0, out1, out2, out3)
    levels, columns = noise_hbm.shape[0], noise_hbm.shape[3]
    pos = position()
    core = lax.axis_index("gx")
    small = [
        pltpu.make_async_copy(idx_hbm, idx, sems.at[GROUP, 0]),
        pltpu.make_async_copy(rates_hbm, rates, sems.at[GROUP, 1]),
    ]
    for copy in small:
        copy.start()
    order = (1, 2, 3, 0)
    copies = {}
    for k in order:
        s = pos ^ k
        rows = pl.ds(pl.multiple_of(8 * (s % 2), 8), 8)
        copies[k] = []
        for t in range(columns // TILE):
            source = noise_hbm.at[:, s // 2, rows, pl.ds(t * TILE, TILE)]
            copies[k].append(pltpu.make_async_copy(source, tiled.at[s // 2, t, :, rows, :], sems.at[k, t]))
            copies[k][t].start()
    for copy in small:
        copy.wait()
    fill_tables(rates, table)
    for field in range(2):
        run = splat(1.0)
        for k in range(levels):
            pre[k] = run
            run = run * table[0, idx[field, k]]
        total = run
        post, gather, after = splat(1.0), splat(0.0), splat(0.0)
        for k in reversed(range(levels)):
            alpha, gain = table[0, idx[field, k]], table[1, idx[field, k]]
            coef[0, field, k : k + 1, :] = alpha[:1]
            coef[1, field, k : k + 1, :] = gain[:1]
            gather = pre[k] * (1.0 - alpha) + after * gather
            wts[0, field, k] = gain * post
            wts[1, field, k] = gain * gather
            post = post * alpha
            after = alpha
        wts[0, field, levels] = total
        wts[1, field, levels] = after * gather
    tiles = columns // TILE
    near = (1 - core) * (tiles - 1)
    slots = TILE // EDGE
    slot = lax.rem(lax.broadcasted_iota(jnp.int32, (8, TILE), 1) // EDGE + (1 - core), slots)
    for k in order:
        for copy in copies[k]:
            copy.wait()
        s = pos ^ k
        field = s // 2
        rows = pl.ds(pl.multiple_of(8 * (s % 2), 8), 8)
        for half in range(2):
            ours = range(half * tiles // 2, (half + 1) * tiles // 2)

            def body(level, sums, field=field, rows=rows, ours=ours):
                fwd, bwd = wts[0, field, level], wts[1, field, level]
                new = []
                for t, (one, two) in zip(ours, sums):
                    value = tiled[field, t, level, rows, :]
                    new.append((one + fwd * value, two + bwd * value))
                return tuple(new)

            sums = lax.fori_loop(0, levels, body, ((splat(0.0), splat(0.0)),) * len(ours), unroll=8)
            for t, (one, two) in zip(ours, sums):
                outs[k][0, :, t * TILE : (t + 1) * TILE] = one
                outs[k][1, :, t * TILE : (t + 1) * TILE] = two
        outs[k][0, :, columns:] = wts[0, field, levels]
        outs[k][1, :, columns:] = wts[1, field, levels]
        for first in range(0, levels, slots):
            edge = splat(0.0)
            for level in range(first, min(levels, first + slots)):
                turned = pltpu.roll(tiled[field, near, level, rows, :], EDGE * (level - first), 1)
                edge = jnp.where(slot == level - first, turned, edge)
            packed[first // slots, field, s % 2] = edge


def scan_group(held, lanes, f_in, r_in):
    columns = held.shape[3] - TILE
    f = [f_in]
    for j in range(GROUP):
        f.append(held[j, 0, :, columns:] * f[j] + held[j, 0, :, lanes])
    r = [None] * GROUP + [r_in]
    for j in reversed(range(GROUP)):
        r[j] = held[j, 1, :, lanes] + held[j, 1, :, columns:] * f[j] + held[j, 0, :, columns:] * r[j + 1]
    return f, r


def hold(refs, held):
    pos = position()
    for k, ref in enumerate(refs):
        held[pos ^ k] = ref[...]


def group_total(m0, m1, m2, m3, after, out, held):
    hold((m0, m1, m2, m3), held)
    columns = held.shape[3] - TILE
    zero = splat(0.0)
    for t in range(columns // TILE):
        lanes = slice(t * TILE, (t + 1) * TILE)
        f, r = scan_group(held, lanes, zero, zero)
        out[0, :, lanes] = f[GROUP]
        out[1, :, lanes] = r[0]
    run, factor = splat(1.0), splat(0.0)
    for j in range(GROUP):
        run = run * held[j, 0, :, columns:]
    for j in reversed(range(GROUP)):
        a, c = held[j, 0, :, columns:], held[j, 1, :, columns:]
        factor = c + a * a * factor
    out[0, :, columns:] = run
    out[1, :, columns:] = factor


def enter_group(m0, m1, m2, m3, entering, after, out0, out1, out2, out3, held):
    hold((m0, m1, m2, m3), held)
    columns = held.shape[3] - TILE
    outs = (out0, out1, out2, out3)
    pos = position()
    for t in range(columns // TILE):
        lanes = slice(t * TILE, (t + 1) * TILE)
        f, r = scan_group(held, lanes, entering[0, :, lanes], entering[1, :, lanes])
        for j in range(GROUP):
            held[j, 0, :, lanes] = f[j]
            held[j, 1, :, lanes] = r[j + 1]
    for k in range(GROUP):
        outs[k][...] = held[pos ^ k, :, :, :columns]


def row_neighbours(top, bottom):
    row = lax.broadcasted_iota(jnp.int32, top.shape, 0)
    first, last = row == 0, row == 7
    down_t, down_b = pltpu.roll(top, 1, 0), pltpu.roll(bottom, 1, 0)
    up_t, up_b = pltpu.roll(top, 7, 0), pltpu.roll(bottom, 7, 0)
    return (
        jnp.where(first, 0.0, down_t) + jnp.where(last, up_b, up_t),
        jnp.where(first, down_t, down_b) + jnp.where(last, 0.0, up_b),
    )


def diffuse(top, bottom, keep):
    width = top.shape[1]

    def masked(value):
        return jnp.concatenate([value[:, : width - TILE], value[:, width - TILE :] * keep], axis=1)

    for _ in range(SWEEPS):
        top, bottom = masked(top), masked(bottom)
        over_t, over_b = row_neighbours(top, bottom)
        top = top + over_t + (pltpu.roll(top, 1, 1) + pltpu.roll(top, width - 1, 1))
        bottom = bottom + over_b + (pltpu.roll(bottom, 1, 1) + pltpu.roll(bottom, width - 1, 1))
    return top, bottom


def edge_mask():
    lane = lax.broadcasted_iota(jnp.int32, (8, TILE), 1)
    core = lax.axis_index("gx")
    return ((lane < TILE // 2) == (core == 0)).astype(F32)


def prepare(coef, codes, thresholds, after, reach, bias, pre):
    levels = coef.shape[2]
    for field in range(2):
        run = splat(1.0)
        for k in range(levels):
            run = run * row(coef, 0, field, k)
            pre[k] = run
        down, up = splat(0.0), splat(1.0)
        for k in reversed(range(levels)):
            alpha = row(coef, 0, field, k)
            down = alpha * down + (1.0 - alpha) * pre[k]
            up = alpha * up
            reach[0, field, k : k + 1, :] = down[:1]
            reach[1, field, k : k + 1, :] = up[:1]
    code = codes[...]
    value = jnp.zeros(code.shape, F32)
    for i in range(thresholds.shape[0]):
        value = jnp.where(code == i, thresholds[i], value)
    bias[...] = value


def local_field(field, coef, packed, noise_hbm, after, out, buf, work, sems):
    levels, _, ys, columns = noise_hbm.shape
    tiles = columns // TILE

    def fetch_group(turn, go):
        at = pl.ds(pl.multiple_of(turn * 8, 8), 8)
        for t in range(tiles):
            source = noise_hbm.at[at, field, :, pl.ds(t * TILE, TILE)]
            copy = pltpu.make_async_copy(source, buf.at[t, at], sems.at[turn, t])
            if go:
                copy.start()
            else:
                copy.wait()

    for turn in range(levels // 8):
        fetch_group(turn, True)
    core = lax.axis_index("gx")
    lane = lax.broadcasted_iota(jnp.int32, (8, TILE), 1)
    keep = edge_mask()
    sent = jnp.where(core == 0, lane, TILE - 1 - lane) < EDGE
    slots = TILE // EDGE
    for level in range(levels):
        for top in range(2):
            edge = packed[level // slots, field, top]
            edge = pltpu.roll(edge, (TILE - EDGE * (level % slots)) % TILE, 1)
            buf[tiles, level, 8 * top : 8 * top + 8, :] = jnp.where(sent, edge, 0.0)
    flat = buf.reshape(tiles + 1, levels * ys, TILE)
    first, last = lane == 0, lane == TILE - 1

    def sweep(get, put, all_tiles):
        above = [splat(0.0)] * (tiles + 1)
        here = get(0)
        for y in range(ys):
            below = get(y + 1) if y + 1 < ys else [splat(0.0)] * (tiles + 1)
            right = [pltpu.roll(v, TILE - 1, 1) for v in here]
            left = [pltpu.roll(v, 1, 1) for v in here]
            new = []
            for t in range(tiles + all_tiles):
                beside = jnp.where(first, left[t - 1], left[t])
                beside += jnp.where(last, right[(t + 1) % (tiles + 1)], right[t])
                new.append(here[t] + beside + (above[t] + below[t]))
            if all_tiles:
                new[tiles] = new[tiles] * keep
            put(y, new)
            above, here = here, below

    def group(turn, _):
        fetch_group(turn, False)
        base = turn * 8 * ys

        def fetch(y):
            at = pl.ds(base + y, 8, stride=ys)
            return [flat[t, at, :] for t in range(tiles + 1)]

        def give(y, new):
            for t, value in enumerate(new):
                flat[t, pl.ds(base + y, 8, stride=ys), :] = value

        def saver(slot):
            def put(y, new):
                for t, value in enumerate(new):
                    work[slot, t, y] = value

            return put

        def loader(slot):
            return lambda y: [work[slot, t, y] for t in range(tiles + 1)]

        get = fetch
        for turn in range(SWEEPS - 1):
            sweep(get, saver(turn % 2), True)
            get = loader(turn % 2)
        sweep(get, give, False)
        return 0

    lax.fori_loop(0, levels // 8, group, 0)
    scale = 0.2**SWEEPS
    spots = [(t, top) for t in range(tiles) for top in range(ys // 8)]

    def forward(level, state):
        alpha, gain = row(coef, 0, field, level), row(coef, 1, field, level) * scale
        new = []
        for (t, top), old in zip(spots, state):
            value = alpha * old + gain * buf[t, level, 8 * top : 8 * top + 8, :]
            buf[t, level, 8 * top : 8 * top + 8, :] = value
            new.append(value)
        return tuple(new)

    def backward(turn, state):
        level = levels - 1 - turn
        alpha = row(coef, 0, field, level)
        gain = 1.0 - alpha
        new = []
        for (t, top), old in zip(spots, state):
            value = alpha * old + gain * buf[t, level, 8 * top : 8 * top + 8, :]
            out[level, 8 * top : 8 * top + 8, t * TILE : (t + 1) * TILE] = value
            new.append(value)
        return tuple(new)

    zeros = (splat(0.0),) * len(spots)
    lax.fori_loop(0, levels, forward, zeros, unroll=2)
    lax.fori_loop(0, levels, backward, zeros, unroll=2)


def edges(m0, m1, m2, m3, after, out):
    columns = m0.shape[2]
    near = pl.ds(pl.multiple_of((1 - lax.axis_index("gx")) * (columns - TILE), TILE), TILE)
    for k, ref in enumerate((m0, m1, m2, m3)):
        out[k] = ref[:, :, near]


def finish(g0, g1, reach, bias, m0, m1, m2, m3, halo, latent_hbm, soft_hbm, state, latent, soft, sems):
    levels, columns = g0.shape[0], g0.shape[2]
    pos = position()
    for k, ref in enumerate((m0, m1, m2, m3)):
        s = pos ^ k
        rows = pl.ds(pl.multiple_of(8 * (s % 2), 8), 8)
        for kind in range(2):
            state[kind, s // 2, rows, :columns] = ref[kind]
            state[kind, s // 2, rows, columns:] = halo[k, kind]
    keep = edge_mask()
    for kind in range(2):
        for field in range(2):
            top, bottom = diffuse(state[kind, field, 0:8, :], state[kind, field, 8:16, :], keep)
            state[kind, field, 0:8, :] = top * 0.2**SWEEPS
            state[kind, field, 8:16, :] = bottom * 0.2**SWEEPS
    parts = sems.shape[0]
    step = levels // parts
    tiles = columns // TILE
    copies = []
    for i in range(parts):

        def body(turn, _, i=i):
            rows = pl.ds(pl.multiple_of(8 * (turn // tiles), 8), 8)
            lanes = pl.ds(pl.multiple_of(TILE * lax.rem(turn, tiles), TILE), TILE)
            f = [state[0, field, rows, lanes] for field in range(2)]
            r = [state[1, field, rows, lanes] for field in range(2)]
            base = bias[rows, lanes]
            for level in range(i * step, (i + 1) * step):
                one = g0[level, rows, lanes] + row(reach, 0, 0, level) * f[0] + row(reach, 1, 0, level) * r[0]
                two = g1[level, rows, lanes] + row(reach, 0, 1, level) * f[1] + row(reach, 1, 1, level) * r[1]
                latent[level, 0, rows, lanes] = one
                latent[level, 1, rows, lanes] = two
                half = 0.5 + 0.5 * jnp.tanh(1.5 * (one - base))
                soft[level, rows, lanes] = half * (0.5 + 0.5 * jnp.tanh(1.5 * two))
            return 0

        lax.fori_loop(0, 2 * tiles, body, 0)
        at = pl.ds(i * step, step)
        copies += [
            pltpu.make_async_copy(latent.at[at], latent_hbm.at[at], sems.at[i, 0]),
            pltpu.make_async_copy(soft.at[at], soft_hbm.at[at], sems.at[i, 1]),
        ]
        for copy in copies[-2:]:
            copy.start()
    for copy in copies:
        copy.wait()


def params(mib):
    return pltpu.CompilerParams(vmem_limit_bytes=mib << 20)


def cost(flops, data):
    return pl.CostEstimate(flops=flops, bytes_accessed=data, transcendentals=0)


def xor_permute(value, axis, by):
    return lax.ppermute(value, axis, [(i, i ^ by) for i in range(lax.axis_size(axis))])


def entering_states(total, groups):
    columns = total.shape[2] - TILE
    group = lax.axis_index("gz") // GROUP

    def wide(value):
        return jnp.tile(value, (1, columns // TILE))

    def fwd(t):
        return t[0, :, :columns]

    def bwd(t):
        return t[1, :, :columns]

    if groups == 2:
        sent = jnp.where(group == 0, jnp.concatenate([total[0, :, :columns], total[0, :, columns:]], axis=1),
                         total[1])
        got = xor_permute(sent, "gz", GROUP)
        zero = jnp.zeros((8, columns), F32)
        below = got[:, :columns] + wide(got[:, columns:]) * fwd(total)
        return jnp.stack([jnp.where(group == 0, zero, got[:, :columns]), jnp.where(group == 0, below, zero)])
    size = GROUP * groups
    totals = [total]
    for turn in range(1, groups):
        totals.append(lax.ppermute(total, "gz", [(i, (i + GROUP * turn) % size) for i in range(size)]))
    stacked = jnp.stack(totals)
    state = jnp.zeros((8, columns), F32)
    f = [state]
    at = [lax.dynamic_index_in_dim(stacked, (group - j) % groups, keepdims=False) for j in range(groups)]
    for j in range(groups):
        state = wide(at[j][0, :, columns:]) * state + fwd(at[j])
        f.append(state)
    state = jnp.zeros((8, columns), F32)
    r = [None] * groups + [state]
    for j in reversed(range(groups)):
        state = bwd(at[j]) + wide(at[j][1, :, columns:]) * f[j] + wide(at[j][0, :, columns:]) * state
        r[j] = state
    return jnp.stack(
        [
            lax.dynamic_index_in_dim(jnp.stack(f[:groups]), group, keepdims=False),
            lax.dynamic_index_in_dim(jnp.stack(r[1:]), group, keepdims=False),
        ]
    )


def shards(noise, scale_index, rates, facies_code, thresholds):
    levels, _, ys, columns = noise.shape
    assert ys == 16 and columns % (2 * TILE) == 0 and levels % 8 == 0
    tiles = columns // TILE
    groups = lax.axis_size("gz") // GROUP
    message = jax.ShapeDtypeStruct((2, 8, columns + TILE), F32)
    folds = -(-levels * EDGE // TILE)
    *mine, coef, packed = pl.pallas_call(
        carries,
        out_shape=[message] * GROUP
        + [
            jax.ShapeDtypeStruct((2, 2, levels, TILE), F32),
            jax.ShapeDtypeStruct((folds, 2, 2, 8, TILE), F32),
        ],
        in_specs=[HBM, HBM, HBM],
        out_specs=[VMEM] * (GROUP + 2),
        scratch_shapes=[
            pltpu.VMEM((2, rates.shape[0], 8, TILE), F32),
            pltpu.VMEM((levels, 8, TILE), F32),
            pltpu.VMEM((2, 2, levels + 1, 8, TILE), F32),
            pltpu.VMEM((2, tiles, levels, ys, TILE), F32),
            pltpu.SMEM((2, levels), jnp.int32),
            pltpu.SMEM(rates.shape, F32),
            pltpu.SemaphoreType.DMA((GROUP + 1, tiles)),
        ],
        compiler_params=params(52),
        cost_estimate=cost(4 * noise.size, 4 * noise.size),
        name="carries",
    )(scale_index.T, rates, noise)
    got = [mine[0]] + [xor_permute(mine[k], "gz", k) for k in range(1, GROUP)]
    halo = xor_permute(packed, "gx", 1)

    def local(field, after):
        return pl.pallas_call(
            functools.partial(local_field, field),
            out_shape=jax.ShapeDtypeStruct((levels, ys, columns), F32),
            in_specs=[VMEM, VMEM, HBM, ANY],
            out_specs=VMEM,
            scratch_shapes=[
                pltpu.VMEM((tiles + 1, levels, ys, TILE), F32),
                pltpu.VMEM((2, tiles + 1, ys, 8, TILE), F32),
                pltpu.SemaphoreType.DMA((levels // 8, tiles)),
            ],
            compiler_params=params(50),
            cost_estimate=cost(80 * noise.size // 2, 4 * noise.size),
            name=f"local{field}",
        )(coef, halo, noise, after)

    local0 = local(0, halo)
    held = pltpu.VMEM((GROUP, 2, 8, columns + TILE), F32)
    total = pl.pallas_call(
        group_total,
        out_shape=message,
        in_specs=[VMEM] * GROUP + [ANY],
        out_specs=VMEM,
        scratch_shapes=[held],
        compiler_params=params(8),
        name="group_total",
    )(*got, local0)
    reach, bias = pl.pallas_call(
        prepare,
        out_shape=[
            jax.ShapeDtypeStruct((2, 2, levels, TILE), F32),
            jax.ShapeDtypeStruct((ys, columns), F32),
        ],
        in_specs=[VMEM, VMEM, SMEM, ANY],
        out_specs=[VMEM] * 2,
        scratch_shapes=[pltpu.VMEM((levels, 8, TILE), F32)],
        compiler_params=params(4),
        cost_estimate=cost(noise.size, noise.size),
        name="prepare",
    )(coef, facies_code, thresholds, total)
    entering = entering_states(total, groups)
    state = jax.ShapeDtypeStruct((2, 8, columns), F32)
    own = pl.pallas_call(
        enter_group,
        out_shape=[state] * GROUP,
        in_specs=[VMEM] * (GROUP + 1) + [ANY],
        out_specs=[VMEM] * GROUP,
        scratch_shapes=[held],
        compiler_params=params(8),
        name="enter_group",
    )(*got, entering, reach)
    states = [own[0]] + [xor_permute(own[k], "gz", k) for k in range(1, GROUP)]
    local1 = local(1, own[0])
    near = pl.pallas_call(
        edges,
        out_shape=jax.ShapeDtypeStruct((GROUP, 2, 8, TILE), F32),
        in_specs=[VMEM] * GROUP + [ANY],
        out_specs=VMEM,
        compiler_params=params(4),
        name="edges",
    )(*states, local1)
    near = xor_permute(near, "gx", 1)
    out = [
        jax.ShapeDtypeStruct(noise.shape, F32),
        jax.ShapeDtypeStruct((levels, ys, columns), F32),
    ]
    latent, soft = pl.pallas_call(
        finish,
        out_shape=out,
        in_specs=[VMEM] * 9,
        out_specs=[ANY, ANY],
        scratch_shapes=[
            pltpu.VMEM((2, 2, ys, columns + TILE), F32),
            pltpu.VMEM(noise.shape, F32),
            pltpu.VMEM((levels, ys, columns), F32),
            pltpu.SemaphoreType.DMA((4, 2)),
        ],
        compiler_params=params(24),
        name="finish",
    )(local0, local1, reach, bias, *states, near)
    return latent, soft


def solution(mesh):
    return jax.shard_map(
        shards,
        mesh=mesh,
        in_specs=(
            P(("parts", "gz"), None, None, "gx"),
            P(("parts", "gz"), None),
            P(),
            P("parts", "gx"),
            P(),
        ),
        out_specs=(P(("parts", "gz"), None, None, "gx"), P(("parts", "gz"), None, "gx")),
        check_vma=False,
    )
```

time: 277 us -> 41.5 us (0.15)
  other arithmetic: 131 us -> 0.03 us
  waiting for transfers between devices: 71.6 us -> 3.66 us
  starting transfers between devices: 61.7 us -> 11.6 us
  Pallas kernels: 0 us -> 23.8 us
  local copies, waits for them, and re-layouts: 8.68 us -> 1.35 us
    dynamic_update_slice x64 -> x0, other arithmetic: 105 us -> none  [shards(): _, local_fwd = lax.scan(forward, start, (alpha, fwd_gain, noise))]
    ppermute x22 -> x9, waiting for transfers between devices: 71.6 us -> 3.66 us  [xor_permute(): lax.ppermute(value, axis, [(i, i ^ by) for i in range(lax.axis_size(axis))])]
    ppermute x22 -> x9, starting transfers between devices: 61.7 us -> 11.6 us  [xor_permute(): lax.ppermute(value, axis, [(i, i ^ by) for i in range(lax.axis_size(axis))])]
    pallas_call x0 -> x8, Pallas kernels: none -> 23.8 us  [the longest x2 15.3 us: local(): pl.pallas_call(functools.partial(local_field, field), out_shape=jax.Shape...]
    add x20 -> x0, other arithmetic: 21.9 us -> none  [the longest x4 13.6 us: sweep_once(): return field + 0.2 * lap]
    another operation x4 -> x0, local copies, waits for them, and re-layouts: 5.09 us -> none
  transfers between devices with their start and end apart: 22 -> 9, of which waited for: 18 -> 3; matrix products, arithmetic and copies ran while one was open for 0% -> 0% of each run, Pallas kernels for 0% -> 39%
where the time goes in v1:
time: 41.5 us; the launch traced here: 41.2 us
  Pallas kernels  23.8 us (57%)
  starting transfers between devices  11.6 us (28%)
  waiting for transfers between devices  3.66 us (9%)
  local copies, waits for them, and re-layouts  1.35 us (3%)
  between operations  0.79 us (2%)
    pallas_call x2, Pallas kernels, local(): pl.pallas_call(functools.partial(local_field, field), out_shape=jax.Shape...  15.3 us
    ppermute x9, starting transfers between devices, xor_permute(): lax.ppermute(value, axis, [(i, i ^ by) for i in range(lax.axis_size(axis))])  11.6 us
    pallas_call x1, Pallas kernels, shards(): pl.pallas_call(finish, out_shape=out, in_specs=[VMEM] * 9, out_specs=[ANY...  4.73 us
    ppermute x9, waiting for transfers between devices, xor_permute(): lax.ppermute(value, axis, [(i, i ^ by) for i in range(lax.axis_size(axis))])  3.66 us
    pallas_call x1, Pallas kernels, shards(): pl.pallas_call(carries, out_shape=[message] * GROUP + [jax.ShapeDtypeStru...  2.92 us
    unnamed x8, local copies, waits for them, and re-layouts  1.34 us
  transfers between devices with their start and end apart: 9, of which 3 were waited for; matrix products, arithmetic and copies ran while one was open for 0% of the time, Pallas kernels for 39%

profile of v1, /device:TPU:0, one launch (start us, length us, event | category | flops | bytes accessed | tf_op | source)
XLA Modules:
  0.0 41.2 jit_solution(13300403498962565233)
XLA Ops:
  0.6 0.7 %copy-done.1 = s32[32,2]{0,1:T(2,128)S(1)} copy-done((s32[32,2]{0,1:T(2,128)S(1)}, s32[32,2]{0,1:T(2,128)}, u32[]{:S(2)}) %copy-start.1) | copy-done | bytes 280
  1.3 0.7 %copy-done.2 = f32[16]{0:T(128)S(1)} copy-done((f32[16]{0:T(128)S(1)}, f32[16]{0:T(128)}, u32[]{:S(2)}) %copy-start.2) | copy-done | bytes 88
  2.0 2.9 %carries.1 = (f32[2,8,1152]{2,1,0:T(8,128)S(1)}, f32[2,8,1152]{2,1,0:T(8,128)S(1)}, f32[2,8,1152]{2,1,0:T(8,128)S(1)}, f32[2,8,1152]{2,1,0:T(8,128)S(1)}, f32[2,...) custom-call(s32[2,32]{1,0:T(2,128)S(1)} %bitcast.23, f32[16]{0:T(128)S(1)} %copy-done.2, ...), custom_call_target="tpu_custom_call" | custom-call | flops 4194304 | bytes 4194304 | tf_op jit(solution)/shard_map/carries/pallas_call | solution.py:442
  4.9 3.0 %collective-permute-start.1 = (f32[2,8,1152]{2,1,0:T(8,128)S(1)}, f32[2,8,1152]{2,1,0:T(8,128)S(1)}, u32[]{:S(2)}, u32[]{:S(2)}) collective-permute-start(f32[2,8,1152]{2,1,0:T(8,128)S(1)} %get-tuple-element.17), channel_id=1, source_target_pairs={{0,2},{2,0},{4,6},{6,4},{8,10},{10,8},{12,14},{14,12},{1,3},{3,1},... | collective-permute-start | bytes 221192 | tf_op jit(solution)/shard_map/ppermute | solution.py:388
  7.9 1.6 %collective-permute-start.2 = (f32[2,8,1152]{2,1,0:T(8,128)S(1)}, f32[2,8,1152]{2,1,0:T(8,128)S(1)}, u32[]{:S(2)}, u32[]{:S(2)}) collective-permute-start(f32[2,8,1152]{2,1,0:T(8,128)S(1)} %get-tuple-element.18), channel_id=1, source_target_pairs={{0,4},{2,6},{4,0},{6,2},{8,12},{10,14},{12,8},{14,10},{1,5},{3,7},... | collective-permute-start | bytes 221192 | tf_op jit(solution)/shard_map/ppermute | solution.py:388
  9.5 0.0 collective-permute-start.3
  9.5 0.0 collective-permute-start
  9.5 1.2 %collective-permute-done.packed.after = f32[1,2,2,8,128]{4,3,2,1,0:T(8,128)S(1)} collective-permute-done((f32[1,2,2,8,128]{4,3,2,1,0:T(8,128)S(1)}, f32[1,2,2,8,128]{4,3,2,1,0:T(8,128)S(1)}, u32[]{:S(2)}, u32[]{:S(2)}) %collective-permute-start) | collective-permute-done | bytes 16416 | tf_op jit(solution)/shard_map/ppermute | solution.py:388
  10.7 7.7 %local0.1.after.g0 = f32[32,16,1024]{2,1,0:T(8,128)S(1)} custom-call(f32[2,2,32,128]{3,2,1,0:T(8,128)S(1)} %get-tuple-element.14.coef, f32[1,2,2,8,128]{4,3,2,1,0:T(8,128)S(1)} %collective-permute-done.packed.after, f32[32,2,16,1024]{3,2,1,0:T(8,128)} %noise_hbm.5, f32[1,2,2,8,128]{4,3,2,1,0:T(8,128)S(1)} %collective-permute-done.packed.after), custom_call_target="tpu_custom_call" | custom-call | flops 41943040 | bytes 4194304 | tf_op jit(solution)/shard_map/local0/pallas_call | solution.py:468
  18.4 0.0 copy-start
  18.4 0.0 copy-start.3
  18.4 0.0 collective-permute-done.2.m2
  18.4 0.1 group_total.1.after
  18.5 3.0 %collective-permute-start.4 = (f32[8,1152]{1,0:T(8,128)S(1)}, f32[8,1152]{1,0:T(8,128)S(1)}, u32[]{:S(2)}, u32[]{:S(2)}) collective-permute-start(f32[8,1152]{1,0:T(8,128)S(1)} %fusion), channel_id=1, source_target_pairs={{0,8},{2,10},{4,12},{6,14},{8,0},{10,2},{12,4},{14,6},{1,9},{3,11}... | collective-permute-start | bytes 110600 | tf_op jit(solution)/shard_map/ppermute | solution.py:388
  21.6 0.7 %prepare.1 = (f32[2,2,32,128]{3,2,1,0:T(8,128)S(1)}, f32[16,1024]{1,0:T(8,128)S(1)}) custom-call(f32[2,2,32,128]{3,2,1,0:T(8,128)S(1)} %get-tuple-element.14.coef, s32[16,1024]{1,0:T(8,128)S(1)} %copy-done, f32[8]{0:T(128)S(1)} %copy-done.3, f32[2,8,1152]{2,1,0:T(8,128)S(1)} %group_total.1.after), custom_call_target="tpu_custom_call" | custom-call | flops 1048576 | bytes 1048576 | tf_op jit(solution)/shard_map/prepare/pallas_call | solution.py:494
  22.2 1.3 %collective-permute-done.4 = f32[8,1152]{1,0:T(8,128)S(1)} collective-permute-done((f32[8,1152]{1,0:T(8,128)S(1)}, f32[8,1152]{1,0:T(8,128)S(1)}, u32[]{:S(2)}, u32[]{:S(2)}) %collective-permute-start.4) | collective-permute-done | bytes 36896 | tf_op jit(solution)/shard_map/ppermute | solution.py:388
  23.5 0.1 enter_group.1
  23.6 2.3 %collective-permute-start.5 = (f32[2,8,1024]{2,1,0:T(8,128)S(1)}, f32[2,8,1024]{2,1,0:T(8,128)S(1)}, u32[]{:S(2)}, u32[]{:S(2)}) collective-permute-start(f32[2,8,1024]{2,1,0:T(8,128)S(1)} %get-tuple-element.23), channel_id=1, source_target_pairs={{0,2},{2,0},{4,6},{6,4},{8,10},{10,8},{12,14},{14,12},{1,3},{3,1},... | collective-permute-start | bytes 196616 | tf_op jit(solution)/shard_map/ppermute | solution.py:388
  26.0 1.2 %collective-permute-start.6 = (f32[2,8,1024]{2,1,0:T(8,128)S(1)}, f32[2,8,1024]{2,1,0:T(8,128)S(1)}, u32[]{:S(2)}, u32[]{:S(2)}) collective-permute-start(f32[2,8,1024]{2,1,0:T(8,128)S(1)} %get-tuple-element.24), channel_id=1, source_target_pairs={{0,4},{2,6},{4,0},{6,2},{8,12},{10,14},{12,8},{14,10},{1,5},{3,7},... | collective-permute-start | bytes 196616 | tf_op jit(solution)/shard_map/ppermute | solution.py:388
  27.1 0.4 collective-permute-start.7
  27.5 7.7 %local1.1.after.g1 = f32[32,16,1024]{2,1,0:T(8,128)S(1)} custom-call(f32[2,2,32,128]{3,2,1,0:T(8,128)S(1)} %get-tuple-element.14.coef, f32[1,2,2,8,128]{4,3,2,1,0:T(8,128)S(1)} %collective-permute-done.packed.after, f32[32,2,16,1024]{3,2,1,0:T(8,128)} %noise_hbm.5, f32[2,8,1024]{2,1,0:T(8,128)S(1)} %get-tuple-element.21.after.m0), custom_call_target="tpu_custom_call" | custom-call | flops 41943040 | bytes 4194304 | tf_op jit(solution)/shard_map/local1/pallas_call | solution.py:468
  35.2 0.1 collective-permute-start.8
  35.3 1.2 %collective-permute-done.8.halo = f32[4,2,8,128]{3,2,1,0:T(8,128)S(1)} collective-permute-done((f32[4,2,8,128]{3,2,1,0:T(8,128)S(1)}, f32[4,2,8,128]{3,2,1,0:T(8,128)S(1)}, u32[]{:S(2)}, u32[]{:S(2)}) %collective-permute-start.8) | collective-permute-done | bytes 32800 | tf_op jit(solution)/shard_map/ppermute | solution.py:388
  36.5 4.7 %finish.1 = (f32[32,2,16,1024]{3,2,1,0:T(8,128)}, f32[32,16,1024]{2,1,0:T(8,128)}) custom-call(f32[32,16,1024]{2,1,0:T(8,128)S(1)} %local0.1.after.g0, f32[32,16,1024]{2,1,0:T(8,128)S(1)} %local1.1.after.g1, f32[2,2,32,128]{3,2,1,0:T(8,128)S(1)} %get-tuple-element.20.after.reach, f32[16,1024]{1,0:T(8,128)S(1)} %get-tuple-element.22.bias, ...), custom_call_target="tpu_custom_call" | custom-call | tf_op jit(solution)/shard_map/finish/pallas_call | solution.py:533
  (16 shorter events, 0.1 us)
Async XLA Ops:
  0.6 0.7 %copy-start.1 = (s32[32,2]{0,1:T(2,128)S(1)}, s32[32,2]{0,1:T(2,128)}, u32[]{:S(2)}) copy-start(s32[32,2]{0,1:T(2,128)} %param.6) | copy-start | bytes 772
  1.3 0.7 %copy-start.2 = (f32[16]{0:T(128)S(1)}, f32[16]{0:T(128)}, u32[]{:S(2)}) copy-start(f32[16]{0:T(128)} %rates_hbm.1) | copy-start | bytes 196
  4.9 13.5 %collective-permute-start.1 = (f32[2,8,1152]{2,1,0:T(8,128)S(1)}, f32[2,8,1152]{2,1,0:T(8,128)S(1)}, u32[]{:S(2)}, u32[]{:S(2)}) collective-permute-start(f32[2,8,1152]{2,1,0:T(8,128)S(1)} %get-tuple-element.17), channel_id=1, source_target_pairs={{0,2},{2,0},{4,6},{6,4},{8,10},{10,8},{12,14},{14,12},{1,3},{3,1},... | collective-permute-start | bytes 221192 | tf_op jit(solution)/shard_map/ppermute | solution.py:388
  7.9 10.5 %collective-permute-start.2 = (f32[2,8,1152]{2,1,0:T(8,128)S(1)}, f32[2,8,1152]{2,1,0:T(8,128)S(1)}, u32[]{:S(2)}, u32[]{:S(2)}) collective-permute-start(f32[2,8,1152]{2,1,0:T(8,128)S(1)} %get-tuple-element.18), channel_id=1, source_target_pairs={{0,4},{2,6},{4,0},{6,2},{8,12},{10,14},{12,8},{14,10},{1,5},{3,7},... | collective-permute-start | bytes 221192 | tf_op jit(solution)/shard_map/ppermute | solution.py:388
  9.5 8.9 %collective-permute-start.3 = (f32[2,8,1152]{2,1,0:T(8,128)S(1)}, f32[2,8,1152]{2,1,0:T(8,128)S(1)}, u32[]{:S(2)}, u32[]{:S(2)}) collective-permute-start(f32[2,8,1152]{2,1,0:T(8,128)S(1)} %get-tuple-element.19), channel_id=1, source_target_pairs={{0,6},{2,4},{4,2},{6,0},{8,14},{10,12},{12,10},{14,8},{1,7},{3,5},... | collective-permute-start | bytes 221192 | tf_op jit(solution)/shard_map/ppermute | solution.py:388
  9.5 1.2 %collective-permute-start = (f32[1,2,2,8,128]{4,3,2,1,0:T(8,128)S(1)}, f32[1,2,2,8,128]{4,3,2,1,0:T(8,128)S(1)}, u32[]{:S(2)}, u32[]{:S(2)}) collective-permute-start(f32[1,2,2,8,128]{4,3,2,1,0:T(8,128)S(1)} %get-tuple-element.15), channel_id=1, source_target_pairs={{0,1},{1,0},{2,3},{3,2},{4,5},{5,4},{6,7},{7,6},{8,9},{9,8},{10,11... | collective-permute-start | bytes 49160 | tf_op jit(solution)/shard_map/ppermute | solution.py:388
  18.4 3.2 %copy-start = (s32[16,1024]{1,0:T(8,128)S(1)}, s32[16,1024]{1,0:T(8,128)}, u32[]{:S(2)}) copy-start(s32[16,1024]{1,0:T(8,128)} %codes.1) | copy-start | bytes 196612
  18.4 3.2 %copy-start.3 = (f32[8]{0:T(128)S(1)}, f32[8]{0:T(128)}, u32[]{:S(2)}) copy-start(f32[8]{0:T(128)} %thresholds.1) | copy-start | bytes 100
  18.5 5.0 %collective-permute-start.4 = (f32[8,1152]{1,0:T(8,128)S(1)}, f32[8,1152]{1,0:T(8,128)S(1)}, u32[]{:S(2)}, u32[]{:S(2)}) collective-permute-start(f32[8,1152]{1,0:T(8,128)S(1)} %fusion), channel_id=1, source_target_pairs={{0,8},{2,10},{4,12},{6,14},{8,0},{10,2},{12,4},{14,6},{1,9},{3,11}... | collective-permute-start | bytes 110600 | tf_op jit(solution)/shard_map/ppermute | solution.py:388
  23.6 11.5 %collective-permute-start.5 = (f32[2,8,1024]{2,1,0:T(8,128)S(1)}, f32[2,8,1024]{2,1,0:T(8,128)S(1)}, u32[]{:S(2)}, u32[]{:S(2)}) collective-permute-start(f32[2,8,1024]{2,1,0:T(8,128)S(1)} %get-tuple-element.23), channel_id=1, source_target_pairs={{0,2},{2,0},{4,6},{6,4},{8,10},{10,8},{12,14},{14,12},{1,3},{3,1},... | collective-permute-start | bytes 196616 | tf_op jit(solution)/shard_map/ppermute | solution.py:388
  26.0 9.2 %collective-permute-start.6 = (f32[2,8,1024]{2,1,0:T(8,128)S(1)}, f32[2,8,1024]{2,1,0:T(8,128)S(1)}, u32[]{:S(2)}, u32[]{:S(2)}) collective-permute-start(f32[2,8,1024]{2,1,0:T(8,128)S(1)} %get-tuple-element.24), channel_id=1, source_target_pairs={{0,4},{2,6},{4,0},{6,2},{8,12},{10,14},{12,8},{14,10},{1,5},{3,7},... | collective-permute-start | bytes 196616 | tf_op jit(solution)/shard_map/ppermute | solution.py:388
  27.1 8.0 %collective-permute-start.7 = (f32[2,8,1024]{2,1,0:T(8,128)S(1)}, f32[2,8,1024]{2,1,0:T(8,128)S(1)}, u32[]{:S(2)}, u32[]{:S(2)}) collective-permute-start(f32[2,8,1024]{2,1,0:T(8,128)S(1)} %get-tuple-element.25), channel_id=1, source_target_pairs={{0,6},{2,4},{4,2},{6,0},{8,14},{10,12},{12,10},{14,8},{1,7},{3,5},... | collective-permute-start | bytes 196616 | tf_op jit(solution)/shard_map/ppermute | solution.py:388
  35.2 1.3 %collective-permute-start.8 = (f32[4,2,8,128]{3,2,1,0:T(8,128)S(1)}, f32[4,2,8,128]{3,2,1,0:T(8,128)S(1)}, u32[]{:S(2)}, u32[]{:S(2)}) collective-permute-start(f32[4,2,8,128]{3,2,1,0:T(8,128)S(1)} %edges.1), channel_id=1, source_target_pairs={{0,1},{1,0},{2,3},{3,2},{4,5},{5,4},{6,7},{7,6},{8,9},{9,8},{10,11... | collective-permute-start | bytes 98312 | tf_op jit(solution)/shard_map/ppermute | solution.py:388

commit v2 on v1

--- a/solution.py
+++ b/solution.py
@@ -10,7 +10,6 @@
 SWEEPS = 4
 GROUP = 4
 TILE = 128
-EDGE = SWEEPS
 F32 = jnp.float32
 SMEM = pl.BlockSpec(memory_space=pltpu.SMEM)
 ANY = pl.BlockSpec(memory_space=pl.ANY)
@@ -26,52 +25,41 @@
     return jnp.broadcast_to(ref[(*at[:-1], pl.ds(at[-1], 1), slice(None))], (8, TILE))
 
 
-def fill_tables(rates_ref, table):
-    for i in range(rates_ref.shape[0]):
-        alpha = jnp.exp(-splat(rates_ref[i]))
-        table[0, i] = alpha
-        table[1, i] = jnp.sqrt(1.0 - alpha * alpha)
+def coefficients(scale_index, rates):
+    slots = jnp.arange(rates.shape[0], dtype=jnp.int32)
+    hits = (scale_index.T[..., None] == slots).astype(F32)
+    alpha = jnp.exp(-jnp.sum(hits * rates, axis=-1))
+    both = jnp.stack([alpha, jnp.sqrt(1.0 - alpha * alpha)])
+    return jnp.broadcast_to(both[..., None], (*both.shape, TILE))
 
 
 def position():
     return lax.rem(lax.axis_index("gz"), GROUP)
 
 
-def carries(idx_hbm, rates_hbm, noise_hbm, out0, out1, out2, out3, coef, packed, table, pre, wts, tiled, idx, rates, sems):
-    outs = (out0, out1, out2, out3)
+def carries(coef, noise_hbm, out0, out1, out2, out3, packed, tiled0, tiled1, held, pre, wts, sems):
+    outs, tiled = (out0, out1, out2, out3), (tiled0, tiled1)
     levels, columns = noise_hbm.shape[0], noise_hbm.shape[3]
+    tiles = columns // TILE
     pos = position()
     core = lax.axis_index("gx")
-    small = [
-        pltpu.make_async_copy(idx_hbm, idx, sems.at[GROUP, 0]),
-        pltpu.make_async_copy(rates_hbm, rates, sems.at[GROUP, 1]),
-    ]
-    for copy in small:
-        copy.start()
-    order = (1, 2, 3, 0)
-    copies = {}
-    for k in order:
-        s = pos ^ k
-        rows = pl.ds(pl.multiple_of(8 * (s % 2), 8), 8)
-        copies[k] = []
-        for t in range(columns // TILE):
+    copies = []
+    for s in range(GROUP):
+        rows = slice(8 * (s % 2), 8 * (s % 2) + 8)
+        copies.append([])
+        for t in range(tiles):
             source = noise_hbm.at[:, s // 2, rows, pl.ds(t * TILE, TILE)]
-            copies[k].append(pltpu.make_async_copy(source, tiled.at[s // 2, t, :, rows, :], sems.at[k, t]))
-            copies[k][t].start()
-    for copy in small:
-        copy.wait()
-    fill_tables(rates, table)
+            copies[s].append(pltpu.make_async_copy(source, tiled[s // 2].at[t, :, rows, :], sems.at[s, t]))
+            copies[s][t].start()
     for field in range(2):
         run = splat(1.0)
         for k in range(levels):
             pre[k] = run
-            run = run * table[0, idx[field, k]]
+            run = run * row(coef, 0, field, k)
         total = run
         post, gather, after = splat(1.0), splat(0.0), splat(0.0)
         for k in reversed(range(levels)):
-            alpha, gain = table[0, idx[field, k]], table[1, idx[field, k]]
-            coef[0, field, k : k + 1, :] = alpha[:1]
-            coef[1, field, k : k + 1, :] = gain[:1]
+            alpha, gain = row(coef, 0, field, k), row(coef, 1, field, k)
             gather = pre[k] * (1.0 - alpha) + after * gather
             wts[0, field, k] = gain * post
             wts[1, field, k] = gain * gather
@@ -79,16 +67,12 @@
             after = alpha
         wts[0, field, levels] = total
         wts[1, field, levels] = after * gather
-    tiles = columns // TILE
     near = (1 - core) * (tiles - 1)
-    slots = TILE // EDGE
-    slot = lax.rem(lax.broadcasted_iota(jnp.int32, (8, TILE), 1) // EDGE + (1 - core), slots)
-    for k in order:
-        for copy in copies[k]:
+    for s in range(GROUP):
+        for copy in copies[s]:
             copy.wait()
-        s = pos ^ k
-        field = s // 2
-        rows = pl.ds(pl.multiple_of(8 * (s % 2), 8), 8)
+        field, k = s // 2, pos ^ s
+        rows = slice(8 * (s % 2), 8 * (s % 2) + 8)
         for half in range(2):
             ours = range(half * tiles // 2, (half + 1) * tiles // 2)
 
@@ -96,22 +80,28 @@
                 fwd, bwd = wts[0, field, level], wts[1, field, level]
                 new = []
                 for t, (one, two) in zip(ours, sums):
-                    value = tiled[field, t, level, rows, :]
+                    value = tiled[field][t, level, rows, :]
                     new.append((one + fwd * value, two + bwd * value))
                 return tuple(new)
 
-            sums = lax.fori_loop(0, levels, body, ((splat(0.0), splat(0.0)),) * len(ours), unroll=8)
+            sums = lax.fori_loop(0, levels, body, ((splat(0.0), splat(0.0)),) * len(ours), unroll=True)
             for t, (one, two) in zip(ours, sums):
-                outs[k][0, :, t * TILE : (t + 1) * TILE] = one
-                outs[k][1, :, t * TILE : (t + 1) * TILE] = two
-        outs[k][0, :, columns:] = wts[0, field, levels]
-        outs[k][1, :, columns:] = wts[1, field, levels]
-        for first in range(0, levels, slots):
-            edge = splat(0.0)
-            for level in range(first, min(levels, first + slots)):
-                turned = pltpu.roll(tiled[field, near, level, rows, :], EDGE * (level - first), 1)
-                edge = jnp.where(slot == level - first, turned, edge)
-            packed[first // slots, field, s % 2] = edge
+                held[k, 0, :, t * TILE : (t + 1) * TILE] = one
+                held[k, 1, :, t * TILE : (t + 1) * TILE] = two
+        held[k, 0, :, columns:] = wts[0, field, levels]
+        held[k, 1, :, columns:] = wts[1, field, levels]
+    for k in range(GROUP):
+        outs[k][...] = held[k]
+    for field in range(2):
+        flat = tiled[field].reshape(tiles, levels * 16, TILE)
+        for first in range(0, 16, TILE // levels):
+            rows = [
+                flat[near, pl.ds(8 * g * 16 + y, 8, stride=16), :]
+                for y in range(first, first + TILE // levels)
+                for g in range(levels // 8)
+            ]
+            turned = jnp.concatenate(rows, axis=0).T
+            packed[field, first * levels // TILE] = jnp.where(core == 0, turned[TILE - 8 :], turned[:8])
 
 
 def scan_group(held, lanes, f_in, r_in):
@@ -217,82 +207,80 @@
     bias[...] = value
 
 
-def local_field(field, coef, packed, noise_hbm, after, out, buf, work, sems):
-    levels, _, ys, columns = noise_hbm.shape
-    tiles = columns // TILE
-
-    def fetch_group(turn, go):
-        at = pl.ds(pl.multiple_of(turn * 8, 8), 8)
-        for t in range(tiles):
-            source = noise_hbm.at[at, field, :, pl.ds(t * TILE, TILE)]
-            copy = pltpu.make_async_copy(source, buf.at[t, at], sems.at[turn, t])
-            if go:
-                copy.start()
-            else:
-                copy.wait()
-
-    for turn in range(levels // 8):
-        fetch_group(turn, True)
+def local_first(coef, packed, tiled, noise_hbm, out, tiled_next, buf, work, sems):
+    copies = [
+        pltpu.make_async_copy(noise_hbm.at[:, 1, :, pl.ds(t * TILE, TILE)], tiled_next.at[t], sems.at[t])
+        for t in range(tiled.shape[0])
+    ]
+    for copy in copies:
+        copy.start()
+    local_field(0, coef, packed, tiled, None, out, buf, work)
+    for copy in copies:
+        copy.wait()
+
+
+def local_field(field, coef, packed, tiled, after, out, buf, work):
+    tiles, levels, ys, _ = tiled.shape
+    columns = tiles * TILE
+    ranges = TILE // levels
+    span = columns // ranges
+    blocks = span // TILE
+    main = 16
     core = lax.axis_index("gx")
     lane = lax.broadcasted_iota(jnp.int32, (8, TILE), 1)
-    keep = edge_mask()
-    sent = jnp.where(core == 0, lane, TILE - 1 - lane) < EDGE
-    slots = TILE // EDGE
-    for level in range(levels):
-        for top in range(2):
-            edge = packed[level // slots, field, top]
-            edge = pltpu.roll(edge, (TILE - EDGE * (level % slots)) % TILE, 1)
-            buf[tiles, level, 8 * top : 8 * top + 8, :] = jnp.where(sent, edge, 0.0)
-    flat = buf.reshape(tiles + 1, levels * ys, TILE)
-    first, last = lane == 0, lane == TILE - 1
-
-    def sweep(get, put, all_tiles):
-        above = [splat(0.0)] * (tiles + 1)
-        here = get(0)
+    keep_left = (lane >= levels) | (core == 1)
+    keep_right = (lane < TILE - levels) | (core == 0)
+    source = tiled.reshape(tiles, levels * ys, TILE)
+    flat = buf.reshape(tiles, levels * ys, TILE)
+    for slot in range(2):
         for y in range(ys):
-            below = get(y + 1) if y + 1 < ys else [splat(0.0)] * (tiles + 1)
-            right = [pltpu.roll(v, TILE - 1, 1) for v in here]
-            left = [pltpu.roll(v, 1, 1) for v in here]
-            new = []
-            for t in range(tiles + all_tiles):
-                beside = jnp.where(first, left[t - 1], left[t])
-                beside += jnp.where(last, right[(t + 1) % (tiles + 1)], right[t])
-                new.append(here[t] + beside + (above[t] + below[t]))
-            if all_tiles:
-                new[tiles] = new[tiles] * keep
-            put(y, new)
+            work[slot, y, 0:8, :] = splat(0.0)
+            work[slot, y, main + span + 8 :, :] = splat(0.0)
+
+    def pieces(y):
+        return [(c, g, pl.ds(8 * g * ys + y, 8, stride=ys)) for c in range(ranges) for g in range(levels // 8)]
+
+    for y in range(ys):
+        for b in range(blocks):
+            rows = [source[c * blocks + b, at, :] for c, g, at in pieces(y)]
+            work[0, y, main + b * TILE : main + (b + 1) * TILE, :] = jnp.concatenate(rows, axis=0).T
+        edge, place = packed[field, y // ranges], y % ranges
+        left = pltpu.roll(work[0, y, main + span - 8 : main + span, :], levels, 1)
+        right = pltpu.roll(work[0, y, main : main + 8, :], TILE - levels, 1)
+        far_left = pltpu.roll(edge, (TILE - levels * place) % TILE, 1)
+        far_right = pltpu.roll(edge, levels * (ranges - 1 - place), 1)
+        left = jnp.where(keep_left, jnp.where(lane < levels, far_left, left), 0.0)
+        right = jnp.where(keep_right, jnp.where(lane >= TILE - levels, far_right, right), 0.0)
+        work[0, y, main - 8 : main, :] = left
+        work[0, y, main + span : main + span + 8, :] = right
+
+    def block(src, at, before, later, keep=None):
+        above, here = splat(0.0), work[src, 0, at, :]
+        for y in range(ys):
+            below = work[src, y + 1, at, :] if y + 1 < ys else splat(0.0)
+            new = here + (work[src, y, before, :] + work[src, y, later, :]) + (above + below)
+            if keep is not None:
+                new = jnp.where(keep, new, 0.0)
+            work[1 - src, y, at, :] = new
             above, here = here, below
 
-    def group(turn, _):
-        fetch_group(turn, False)
-        base = turn * 8 * ys
-
-        def fetch(y):
-            at = pl.ds(base + y, 8, stride=ys)
-            return [flat[t, at, :] for t in range(tiles + 1)]
-
-        def give(y, new):
-            for t, value in enumerate(new):
-                flat[t, pl.ds(base + y, 8, stride=ys), :] = value
-
-        def saver(slot):
-            def put(y, new):
-                for t, value in enumerate(new):
-                    work[slot, t, y] = value
-
-            return put
-
-        def loader(slot):
-            return lambda y: [work[slot, t, y] for t in range(tiles + 1)]
-
-        get = fetch
-        for turn in range(SWEEPS - 1):
-            sweep(get, saver(turn % 2), True)
-            get = loader(turn % 2)
-        sweep(get, give, False)
-        return 0
-
-    lax.fori_loop(0, levels // 8, group, 0)
+    for turn in range(SWEEPS):
+        src = turn % 2
+
+        def step(r, _, src=src):
+            at = pl.multiple_of(main + 8 * r, 8)
+            block(src, pl.ds(at, 8), pl.ds(at - 1, 8), pl.ds(at + 1, 8))
+            return 0
+
+        lax.fori_loop(0, span // 8, step, 0, unroll=True)
+        if turn + 1 < SWEEPS:
+            for at, keep in ((main - 8, keep_left), (main + span, keep_right)):
+                block(src, pl.ds(at, 8), pl.ds(at - 1, 8), pl.ds(at + 1, 8), keep)
+    for y in range(ys):
+        for b in range(blocks):
+            turned = work[SWEEPS % 2, y, main + b * TILE : main + (b + 1) * TILE, :].T
+            for i, (c, g, at) in enumerate(pieces(y)):
+                flat[c * blocks + b, at, :] = turned[8 * i : 8 * i + 8]
     scale = 0.2**SWEEPS
     spots = [(t, top) for t in range(tiles) for top in range(ys // 8)]
 
@@ -317,8 +305,8 @@
         return tuple(new)
 
     zeros = (splat(0.0),) * len(spots)
-    lax.fori_loop(0, levels, forward, zeros, unroll=2)
-    lax.fori_loop(0, levels, backward, zeros, unroll=2)
+    lax.fori_loop(0, levels, forward, zeros, unroll=True)
+    lax.fori_loop(0, levels, backward, zeros, unroll=True)
 
 
 def edges(m0, m1, m2, m3, after, out):
@@ -364,7 +352,7 @@
                 soft[level, rows, lanes] = half * (0.5 + 0.5 * jnp.tanh(1.5 * two))
             return 0
 
-        lax.fori_loop(0, 2 * tiles, body, 0)
+        lax.fori_loop(0, 2 * tiles, body, 0, unroll=True)
         at = pl.ds(i * step, step)
         copies += [
             pltpu.make_async_copy(latent.at[at], latent_hbm.at[at], sems.at[i, 0]),
@@ -434,53 +422,50 @@
 
 def shards(noise, scale_index, rates, facies_code, thresholds):
     levels, _, ys, columns = noise.shape
-    assert ys == 16 and columns % (2 * TILE) == 0 and levels % 8 == 0
+    assert ys == 16 and levels % 8 == 0 and TILE % levels == 0 and columns * levels % (TILE * TILE) == 0
     tiles = columns // TILE
     groups = lax.axis_size("gz") // GROUP
     message = jax.ShapeDtypeStruct((2, 8, columns + TILE), F32)
-    folds = -(-levels * EDGE // TILE)
-    *mine, coef, packed = pl.pallas_call(
+    coef = coefficients(scale_index, rates)
+    *mine, packed, tiled0 = pl.pallas_call(
         carries,
         out_shape=[message] * GROUP
         + [
-            jax.ShapeDtypeStruct((2, 2, levels, TILE), F32),
-            jax.ShapeDtypeStruct((folds, 2, 2, 8, TILE), F32),
+            jax.ShapeDtypeStruct((2, ys * levels // TILE, 8, TILE), F32),
+            jax.ShapeDtypeStruct((tiles, levels, ys, TILE), F32),
         ],
-        in_specs=[HBM, HBM, HBM],
+        in_specs=[VMEM, HBM],
         out_specs=[VMEM] * (GROUP + 2),
         scratch_shapes=[
-            pltpu.VMEM((2, rates.shape[0], 8, TILE), F32),
+            pltpu.VMEM((tiles, levels, ys, TILE), F32),
+            pltpu.VMEM((GROUP, 2, 8, columns + TILE), F32),
             pltpu.VMEM((levels, 8, TILE), F32),
             pltpu.VMEM((2, 2, levels + 1, 8, TILE), F32),
-            pltpu.VMEM((2, tiles, levels, ys, TILE), F32),
-            pltpu.SMEM((2, levels), jnp.int32),
-            pltpu.SMEM(rates.shape, F32),
-            pltpu.SemaphoreType.DMA((GROUP + 1, tiles)),
+            pltpu.SemaphoreType.DMA((GROUP, tiles)),
         ],
-        compiler_params=params(52),
+        compiler_params=params(50),
         cost_estimate=cost(4 * noise.size, 4 * noise.size),
         name="carries",
-    )(scale_index.T, rates, noise)
+    )(coef, noise)
     got = [mine[0]] + [xor_permute(mine[k], "gz", k) for k in range(1, GROUP)]
     halo = xor_permute(packed, "gx", 1)
 
-    def local(field, after):
-        return pl.pallas_call(
-            functools.partial(local_field, field),
-            out_shape=jax.ShapeDtypeStruct((levels, ys, columns), F32),
-            in_specs=[VMEM, VMEM, HBM, ANY],
-            out_specs=VMEM,
-            scratch_shapes=[
-                pltpu.VMEM((tiles + 1, levels, ys, TILE), F32),
-                pltpu.VMEM((2, tiles + 1, ys, 8, TILE), F32),
-                pltpu.SemaphoreType.DMA((levels // 8, tiles)),
-            ],
-            compiler_params=params(50),
-            cost_estimate=cost(80 * noise.size // 2, 4 * noise.size),
-            name=f"local{field}",
-        )(coef, halo, noise, after)
-
-    local0 = local(0, halo)
+    field_out = jax.ShapeDtypeStruct((levels, ys, columns), F32)
+    field_tiled = jax.ShapeDtypeStruct((tiles, levels, ys, TILE), F32)
+    scratch = [
+        pltpu.VMEM((tiles, levels, ys, TILE), F32),
+        pltpu.VMEM((2, ys, columns * levels // TILE + 32, TILE), F32),
+    ]
+    local0, tiled1 = pl.pallas_call(
+        local_first,
+        out_shape=[field_out, field_tiled],
+        in_specs=[VMEM, VMEM, VMEM, HBM],
+        out_specs=[VMEM] * 2,
+        scratch_shapes=[*scratch, pltpu.SemaphoreType.DMA((tiles,))],
+        compiler_params=params(45),
+        cost_estimate=cost(40 * noise.size, 4 * noise.size),
+        name="local0",
+    )(coef, halo, tiled0, noise)
     held = pltpu.VMEM((GROUP, 2, 8, columns + TILE), F32)
     total = pl.pallas_call(
         group_total,
@@ -516,7 +501,16 @@
         name="enter_group",
     )(*got, entering, reach)
     states = [own[0]] + [xor_permute(own[k], "gz", k) for k in range(1, GROUP)]
-    local1 = local(1, own[0])
+    local1 = pl.pallas_call(
+        functools.partial(local_field, 1),
+        out_shape=field_out,
+        in_specs=[VMEM, VMEM, VMEM, ANY],
+        out_specs=VMEM,
+        scratch_shapes=scratch,
+        compiler_params=params(16),
+        cost_estimate=cost(40 * noise.size, 4 * noise.size),
+        name="local1",
+    )(coef, halo, tiled1, own[0])
     near = pl.pallas_call(
         edges,
         out_shape=jax.ShapeDtypeStruct((GROUP, 2, 8, TILE), F32),
@@ -539,7 +533,7 @@
             pltpu.VMEM((2, 2, ys, columns + TILE), F32),
             pltpu.VMEM(noise.shape, F32),
             pltpu.VMEM((levels, ys, columns), F32),
-            pltpu.SemaphoreType.DMA((4, 2)),
+            pltpu.SemaphoreType.DMA((8, 2)),
         ],
         compiler_params=params(24),
         name="finish",

time: 41.5 us -> 34.7 us (0.84)
  Pallas kernels: 23.8 us -> 17 us
  local copies, waits for them, and re-layouts: 1.35 us -> 0.09 us
  other arithmetic: 0.03 us -> 0.83 us
  waiting for transfers between devices: 3.66 us -> 4.33 us
    pallas_call x2, Pallas kernels: 15.3 us -> 8.38 us  [the longest x1 4.24 us: shards(): pl.pallas_call(local_first, out_shape=[field_out, field_tiled], in_specs=...]
    unnamed x8 -> x4, local copies, waits for them, and re-layouts: 1.34 us -> 0.01 us
    reduce_sum x0 -> x1, other arithmetic: none -> 0.78 us  [coefficients(): alpha = jnp.exp(-jnp.sum(hits * rates, axis=-1))]
    ppermute x9, waiting for transfers between devices: 3.66 us -> 4.33 us  [xor_permute(): lax.ppermute(value, axis, [(i, i ^ by) for i in range(lax.axis_size(axis))])]
  transfers between devices with their start and end apart: 9 -> 9, of which waited for: 3 -> 4; matrix products, arithmetic and copies ran while one was open for 0% -> 0% of each run, Pallas kernels for 39% -> 26%
where the time goes in v2:
time: 34.7 us; the launch traced here: 34.5 us
  Pallas kernels  17 us (49%)
  starting transfers between devices  11.5 us (33%)
  waiting for transfers between devices  4.33 us (12%)
  other arithmetic  0.83 us (2%)
  between operations  0.77 us (2%)
    ppermute x9, starting transfers between devices, xor_permute(): lax.ppermute(value, axis, [(i, i ^ by) for i in range(lax.axis_size(axis))])  11.5 us
    pallas_call x1, Pallas kernels, shards(): pl.pallas_call(finish, out_shape=out, in_specs=[VMEM] * 9, out_specs=[ANY...  4.83 us
    ppermute x9, waiting for transfers between devices, xor_permute(): lax.ppermute(value, axis, [(i, i ^ by) for i in range(lax.axis_size(axis))])  4.33 us
    pallas_call x1, Pallas kernels, shards(): pl.pallas_call(local_first, out_shape=[field_out, field_tiled], in_specs=...  4.24 us
    pallas_call x1, Pallas kernels, shards(): pl.pallas_call(functools.partial(local_field, 1), out_shape=field_out, in...  4.14 us
    pallas_call x1, Pallas kernels, shards(): pl.pallas_call(carries, out_shape=[message] * GROUP + [jax.ShapeDtypeStru...  2.95 us
    reduce_sum x1, other arithmetic, coefficients(): alpha = jnp.exp(-jnp.sum(hits * rates, axis=-1))  0.78 us
  transfers between devices with their start and end apart: 9, of which 4 were waited for; matrix products, arithmetic and copies ran while one was open for 0% of the time, Pallas kernels for 26%

profile of v2, /device:TPU:0, one launch (start us, length us, event | category | flops | bytes accessed | tf_op | source)
XLA Modules:
  0.0 34.5 jit_solution(5201793199004160705)
XLA Ops:
  0.6 0.8 %select_reduce_fusion = f32[2,32]{1,0:T(2,128)S(1)} fusion(f32[16]{0:T(128)} %param.7, s32[2,32]{1,0:T(2,128)} %bitcast.27), kind=kLoop, calls=%fused_computation.9 | loop fusion | flops 3008 | bytes 576 | tf_op jit(solution)/shard_map/reduce_sum | solution.py:31
  1.4 0.1 broadcast_in_dim.4.coef
  1.5 2.9 %carries.1 = (f32[2,8,1152]{2,1,0:T(8,128)S(1)}, f32[2,8,1152]{2,1,0:T(8,128)S(1)}, f32[2,8,1152]{2,1,0:T(8,128)S(1)}, f32[2,8,1152]{2,1,0:T(8,128)S(1)}, f32[2,...) custom-call(f32[2,2,32,128]{3,2,1,0:T(8,128)S(1)} %broadcast_in_dim.4.coef, f32[32,2,16,1024]{3,2,1,0:T(8,128)} %noise_hbm.3), custom_call_target="tpu_custom_call" | custom-call | flops 4194304 | bytes 4194304 | tf_op jit(solution)/shard_map/carries/pallas_call | solution.py:430
  4.5 3.0 %collective-permute-start.1 = (f32[2,8,1152]{2,1,0:T(8,128)S(1)}, f32[2,8,1152]{2,1,0:T(8,128)S(1)}, u32[]{:S(2)}, u32[]{:S(2)}) collective-permute-start(f32[2,8,1152]{2,1,0:T(8,128)S(1)} %get-tuple-element.21), channel_id=1, source_target_pairs={{0,2},{2,0},{4,6},{6,4},{8,10},{10,8},{12,14},{14,12},{1,3},{3,1},... | collective-permute-start | bytes 221192 | tf_op jit(solution)/shard_map/ppermute | solution.py:376
  7.5 1.6 %collective-permute-start.2 = (f32[2,8,1152]{2,1,0:T(8,128)S(1)}, f32[2,8,1152]{2,1,0:T(8,128)S(1)}, u32[]{:S(2)}, u32[]{:S(2)}) collective-permute-start(f32[2,8,1152]{2,1,0:T(8,128)S(1)} %get-tuple-element.22), channel_id=1, source_target_pairs={{0,4},{2,6},{4,0},{6,2},{8,12},{10,14},{12,8},{14,10},{1,5},{3,7},... | collective-permute-start | bytes 221192 | tf_op jit(solution)/shard_map/ppermute | solution.py:376
  9.1 0.0 collective-permute-start.3
  9.1 0.0 collective-permute-start
  9.1 1.2 %collective-permute-done.packed = f32[2,4,8,128]{3,2,1,0:T(8,128)S(1)} collective-permute-done((f32[2,4,8,128]{3,2,1,0:T(8,128)S(1)}, f32[2,4,8,128]{3,2,1,0:T(8,128)S(1)}, u32[]{:S(2)}, u32[]{:S(2)}) %collective-permute-start) | collective-permute-done | bytes 32800 | tf_op jit(solution)/shard_map/ppermute | solution.py:376
  10.3 4.2 %local0.1 = (f32[32,16,1024]{2,1,0:T(8,128)S(1)}, f32[8,32,16,128]{3,2,1,0:T(8,128)S(1)}) custom-call(f32[2,2,32,128]{3,2,1,0:T(8,128)S(1)} %broadcast_in_dim.4.coef, f32[2,4,8,128]{3,2,1,0:T(8,128)S(1)} %collective-permute-done.packed, f32[8,32,16,128]{3,2,1,0:T(8,128)S(1)} %get-tuple-element.17.tiled, f32[32,2,16,1024]{3,2,1,0:T(8,128)} %noise_hbm.3), custom_call_target="tpu_custom_call" | custom-call | flops 41943040 | bytes 4194304 | tf_op jit(solution)/shard_map/local0/pallas_call | solution.py:459
  14.5 0.0 copy-start
  14.6 0.0 copy-start.1
  14.6 0.0 collective-permute-done.1.m1
  14.6 0.1 group_total.1.after
  14.7 3.0 %collective-permute-start.4 = (f32[8,1152]{1,0:T(8,128)S(1)}, f32[8,1152]{1,0:T(8,128)S(1)}, u32[]{:S(2)}, u32[]{:S(2)}) collective-permute-start(f32[8,1152]{1,0:T(8,128)S(1)} %fusion), channel_id=1, source_target_pairs={{0,8},{2,10},{4,12},{6,14},{8,0},{10,2},{12,4},{14,6},{1,9},{3,11}... | collective-permute-start | bytes 110600 | tf_op jit(solution)/shard_map/ppermute | solution.py:376
  17.8 0.7 %prepare.1 = (f32[2,2,32,128]{3,2,1,0:T(8,128)S(1)}, f32[16,1024]{1,0:T(8,128)S(1)}) custom-call(f32[2,2,32,128]{3,2,1,0:T(8,128)S(1)} %broadcast_in_dim.4.coef, s32[16,1024]{1,0:T(8,128)S(1)} %copy-done, f32[8]{0:T(128)S(1)} %copy-done.1, f32[2,8,1152]{2,1,0:T(8,128)S(1)} %group_total.1.after), custom_call_target="tpu_custom_call" | custom-call | flops 1048576 | bytes 1048576 | tf_op jit(solution)/shard_map/prepare/pallas_call | solution.py:479
  18.4 1.3 %collective-permute-done.4 = f32[8,1152]{1,0:T(8,128)S(1)} collective-permute-done((f32[8,1152]{1,0:T(8,128)S(1)}, f32[8,1152]{1,0:T(8,128)S(1)}, u32[]{:S(2)}, u32[]{:S(2)}) %collective-permute-start.4) | collective-permute-done | bytes 36896 | tf_op jit(solution)/shard_map/ppermute | solution.py:376
  19.7 0.1 enter_group.1
  19.8 2.3 %collective-permute-start.5 = (f32[2,8,1024]{2,1,0:T(8,128)S(1)}, f32[2,8,1024]{2,1,0:T(8,128)S(1)}, u32[]{:S(2)}, u32[]{:S(2)}) collective-permute-start(f32[2,8,1024]{2,1,0:T(8,128)S(1)} %get-tuple-element.27), channel_id=1, source_target_pairs={{0,2},{2,0},{4,6},{6,4},{8,10},{10,8},{12,14},{14,12},{1,3},{3,1},... | collective-permute-start | bytes 196616 | tf_op jit(solution)/shard_map/ppermute | solution.py:376
  22.1 1.2 %collective-permute-start.6 = (f32[2,8,1024]{2,1,0:T(8,128)S(1)}, f32[2,8,1024]{2,1,0:T(8,128)S(1)}, u32[]{:S(2)}, u32[]{:S(2)}) collective-permute-start(f32[2,8,1024]{2,1,0:T(8,128)S(1)} %get-tuple-element.28), channel_id=1, source_target_pairs={{0,4},{2,6},{4,0},{6,2},{8,12},{10,14},{12,8},{14,10},{1,5},{3,7},... | collective-permute-start | bytes 196616 | tf_op jit(solution)/shard_map/ppermute | solution.py:376
  23.3 0.4 %collective-permute-start.7 = (f32[2,8,1024]{2,1,0:T(8,128)S(1)}, f32[2,8,1024]{2,1,0:T(8,128)S(1)}, u32[]{:S(2)}, u32[]{:S(2)}) collective-permute-start(f32[2,8,1024]{2,1,0:T(8,128)S(1)} %get-tuple-element.29), channel_id=1, source_target_pairs={{0,6},{2,4},{4,2},{6,0},{8,14},{10,12},{12,10},{14,8},{1,7},{3,5},... | collective-permute-start | bytes 196616 | tf_op jit(solution)/shard_map/ppermute | solution.py:376
  23.7 4.1 %local1.1.after.g1 = f32[32,16,1024]{2,1,0:T(8,128)S(1)} custom-call(f32[2,2,32,128]{3,2,1,0:T(8,128)S(1)} %broadcast_in_dim.4.coef, f32[2,4,8,128]{3,2,1,0:T(8,128)S(1)} %collective-permute-done.packed, f32[8,32,16,128]{3,2,1,0:T(8,128)S(1)} %get-tuple-element.19.tiled, f32[2,8,1024]{2,1,0:T(8,128)S(1)} %get-tuple-element.25.after.m0), custom_call_target="tpu_custom_call" | custom-call | flops 41943040 | bytes 4194304 | tf_op jit(solution)/shard_map/local1/pallas_call | solution.py:504
  27.8 0.6 %collective-permute-done.7.m3 = f32[2,8,1024]{2,1,0:T(8,128)S(1)} collective-permute-done((f32[2,8,1024]{2,1,0:T(8,128)S(1)}, f32[2,8,1024]{2,1,0:T(8,128)S(1)}, u32[]{:S(2)}, u32[]{:S(2)}) %collective-permute-start.7) | collective-permute-done | bytes 65568 | tf_op jit(solution)/shard_map/ppermute | solution.py:376
  28.5 1.2 %collective-permute-done.8.halo = f32[4,2,8,128]{3,2,1,0:T(8,128)S(1)} collective-permute-done((f32[4,2,8,128]{3,2,1,0:T(8,128)S(1)}, f32[4,2,8,128]{3,2,1,0:T(8,128)S(1)}, u32[]{:S(2)}, u32[]{:S(2)}) %collective-permute-start.8) | collective-permute-done | bytes 32800 | tf_op jit(solution)/shard_map/ppermute | solution.py:376
  29.7 4.8 %finish.1 = (f32[32,2,16,1024]{3,2,1,0:T(8,128)}, f32[32,16,1024]{2,1,0:T(8,128)}) custom-call(f32[32,16,1024]{2,1,0:T(8,128)S(1)} %get-tuple-element.18.after.g0, f32[32,16,1024]{2,1,0:T(8,128)S(1)} %local1.1.after.g1, f32[2,2,32,128]{3,2,1,0:T(8,128)S(1)} %get-tuple-element.24.after.reach, f32[16,1024]{1,0:T(8,128)S(1)} %get-tuple-element.26.bias, ...), custom_call_target="tpu_custom_call" | custom-call | tf_op jit(solution)/shard_map/finish/pallas_call | solution.py:527
  (17 shorter events, 0.1 us)
Async XLA Ops:
  4.5 10.1 %collective-permute-start.1 = (f32[2,8,1152]{2,1,0:T(8,128)S(1)}, f32[2,8,1152]{2,1,0:T(8,128)S(1)}, u32[]{:S(2)}, u32[]{:S(2)}) collective-permute-start(f32[2,8,1152]{2,1,0:T(8,128)S(1)} %get-tuple-element.21), channel_id=1, source_target_pairs={{0,2},{2,0},{4,6},{6,4},{8,10},{10,8},{12,14},{14,12},{1,3},{3,1},... | collective-permute-start | bytes 221192 | tf_op jit(solution)/shard_map/ppermute | solution.py:376
  7.5 7.1 %collective-permute-start.2 = (f32[2,8,1152]{2,1,0:T(8,128)S(1)}, f32[2,8,1152]{2,1,0:T(8,128)S(1)}, u32[]{:S(2)}, u32[]{:S(2)}) collective-permute-start(f32[2,8,1152]{2,1,0:T(8,128)S(1)} %get-tuple-element.22), channel_id=1, source_target_pairs={{0,4},{2,6},{4,0},{6,2},{8,12},{10,14},{12,8},{14,10},{1,5},{3,7},... | collective-permute-start | bytes 221192 | tf_op jit(solution)/shard_map/ppermute | solution.py:376
  9.1 5.5 %collective-permute-start.3 = (f32[2,8,1152]{2,1,0:T(8,128)S(1)}, f32[2,8,1152]{2,1,0:T(8,128)S(1)}, u32[]{:S(2)}, u32[]{:S(2)}) collective-permute-start(f32[2,8,1152]{2,1,0:T(8,128)S(1)} %get-tuple-element.23), channel_id=1, source_target_pairs={{0,6},{2,4},{4,2},{6,0},{8,14},{10,12},{12,10},{14,8},{1,7},{3,5},... | collective-permute-start | bytes 221192 | tf_op jit(solution)/shard_map/ppermute | solution.py:376
  9.1 1.2 %collective-permute-start = (f32[2,4,8,128]{3,2,1,0:T(8,128)S(1)}, f32[2,4,8,128]{3,2,1,0:T(8,128)S(1)}, u32[]{:S(2)}, u32[]{:S(2)}) collective-permute-start(f32[2,4,8,128]{3,2,1,0:T(8,128)S(1)} %get-tuple-element.16), channel_id=1, source_target_pairs={{0,1},{1,0},{2,3},{3,2},{4,5},{5,4},{6,7},{7,6},{8,9},{9,8},{10,11... | collective-permute-start | bytes 98312 | tf_op jit(solution)/shard_map/ppermute | solution.py:376
  14.5 3.2 %copy-start = (s32[16,1024]{1,0:T(8,128)S(1)}, s32[16,1024]{1,0:T(8,128)}, u32[]{:S(2)}) copy-start(s32[16,1024]{1,0:T(8,128)} %codes.1) | copy-start | bytes 196612
  14.6 3.2 %copy-start.1 = (f32[8]{0:T(128)S(1)}, f32[8]{0:T(128)}, u32[]{:S(2)}) copy-start(f32[8]{0:T(128)} %thresholds.1) | copy-start | bytes 100
  14.7 5.0 %collective-permute-start.4 = (f32[8,1152]{1,0:T(8,128)S(1)}, f32[8,1152]{1,0:T(8,128)S(1)}, u32[]{:S(2)}, u32[]{:S(2)}) collective-permute-start(f32[8,1152]{1,0:T(8,128)S(1)} %fusion), channel_id=1, source_target_pairs={{0,8},{2,10},{4,12},{6,14},{8,0},{10,2},{12,4},{14,6},{1,9},{3,11}... | collective-permute-start | bytes 110600 | tf_op jit(solution)/shard_map/ppermute | solution.py:376
  19.8 8.0 %collective-permute-start.5 = (f32[2,8,1024]{2,1,0:T(8,128)S(1)}, f32[2,8,1024]{2,1,0:T(8,128)S(1)}, u32[]{:S(2)}, u32[]{:S(2)}) collective-permute-start(f32[2,8,1024]{2,1,0:T(8,128)S(1)} %get-tuple-element.27), channel_id=1, source_target_pairs={{0,2},{2,0},{4,6},{6,4},{8,10},{10,8},{12,14},{14,12},{1,3},{3,1},... | collective-permute-start | bytes 196616 | tf_op jit(solution)/shard_map/ppermute | solution.py:376
  22.1 5.7 %collective-permute-start.6 = (f32[2,8,1024]{2,1,0:T(8,128)S(1)}, f32[2,8,1024]{2,1,0:T(8,128)S(1)}, u32[]{:S(2)}, u32[]{:S(2)}) collective-permute-start(f32[2,8,1024]{2,1,0:T(8,128)S(1)} %get-tuple-element.28), channel_id=1, source_target_pairs={{0,4},{2,6},{4,0},{6,2},{8,12},{10,14},{12,8},{14,10},{1,5},{3,7},... | collective-permute-start | bytes 196616 | tf_op jit(solution)/shard_map/ppermute | solution.py:376
  23.3 5.2 %collective-permute-start.7 = (f32[2,8,1024]{2,1,0:T(8,128)S(1)}, f32[2,8,1024]{2,1,0:T(8,128)S(1)}, u32[]{:S(2)}, u32[]{:S(2)}) collective-permute-start(f32[2,8,1024]{2,1,0:T(8,128)S(1)} %get-tuple-element.29), channel_id=1, source_target_pairs={{0,6},{2,4},{4,2},{6,0},{8,14},{10,12},{12,10},{14,8},{1,7},{3,5},... | collective-permute-start | bytes 196616 | tf_op jit(solution)/shard_map/ppermute | solution.py:376
  28.5 1.2 %collective-permute-start.8 = (f32[4,2,8,128]{3,2,1,0:T(8,128)S(1)}, f32[4,2,8,128]{3,2,1,0:T(8,128)S(1)}, u32[]{:S(2)}, u32[]{:S(2)}) collective-permute-start(f32[4,2,8,128]{3,2,1,0:T(8,128)S(1)} %edges.1), channel_id=1, source_target_pairs={{0,1},{1,0},{2,3},{3,2},{4,5},{5,4},{6,7},{7,6},{8,9},{9,8},{10,11... | collective-permute-start | bytes 98312 | tf_op jit(solution)/shard_map/ppermute | solution.py:376

commit v3 on v2

--- a/solution.py
+++ b/solution.py
@@ -155,29 +155,26 @@
         outs[k][...] = held[pos ^ k, :, :, :columns]
 
 
-def row_neighbours(top, bottom):
-    row = lax.broadcasted_iota(jnp.int32, top.shape, 0)
-    first, last = row == 0, row == 7
-    down_t, down_b = pltpu.roll(top, 1, 0), pltpu.roll(bottom, 1, 0)
-    up_t, up_b = pltpu.roll(top, 7, 0), pltpu.roll(bottom, 7, 0)
-    return (
-        jnp.where(first, 0.0, down_t) + jnp.where(last, up_b, up_t),
-        jnp.where(first, down_t, down_b) + jnp.where(last, 0.0, up_b),
-    )
-
-
-def diffuse(top, bottom, keep):
-    width = top.shape[1]
-
-    def masked(value):
-        return jnp.concatenate([value[:, : width - TILE], value[:, width - TILE :] * keep], axis=1)
-
-    for _ in range(SWEEPS):
-        top, bottom = masked(top), masked(bottom)
-        over_t, over_b = row_neighbours(top, bottom)
-        top = top + over_t + (pltpu.roll(top, 1, 1) + pltpu.roll(top, width - 1, 1))
-        bottom = bottom + over_b + (pltpu.roll(bottom, 1, 1) + pltpu.roll(bottom, width - 1, 1))
-    return top, bottom
+def diffuse(work, tiles, keep):
+    fields = work.shape[1]
+    lane = lax.broadcasted_iota(jnp.int32, (8, TILE), 1)
+    line = lax.broadcasted_iota(jnp.int32, (8, TILE), 0)
+    for turn in range(SWEEPS):
+        src, dst = turn % 2, 1 - turn % 2
+        for field in range(fields):
+            for t in range(tiles):
+                pair = [work[src, field, half, t] for half in range(2)]
+                above = [pltpu.roll(v, 1, 0) for v in pair]
+                below = [pltpu.roll(v, 7, 0) for v in pair]
+                above = [jnp.where(line == 0, 0.0, above[0]), jnp.where(line == 0, above[0], above[1])]
+                below = [jnp.where(line == 7, below[1], below[0]), jnp.where(line == 7, 0.0, below[1])]
+                for half, value in enumerate(pair):
+                    before = work[src, field, half, (t - 1) % tiles]
+                    later = work[src, field, half, (t + 1) % tiles]
+                    side = pltpu.roll(jnp.where(lane == TILE - 1, before, value), 1, 1)
+                    side += pltpu.roll(jnp.where(lane == 0, later, value), TILE - 1, 1)
+                    new = value + side + (above[half] + below[half])
+                    work[dst, field, half, t] = new * keep if t == tiles - 1 else new
 
 
 def edge_mask():
@@ -316,21 +313,42 @@
         out[k] = ref[:, :, near]
 
 
-def finish(g0, g1, reach, bias, m0, m1, m2, m3, halo, latent_hbm, soft_hbm, state, latent, soft, sems):
-    levels, columns = g0.shape[0], g0.shape[2]
+def spread(m0, m1, m2, m3, after, out, work):
+    columns = m0.shape[2]
+    tiles = columns // TILE
     pos = position()
     for k, ref in enumerate((m0, m1, m2, m3)):
         s = pos ^ k
-        rows = pl.ds(pl.multiple_of(8 * (s % 2), 8), 8)
         for kind in range(2):
-            state[kind, s // 2, rows, :columns] = ref[kind]
-            state[kind, s // 2, rows, columns:] = halo[k, kind]
+            for t in range(tiles):
+                work[0, 2 * kind + s // 2, s % 2, t] = ref[kind, :, t * TILE : (t + 1) * TILE]
+    for field in range(4):
+        for half in range(2):
+            work[0, field, half, tiles] = splat(0.0)
+    diffuse(work, tiles + 1, edge_mask())
+    for field in range(4):
+        for half in range(2):
+            for t in range(tiles):
+                at = (field // 2, field % 2, slice(8 * half, 8 * half + 8), slice(t * TILE, (t + 1) * TILE))
+                out[at] = work[SWEEPS % 2, field, half, t] * 0.2**SWEEPS
+
+
+def finish(g0, g1, reach, bias, own, halo, latent_hbm, soft_hbm, state, work, latent, soft, sems):
+    levels, columns = g0.shape[0], g0.shape[2]
+    pos = position()
     keep = edge_mask()
-    for kind in range(2):
-        for field in range(2):
-            top, bottom = diffuse(state[kind, field, 0:8, :], state[kind, field, 8:16, :], keep)
-            state[kind, field, 0:8, :] = top * 0.2**SWEEPS
-            state[kind, field, 8:16, :] = bottom * 0.2**SWEEPS
+    for k in range(GROUP):
+        s = pos ^ k
+        for kind in range(2):
+            work[0, 2 * kind + s // 2, s % 2, 1] = halo[k, kind] * keep
+            work[0, 2 * kind + s // 2, s % 2, 0] = splat(0.0)
+    diffuse(work, 2, keep)
+    state[...] = own[...]
+    near = pl.ds(pl.multiple_of((1 - lax.axis_index("gx")) * (columns - TILE), TILE), TILE)
+    for field in range(4):
+        for half in range(2):
+            at = (field // 2, field % 2, slice(8 * half, 8 * half + 8), near)
+            state[at] += work[SWEEPS % 2, field, half, 0] * 0.2**SWEEPS
     parts = sems.shape[0]
     step = levels // parts
     tiles = columns // TILE
@@ -519,6 +537,16 @@
         compiler_params=params(4),
         name="edges",
     )(*states, local1)
+    spread_out = pl.pallas_call(
+        spread,
+        out_shape=jax.ShapeDtypeStruct((2, 2, ys, columns), F32),
+        in_specs=[VMEM] * GROUP + [ANY],
+        out_specs=VMEM,
+        scratch_shapes=[pltpu.VMEM((2, 4, 2, tiles + 1, 8, TILE), F32)],
+        compiler_params=params(8),
+        cost_estimate=cost(4 * noise.size, noise.size),
+        name="spread",
+    )(*states, near)
     near = xor_permute(near, "gx", 1)
     out = [
         jax.ShapeDtypeStruct(noise.shape, F32),
@@ -527,17 +555,18 @@
     latent, soft = pl.pallas_call(
         finish,
         out_shape=out,
-        in_specs=[VMEM] * 9,
+        in_specs=[VMEM] * 6,
         out_specs=[ANY, ANY],
         scratch_shapes=[
-            pltpu.VMEM((2, 2, ys, columns + TILE), F32),
+            pltpu.VMEM((2, 2, ys, columns), F32),
+            pltpu.VMEM((2, 4, 2, 2, 8, TILE), F32),
             pltpu.VMEM(noise.shape, F32),
             pltpu.VMEM((levels, ys, columns), F32),
             pltpu.SemaphoreType.DMA((8, 2)),
         ],
         compiler_params=params(24),
         name="finish",
-    )(local0, local1, reach, bias, *states, near)
+    )(local0, local1, reach, bias, spread_out, near)
     return latent, soft
 
 

time: 34.7 us -> 33.1 us (0.954)
  Pallas kernels: 17 us -> 16.1 us
  waiting for transfers between devices: 4.33 us -> 3.61 us
    pallas_call x1 -> x2, Pallas kernels: 4.83 us -> 3.97 us  [the longest x1 3.25 us: shards(): pl.pallas_call(finish, out_shape=out, in_specs=[VMEM] * 6, out_specs=[ANY...]
    ppermute x9, waiting for transfers between devices: 4.33 us -> 3.61 us  [xor_permute(): lax.ppermute(value, axis, [(i, i ^ by) for i in range(lax.axis_size(axis))])]
  transfers between devices with their start and end apart: 9 -> 9, of which waited for: 4 -> 4; matrix products, arithmetic and copies ran while one was open for 0% -> 0% of each run, Pallas kernels for 26% -> 30%
where the time goes in v3:
time: 33.1 us; the launch traced here: 32.9 us
  Pallas kernels  16.1 us (49%)
  starting transfers between devices  11.5 us (35%)
  waiting for transfers between devices  3.61 us (11%)
  other arithmetic  0.83 us (3%)
  between operations  0.77 us (2%)
    ppermute x9, starting transfers between devices, xor_permute(): lax.ppermute(value, axis, [(i, i ^ by) for i in range(lax.axis_size(axis))])  11.5 us
    pallas_call x1, Pallas kernels, shards(): pl.pallas_call(local_first, out_shape=[field_out, field_tiled], in_specs=...  4.24 us
    pallas_call x1, Pallas kernels, shards(): pl.pallas_call(functools.partial(local_field, 1), out_shape=field_out, in...  4.14 us
    ppermute x9, waiting for transfers between devices, xor_permute(): lax.ppermute(value, axis, [(i, i ^ by) for i in range(lax.axis_size(axis))])  3.61 us
    pallas_call x1, Pallas kernels, shards(): pl.pallas_call(finish, out_shape=out, in_specs=[VMEM] * 6, out_specs=[ANY...  3.25 us
    pallas_call x1, Pallas kernels, shards(): pl.pallas_call(carries, out_shape=[message] * GROUP + [jax.ShapeDtypeStru...  2.95 us
    reduce_sum x1, other arithmetic, coefficients(): alpha = jnp.exp(-jnp.sum(hits * rates, axis=-1))  0.78 us
    pallas_call x1, Pallas kernels, shards(): pl.pallas_call(spread, out_shape=jax.ShapeDtypeStruct((2, 2, ys, columns)...  0.72 us
  transfers between devices with their start and end apart: 9, of which 4 were waited for; matrix products, arithmetic and copies ran while one was open for 0% of the time, Pallas kernels for 30%

profile of v3, /device:TPU:0, one launch (start us, length us, event | category | flops | bytes accessed | tf_op | source)
XLA Modules:
  0.0 32.9 jit_solution(10963651984243621083)
XLA Ops:
  0.6 0.8 %select_reduce_fusion = f32[2,32]{1,0:T(2,128)S(1)} fusion(f32[16]{0:T(128)} %param.7, s32[2,32]{1,0:T(2,128)} %bitcast.27), kind=kLoop, calls=%fused_computation.9 | loop fusion | flops 3008 | bytes 576 | tf_op jit(solution)/shard_map/reduce_sum | solution.py:31
  1.4 0.1 broadcast_in_dim.4.coef
  1.5 2.9 %carries.1 = (f32[2,8,1152]{2,1,0:T(8,128)S(1)}, f32[2,8,1152]{2,1,0:T(8,128)S(1)}, f32[2,8,1152]{2,1,0:T(8,128)S(1)}, f32[2,8,1152]{2,1,0:T(8,128)S(1)}, f32[2,...) custom-call(f32[2,2,32,128]{3,2,1,0:T(8,128)S(1)} %broadcast_in_dim.4.coef, f32[32,2,16,1024]{3,2,1,0:T(8,128)} %noise_hbm.3), custom_call_target="tpu_custom_call" | custom-call | flops 4194304 | bytes 4194304 | tf_op jit(solution)/shard_map/carries/pallas_call | solution.py:448
  4.5 3.0 %collective-permute-start.1 = (f32[2,8,1152]{2,1,0:T(8,128)S(1)}, f32[2,8,1152]{2,1,0:T(8,128)S(1)}, u32[]{:S(2)}, u32[]{:S(2)}) collective-permute-start(f32[2,8,1152]{2,1,0:T(8,128)S(1)} %get-tuple-element.21), channel_id=1, source_target_pairs={{0,2},{2,0},{4,6},{6,4},{8,10},{10,8},{12,14},{14,12},{1,3},{3,1},... | collective-permute-start | bytes 221192 | tf_op jit(solution)/shard_map/ppermute | solution.py:394
  7.5 1.6 %collective-permute-start.2 = (f32[2,8,1152]{2,1,0:T(8,128)S(1)}, f32[2,8,1152]{2,1,0:T(8,128)S(1)}, u32[]{:S(2)}, u32[]{:S(2)}) collective-permute-start(f32[2,8,1152]{2,1,0:T(8,128)S(1)} %get-tuple-element.22), channel_id=1, source_target_pairs={{0,4},{2,6},{4,0},{6,2},{8,12},{10,14},{12,8},{14,10},{1,5},{3,7},... | collective-permute-start | bytes 221192 | tf_op jit(solution)/shard_map/ppermute | solution.py:394
  9.1 0.0 collective-permute-start.3
  9.1 0.0 collective-permute-start
  9.1 1.2 %collective-permute-done.packed = f32[2,4,8,128]{3,2,1,0:T(8,128)S(1)} collective-permute-done((f32[2,4,8,128]{3,2,1,0:T(8,128)S(1)}, f32[2,4,8,128]{3,2,1,0:T(8,128)S(1)}, u32[]{:S(2)}, u32[]{:S(2)}) %collective-permute-start) | collective-permute-done | bytes 32800 | tf_op jit(solution)/shard_map/ppermute | solution.py:394
  10.3 4.2 %local0.1 = (f32[32,16,1024]{2,1,0:T(8,128)S(1)}, f32[8,32,16,128]{3,2,1,0:T(8,128)S(1)}) custom-call(f32[2,2,32,128]{3,2,1,0:T(8,128)S(1)} %broadcast_in_dim.4.coef, f32[2,4,8,128]{3,2,1,0:T(8,128)S(1)} %collective-permute-done.packed, f32[8,32,16,128]{3,2,1,0:T(8,128)S(1)} %get-tuple-element.17.tiled, f32[32,2,16,1024]{3,2,1,0:T(8,128)} %noise_hbm.3), custom_call_target="tpu_custom_call" | custom-call | flops 41943040 | bytes 4194304 | tf_op jit(solution)/shard_map/local0/pallas_call | solution.py:477
  14.5 0.0 copy-start
  14.6 0.0 copy-start.1
  14.6 0.1 group_total.1.after
  14.7 3.0 %collective-permute-start.4 = (f32[8,1152]{1,0:T(8,128)S(1)}, f32[8,1152]{1,0:T(8,128)S(1)}, u32[]{:S(2)}, u32[]{:S(2)}) collective-permute-start(f32[8,1152]{1,0:T(8,128)S(1)} %fusion), channel_id=1, source_target_pairs={{0,8},{2,10},{4,12},{6,14},{8,0},{10,2},{12,4},{14,6},{1,9},{3,11}... | collective-permute-start | bytes 110600 | tf_op jit(solution)/shard_map/ppermute | solution.py:394
  17.8 0.7 %prepare.1 = (f32[2,2,32,128]{3,2,1,0:T(8,128)S(1)}, f32[16,1024]{1,0:T(8,128)S(1)}) custom-call(f32[2,2,32,128]{3,2,1,0:T(8,128)S(1)} %broadcast_in_dim.4.coef, s32[16,1024]{1,0:T(8,128)S(1)} %copy-done, f32[8]{0:T(128)S(1)} %copy-done.1, f32[2,8,1152]{2,1,0:T(8,128)S(1)} %group_total.1.after), custom_call_target="tpu_custom_call" | custom-call | flops 1048576 | bytes 1048576 | tf_op jit(solution)/shard_map/prepare/pallas_call | solution.py:497
  18.4 1.3 %collective-permute-done.4 = f32[8,1152]{1,0:T(8,128)S(1)} collective-permute-done((f32[8,1152]{1,0:T(8,128)S(1)}, f32[8,1152]{1,0:T(8,128)S(1)}, u32[]{:S(2)}, u32[]{:S(2)}) %collective-permute-start.4) | collective-permute-done | bytes 36896 | tf_op jit(solution)/shard_map/ppermute | solution.py:394
  19.7 0.1 enter_group.1
  19.8 2.3 %collective-permute-start.5 = (f32[2,8,1024]{2,1,0:T(8,128)S(1)}, f32[2,8,1024]{2,1,0:T(8,128)S(1)}, u32[]{:S(2)}, u32[]{:S(2)}) collective-permute-start(f32[2,8,1024]{2,1,0:T(8,128)S(1)} %get-tuple-element.27), channel_id=1, source_target_pairs={{0,2},{2,0},{4,6},{6,4},{8,10},{10,8},{12,14},{14,12},{1,3},{3,1},... | collective-permute-start | bytes 196616 | tf_op jit(solution)/shard_map/ppermute | solution.py:394
  22.1 1.2 %collective-permute-start.6 = (f32[2,8,1024]{2,1,0:T(8,128)S(1)}, f32[2,8,1024]{2,1,0:T(8,128)S(1)}, u32[]{:S(2)}, u32[]{:S(2)}) collective-permute-start(f32[2,8,1024]{2,1,0:T(8,128)S(1)} %get-tuple-element.28), channel_id=1, source_target_pairs={{0,4},{2,6},{4,0},{6,2},{8,12},{10,14},{12,8},{14,10},{1,5},{3,7},... | collective-permute-start | bytes 196616 | tf_op jit(solution)/shard_map/ppermute | solution.py:394
  23.3 0.4 %collective-permute-start.7 = (f32[2,8,1024]{2,1,0:T(8,128)S(1)}, f32[2,8,1024]{2,1,0:T(8,128)S(1)}, u32[]{:S(2)}, u32[]{:S(2)}) collective-permute-start(f32[2,8,1024]{2,1,0:T(8,128)S(1)} %get-tuple-element.29), channel_id=1, source_target_pairs={{0,6},{2,4},{4,2},{6,0},{8,14},{10,12},{12,10},{14,8},{1,7},{3,5},... | collective-permute-start | bytes 196616 | tf_op jit(solution)/shard_map/ppermute | solution.py:394
  23.7 4.1 %local1.1.after.g1 = f32[32,16,1024]{2,1,0:T(8,128)S(1)} custom-call(f32[2,2,32,128]{3,2,1,0:T(8,128)S(1)} %broadcast_in_dim.4.coef, f32[2,4,8,128]{3,2,1,0:T(8,128)S(1)} %collective-permute-done.packed, f32[8,32,16,128]{3,2,1,0:T(8,128)S(1)} %get-tuple-element.19.tiled, f32[2,8,1024]{2,1,0:T(8,128)S(1)} %get-tuple-element.25.after.m0), custom_call_target="tpu_custom_call" | custom-call | flops 41943040 | bytes 4194304 | tf_op jit(solution)/shard_map/local1/pallas_call | solution.py:522
  27.8 0.6 %collective-permute-done.7.m3 = f32[2,8,1024]{2,1,0:T(8,128)S(1)} collective-permute-done((f32[2,8,1024]{2,1,0:T(8,128)S(1)}, f32[2,8,1024]{2,1,0:T(8,128)S(1)}, u32[]{:S(2)}, u32[]{:S(2)}) %collective-permute-start.7) | collective-permute-done | bytes 65568 | tf_op jit(solution)/shard_map/ppermute | solution.py:394
  28.5 0.7 %spread.1.own = f32[2,2,16,1024]{3,2,1,0:T(8,128)S(1)} custom-call(f32[2,8,1024]{2,1,0:T(8,128)S(1)} %get-tuple-element.25.after.m0, f32[2,8,1024]{2,1,0:T(8,128)S(1)} %collective-permute-done.5.m1, f32[2,8,1024]{2,1,0:T(8,128)S(1)} %collective-permute-done.6.m2, f32[2,8,1024]{2,1,0:T(8,128)S(1)} %collective-permute-done.7.m3, f32[4,2,8,128]{3,2,1,0:T(8,128)S(1)} %edges.1.after), custom_call_target="tpu_custom_call" | custom-call | flops 4194304 | bytes 1048576 | tf_op jit(solution)/shard_map/spread/pallas_call | solution.py:540
  29.2 0.5 %collective-permute-done.8.halo = f32[4,2,8,128]{3,2,1,0:T(8,128)S(1)} collective-permute-done((f32[4,2,8,128]{3,2,1,0:T(8,128)S(1)}, f32[4,2,8,128]{3,2,1,0:T(8,128)S(1)}, u32[]{:S(2)}, u32[]{:S(2)}) %collective-permute-start.8) | collective-permute-done | bytes 32800 | tf_op jit(solution)/shard_map/ppermute | solution.py:394
  29.7 3.2 %finish.1 = (f32[32,2,16,1024]{3,2,1,0:T(8,128)}, f32[32,16,1024]{2,1,0:T(8,128)}) custom-call(f32[32,16,1024]{2,1,0:T(8,128)S(1)} %get-tuple-element.18.after.g0, f32[32,16,1024]{2,1,0:T(8,128)S(1)} %local1.1.after.g1, f32[2,2,32,128]{3,2,1,0:T(8,128)S(1)} %get-tuple-element.24.after.reach, f32[16,1024]{1,0:T(8,128)S(1)} %get-tuple-element.26.bias, ...), custom_call_target="tpu_custom_call" | custom-call | tf_op jit(solution)/shard_map/finish/pallas_call | solution.py:555
  (18 shorter events, 0.1 us)
Async XLA Ops:
  4.5 10.1 %collective-permute-start.1 = (f32[2,8,1152]{2,1,0:T(8,128)S(1)}, f32[2,8,1152]{2,1,0:T(8,128)S(1)}, u32[]{:S(2)}, u32[]{:S(2)}) collective-permute-start(f32[2,8,1152]{2,1,0:T(8,128)S(1)} %get-tuple-element.21), channel_id=1, source_target_pairs={{0,2},{2,0},{4,6},{6,4},{8,10},{10,8},{12,14},{14,12},{1,3},{3,1},... | collective-permute-start | bytes 221192 | tf_op jit(solution)/shard_map/ppermute | solution.py:394
  7.5 7.1 %collective-permute-start.2 = (f32[2,8,1152]{2,1,0:T(8,128)S(1)}, f32[2,8,1152]{2,1,0:T(8,128)S(1)}, u32[]{:S(2)}, u32[]{:S(2)}) collective-permute-start(f32[2,8,1152]{2,1,0:T(8,128)S(1)} %get-tuple-element.22), channel_id=1, source_target_pairs={{0,4},{2,6},{4,0},{6,2},{8,12},{10,14},{12,8},{14,10},{1,5},{3,7},... | collective-permute-start | bytes 221192 | tf_op jit(solution)/shard_map/ppermute | solution.py:394
  9.1 5.5 %collective-permute-start.3 = (f32[2,8,1152]{2,1,0:T(8,128)S(1)}, f32[2,8,1152]{2,1,0:T(8,128)S(1)}, u32[]{:S(2)}, u32[]{:S(2)}) collective-permute-start(f32[2,8,1152]{2,1,0:T(8,128)S(1)} %get-tuple-element.23), channel_id=1, source_target_pairs={{0,6},{2,4},{4,2},{6,0},{8,14},{10,12},{12,10},{14,8},{1,7},{3,5},... | collective-permute-start | bytes 221192 | tf_op jit(solution)/shard_map/ppermute | solution.py:394
  9.1 1.2 %collective-permute-start = (f32[2,4,8,128]{3,2,1,0:T(8,128)S(1)}, f32[2,4,8,128]{3,2,1,0:T(8,128)S(1)}, u32[]{:S(2)}, u32[]{:S(2)}) collective-permute-start(f32[2,4,8,128]{3,2,1,0:T(8,128)S(1)} %get-tuple-element.16), channel_id=1, source_target_pairs={{0,1},{1,0},{2,3},{3,2},{4,5},{5,4},{6,7},{7,6},{8,9},{9,8},{10,11... | collective-permute-start | bytes 98312 | tf_op jit(solution)/shard_map/ppermute | solution.py:394
  14.5 3.2 %copy-start = (s32[16,1024]{1,0:T(8,128)S(1)}, s32[16,1024]{1,0:T(8,128)}, u32[]{:S(2)}) copy-start(s32[16,1024]{1,0:T(8,128)} %codes.1) | copy-start | bytes 196612
  14.6 3.2 %copy-start.1 = (f32[8]{0:T(128)S(1)}, f32[8]{0:T(128)}, u32[]{:S(2)}) copy-start(f32[8]{0:T(128)} %thresholds.1) | copy-start | bytes 100
  14.7 5.0 %collective-permute-start.4 = (f32[8,1152]{1,0:T(8,128)S(1)}, f32[8,1152]{1,0:T(8,128)S(1)}, u32[]{:S(2)}, u32[]{:S(2)}) collective-permute-start(f32[8,1152]{1,0:T(8,128)S(1)} %fusion), channel_id=1, source_target_pairs={{0,8},{2,10},{4,12},{6,14},{8,0},{10,2},{12,4},{14,6},{1,9},{3,11}... | collective-permute-start | bytes 110600 | tf_op jit(solution)/shard_map/ppermute | solution.py:394
  19.8 8.0 %collective-permute-start.5 = (f32[2,8,1024]{2,1,0:T(8,128)S(1)}, f32[2,8,1024]{2,1,0:T(8,128)S(1)}, u32[]{:S(2)}, u32[]{:S(2)}) collective-permute-start(f32[2,8,1024]{2,1,0:T(8,128)S(1)} %get-tuple-element.27), channel_id=1, source_target_pairs={{0,2},{2,0},{4,6},{6,4},{8,10},{10,8},{12,14},{14,12},{1,3},{3,1},... | collective-permute-start | bytes 196616 | tf_op jit(solution)/shard_map/ppermute | solution.py:394
  22.1 5.7 %collective-permute-start.6 = (f32[2,8,1024]{2,1,0:T(8,128)S(1)}, f32[2,8,1024]{2,1,0:T(8,128)S(1)}, u32[]{:S(2)}, u32[]{:S(2)}) collective-permute-start(f32[2,8,1024]{2,1,0:T(8,128)S(1)} %get-tuple-element.28), channel_id=1, source_target_pairs={{0,4},{2,6},{4,0},{6,2},{8,12},{10,14},{12,8},{14,10},{1,5},{3,7},... | collective-permute-start | bytes 196616 | tf_op jit(solution)/shard_map/ppermute | solution.py:394
  23.3 5.2 %collective-permute-start.7 = (f32[2,8,1024]{2,1,0:T(8,128)S(1)}, f32[2,8,1024]{2,1,0:T(8,128)S(1)}, u32[]{:S(2)}, u32[]{:S(2)}) collective-permute-start(f32[2,8,1024]{2,1,0:T(8,128)S(1)} %get-tuple-element.29), channel_id=1, source_target_pairs={{0,6},{2,4},{4,2},{6,0},{8,14},{10,12},{12,10},{14,8},{1,7},{3,5},... | collective-permute-start | bytes 196616 | tf_op jit(solution)/shard_map/ppermute | solution.py:394
  28.5 1.2 %collective-permute-start.8 = (f32[4,2,8,128]{3,2,1,0:T(8,128)S(1)}, f32[4,2,8,128]{3,2,1,0:T(8,128)S(1)}, u32[]{:S(2)}, u32[]{:S(2)}) collective-permute-start(f32[4,2,8,128]{3,2,1,0:T(8,128)S(1)} %edges.1.after), channel_id=1, source_target_pairs={{0,1},{1,0},{2,3},{3,2},{4,5},{5,4},{6,7},{7,6},{8,9},{9,8},{10,11... | collective-permute-start | bytes 98312 | tf_op jit(solution)/shard_map/ppermute | solution.py:394

commit v4 on v3

--- a/solution.py
+++ b/solution.py
@@ -25,24 +25,29 @@
     return jnp.broadcast_to(ref[(*at[:-1], pl.ds(at[-1], 1), slice(None))], (8, TILE))
 
 
-def coefficients(scale_index, rates):
-    slots = jnp.arange(rates.shape[0], dtype=jnp.int32)
-    hits = (scale_index.T[..., None] == slots).astype(F32)
-    alpha = jnp.exp(-jnp.sum(hits * rates, axis=-1))
-    both = jnp.stack([alpha, jnp.sqrt(1.0 - alpha * alpha)])
-    return jnp.broadcast_to(both[..., None], (*both.shape, TILE))
+def fill_tables(rates, table):
+    for i in range(rates.shape[0]):
+        alpha = jnp.exp(-splat(rates[i]))
+        table[0, i] = alpha
+        table[1, i] = jnp.sqrt(1.0 - alpha * alpha)
 
 
 def position():
     return lax.rem(lax.axis_index("gz"), GROUP)
 
 
-def carries(coef, noise_hbm, out0, out1, out2, out3, packed, tiled0, tiled1, held, pre, wts, sems):
+def carries(idx_hbm, rates_hbm, noise_hbm, out0, out1, out2, out3, coef, packed, tiled0, tiled1, held, table, pre, wts, idx, rates, sems):
     outs, tiled = (out0, out1, out2, out3), (tiled0, tiled1)
     levels, columns = noise_hbm.shape[0], noise_hbm.shape[3]
     tiles = columns // TILE
     pos = position()
     core = lax.axis_index("gx")
+    small = [
+        pltpu.make_async_copy(idx_hbm, idx, sems.at[GROUP, 0]),
+        pltpu.make_async_copy(rates_hbm, rates, sems.at[GROUP, 1]),
+    ]
+    for copy in small:
+        copy.start()
     copies = []
     for s in range(GROUP):
         rows = slice(8 * (s % 2), 8 * (s % 2) + 8)
@@ -51,15 +56,20 @@
             source = noise_hbm.at[:, s // 2, rows, pl.ds(t * TILE, TILE)]
             copies[s].append(pltpu.make_async_copy(source, tiled[s // 2].at[t, :, rows, :], sems.at[s, t]))
             copies[s][t].start()
+    for copy in small:
+        copy.wait()
+    fill_tables(rates, table)
     for field in range(2):
         run = splat(1.0)
         for k in range(levels):
             pre[k] = run
-            run = run * row(coef, 0, field, k)
+            run = run * table[0, idx[field, k]]
         total = run
         post, gather, after = splat(1.0), splat(0.0), splat(0.0)
         for k in reversed(range(levels)):
-            alpha, gain = row(coef, 0, field, k), row(coef, 1, field, k)
+            alpha, gain = table[0, idx[field, k]], table[1, idx[field, k]]
+            coef[0, field, k : k + 1, :] = alpha[:1]
+            coef[1, field, k : k + 1, :] = gain[:1]
             gather = pre[k] * (1.0 - alpha) + after * gather
             wts[0, field, k] = gain * post
             wts[1, field, k] = gain * gather
@@ -90,18 +100,19 @@
                 held[k, 1, :, t * TILE : (t + 1) * TILE] = two
         held[k, 0, :, columns:] = wts[0, field, levels]
         held[k, 1, :, columns:] = wts[1, field, levels]
-    for k in range(GROUP):
-        outs[k][...] = held[k]
-    for field in range(2):
+        if s % 2 == 0:
+            continue
         flat = tiled[field].reshape(tiles, levels * 16, TILE)
         for first in range(0, 16, TILE // levels):
-            rows = [
+            parts = [
                 flat[near, pl.ds(8 * g * 16 + y, 8, stride=16), :]
                 for y in range(first, first + TILE // levels)
                 for g in range(levels // 8)
             ]
-            turned = jnp.concatenate(rows, axis=0).T
+            turned = jnp.concatenate(parts, axis=0).T
             packed[field, first * levels // TILE] = jnp.where(core == 0, turned[TILE - 8 :], turned[:8])
+    for k in range(GROUP):
+        outs[k][...] = held[k]
 
 
 def scan_group(held, lanes, f_in, r_in):
@@ -380,6 +391,10 @@
             copy.start()
     for copy in copies:
         copy.wait()
+
+
+def in_hbm(value):
+    return pltpu.with_memory_space_constraint(value, pltpu.HBM)
 
 
 def params(mib):
@@ -444,27 +459,30 @@
     tiles = columns // TILE
     groups = lax.axis_size("gz") // GROUP
     message = jax.ShapeDtypeStruct((2, 8, columns + TILE), F32)
-    coef = coefficients(scale_index, rates)
-    *mine, packed, tiled0 = pl.pallas_call(
+    *mine, coef, packed, tiled0 = pl.pallas_call(
         carries,
         out_shape=[message] * GROUP
         + [
+            jax.ShapeDtypeStruct((2, 2, levels, TILE), F32),
             jax.ShapeDtypeStruct((2, ys * levels // TILE, 8, TILE), F32),
             jax.ShapeDtypeStruct((tiles, levels, ys, TILE), F32),
         ],
-        in_specs=[VMEM, HBM],
-        out_specs=[VMEM] * (GROUP + 2),
+        in_specs=[HBM, HBM, HBM],
+        out_specs=[VMEM] * (GROUP + 3),
         scratch_shapes=[
             pltpu.VMEM((tiles, levels, ys, TILE), F32),
             pltpu.VMEM((GROUP, 2, 8, columns + TILE), F32),
+            pltpu.VMEM((2, rates.shape[0], 8, TILE), F32),
             pltpu.VMEM((levels, 8, TILE), F32),
             pltpu.VMEM((2, 2, levels + 1, 8, TILE), F32),
-            pltpu.SemaphoreType.DMA((GROUP, tiles)),
+            pltpu.SMEM((2, levels), jnp.int32),
+            pltpu.SMEM(rates.shape, F32),
+            pltpu.SemaphoreType.DMA((GROUP + 1, tiles)),
         ],
         compiler_params=params(50),
         cost_estimate=cost(4 * noise.size, 4 * noise.size),
         name="carries",
-    )(coef, noise)
+    )(in_hbm(scale_index.T), in_hbm(rates), in_hbm(noise))
     got = [mine[0]] + [xor_permute(mine[k], "gz", k) for k in range(1, GROUP)]
     halo = xor_permute(packed, "gx", 1)
 

time: 33.1 us -> 32.2 us (0.973)
  other arithmetic: 0.83 us -> 0.03 us
    reduce_sum x1 -> x0, other arithmetic: 0.78 us -> none  [coefficients(): alpha = jnp.exp(-jnp.sum(hits * rates, axis=-1))]
where the time goes in v4:
time: 32.2 us; the launch traced here: 32.1 us
  Pallas kernels  16.1 us (50%)
  starting transfers between devices  11.5 us (36%)
  waiting for transfers between devices  3.61 us (11%)
  between operations  0.76 us (2%)
    ppermute x9, starting transfers between devices, xor_permute(): lax.ppermute(value, axis, [(i, i ^ by) for i in range(lax.axis_size(axis))])  11.5 us
    pallas_call x1, Pallas kernels, shards(): pl.pallas_call(local_first, out_shape=[field_out, field_tiled], in_specs=...  4.24 us
    pallas_call x1, Pallas kernels, shards(): pl.pallas_call(functools.partial(local_field, 1), out_shape=field_out, in...  4.14 us
    ppermute x9, waiting for transfers between devices, xor_permute(): lax.ppermute(value, axis, [(i, i ^ by) for i in range(lax.axis_size(axis))])  3.61 us
    pallas_call x1, Pallas kernels, shards(): pl.pallas_call(finish, out_shape=out, in_specs=[VMEM] * 6, out_specs=[ANY...  3.25 us
    pallas_call x1, Pallas kernels, shards(): pl.pallas_call(carries, out_shape=[message] * GROUP + [jax.ShapeDtypeStru...  2.94 us
    pallas_call x1, Pallas kernels, shards(): pl.pallas_call(spread, out_shape=jax.ShapeDtypeStruct((2, 2, ys, columns)...  0.72 us
    pallas_call x1, Pallas kernels, shards(): pl.pallas_call(prepare, out_shape=[jax.ShapeDtypeStruct((2, 2, levels, TI...  0.66 us
  transfers between devices with their start and end apart: 9, of which 4 were waited for; matrix products, arithmetic and copies ran while one was open for 0% of the time, Pallas kernels for 30%

profile of v4, /device:TPU:0, one launch (start us, length us, event | category | flops | bytes accessed | tf_op | source)
XLA Modules:
  0.0 32.1 jit_solution(71186908693085713)
XLA Ops:
  0.6 2.9 %carries.1 = (f32[2,8,1152]{2,1,0:T(8,128)S(1)}, f32[2,8,1152]{2,1,0:T(8,128)S(1)}, f32[2,8,1152]{2,1,0:T(8,128)S(1)}, f32[2,8,1152]{2,1,0:T(8,128)S(1)}, f32[2,...) custom-call(s32[2,32]{1,0:T(2,128)} %bitcast.23, f32[16]{0:T(128)} %rates_hbm.1, ...), custom_call_target="tpu_custom_call" | custom-call | flops 4194304 | bytes 4194304 | tf_op jit(solution)/shard_map/carries/pallas_call | solution.py:462
  3.6 3.0 %collective-permute-start.1 = (f32[2,8,1152]{2,1,0:T(8,128)S(1)}, f32[2,8,1152]{2,1,0:T(8,128)S(1)}, u32[]{:S(2)}, u32[]{:S(2)}) collective-permute-start(f32[2,8,1152]{2,1,0:T(8,128)S(1)} %get-tuple-element.23), channel_id=1, source_target_pairs={{0,2},{2,0},{4,6},{6,4},{8,10},{10,8},{12,14},{14,12},{1,3},{3,1},... | collective-permute-start | bytes 221192 | tf_op jit(solution)/shard_map/ppermute | solution.py:409
  6.6 1.6 %collective-permute-start.2 = (f32[2,8,1152]{2,1,0:T(8,128)S(1)}, f32[2,8,1152]{2,1,0:T(8,128)S(1)}, u32[]{:S(2)}, u32[]{:S(2)}) collective-permute-start(f32[2,8,1152]{2,1,0:T(8,128)S(1)} %get-tuple-element.24), channel_id=1, source_target_pairs={{0,4},{2,6},{4,0},{6,2},{8,12},{10,14},{12,8},{14,10},{1,5},{3,7},... | collective-permute-start | bytes 221192 | tf_op jit(solution)/shard_map/ppermute | solution.py:409
  8.2 0.0 collective-permute-start
  8.2 1.2 %collective-permute-done.packed = f32[2,4,8,128]{3,2,1,0:T(8,128)S(1)} collective-permute-done((f32[2,4,8,128]{3,2,1,0:T(8,128)S(1)}, f32[2,4,8,128]{3,2,1,0:T(8,128)S(1)}, u32[]{:S(2)}, u32[]{:S(2)}) %collective-permute-start) | collective-permute-done | bytes 32800 | tf_op jit(solution)/shard_map/ppermute | solution.py:409
  9.4 4.2 %local0.1 = (f32[32,16,1024]{2,1,0:T(8,128)S(1)}, f32[8,32,16,128]{3,2,1,0:T(8,128)S(1)}) custom-call(f32[2,2,32,128]{3,2,1,0:T(8,128)S(1)} %get-tuple-element.17.coef, f32[2,4,8,128]{3,2,1,0:T(8,128)S(1)} %collective-permute-done.packed, f32[8,32,16,128]{3,2,1,0:T(8,128)S(1)} %get-tuple-element.19.tiled, f32[32,2,16,1024]{3,2,1,0:T(8,128)} %noise_hbm.3), custom_call_target="tpu_custom_call" | custom-call | flops 41943040 | bytes 4194304 | tf_op jit(solution)/shard_map/local0/pallas_call | solution.py:495
  13.7 0.0 copy-start
  13.7 0.0 copy-start.1
  13.7 0.0 collective-permute-done.2.m2
  13.7 0.0 collective-permute-done.3.m3
  13.7 0.1 group_total.1.after
  13.8 3.0 %collective-permute-start.4 = (f32[8,1152]{1,0:T(8,128)S(1)}, f32[8,1152]{1,0:T(8,128)S(1)}, u32[]{:S(2)}, u32[]{:S(2)}) collective-permute-start(f32[8,1152]{1,0:T(8,128)S(1)} %fusion), channel_id=1, source_target_pairs={{0,8},{2,10},{4,12},{6,14},{8,0},{10,2},{12,4},{14,6},{1,9},{3,11}... | collective-permute-start | bytes 110600 | tf_op jit(solution)/shard_map/ppermute | solution.py:409
  16.9 0.7 %prepare.1 = (f32[2,2,32,128]{3,2,1,0:T(8,128)S(1)}, f32[16,1024]{1,0:T(8,128)S(1)}) custom-call(f32[2,2,32,128]{3,2,1,0:T(8,128)S(1)} %get-tuple-element.17.coef, s32[16,1024]{1,0:T(8,128)S(1)} %copy-done, f32[8]{0:T(128)S(1)} %copy-done.1, f32[2,8,1152]{2,1,0:T(8,128)S(1)} %group_total.1.after), custom_call_target="tpu_custom_call" | custom-call | flops 1048576 | bytes 1048576 | tf_op jit(solution)/shard_map/prepare/pallas_call | solution.py:515
  17.5 1.3 %collective-permute-done.4 = f32[8,1152]{1,0:T(8,128)S(1)} collective-permute-done((f32[8,1152]{1,0:T(8,128)S(1)}, f32[8,1152]{1,0:T(8,128)S(1)}, u32[]{:S(2)}, u32[]{:S(2)}) %collective-permute-start.4) | collective-permute-done | bytes 36896 | tf_op jit(solution)/shard_map/ppermute | solution.py:409
  18.8 0.1 enter_group.1
  18.9 2.3 %collective-permute-start.5 = (f32[2,8,1024]{2,1,0:T(8,128)S(1)}, f32[2,8,1024]{2,1,0:T(8,128)S(1)}, u32[]{:S(2)}, u32[]{:S(2)}) collective-permute-start(f32[2,8,1024]{2,1,0:T(8,128)S(1)} %get-tuple-element.29), channel_id=1, source_target_pairs={{0,2},{2,0},{4,6},{6,4},{8,10},{10,8},{12,14},{14,12},{1,3},{3,1},... | collective-permute-start | bytes 196616 | tf_op jit(solution)/shard_map/ppermute | solution.py:409
  21.2 1.2 %collective-permute-start.6 = (f32[2,8,1024]{2,1,0:T(8,128)S(1)}, f32[2,8,1024]{2,1,0:T(8,128)S(1)}, u32[]{:S(2)}, u32[]{:S(2)}) collective-permute-start(f32[2,8,1024]{2,1,0:T(8,128)S(1)} %get-tuple-element.30), channel_id=1, source_target_pairs={{0,4},{2,6},{4,0},{6,2},{8,12},{10,14},{12,8},{14,10},{1,5},{3,7},... | collective-permute-start | bytes 196616 | tf_op jit(solution)/shard_map/ppermute | solution.py:409
  22.4 0.4 %collective-permute-start.7 = (f32[2,8,1024]{2,1,0:T(8,128)S(1)}, f32[2,8,1024]{2,1,0:T(8,128)S(1)}, u32[]{:S(2)}, u32[]{:S(2)}) collective-permute-start(f32[2,8,1024]{2,1,0:T(8,128)S(1)} %get-tuple-element.31), channel_id=1, source_target_pairs={{0,6},{2,4},{4,2},{6,0},{8,14},{10,12},{12,10},{14,8},{1,7},{3,5},... | collective-permute-start | bytes 196616 | tf_op jit(solution)/shard_map/ppermute | solution.py:409
  22.8 4.1 %local1.1.after.g1 = f32[32,16,1024]{2,1,0:T(8,128)S(1)} custom-call(f32[2,2,32,128]{3,2,1,0:T(8,128)S(1)} %get-tuple-element.17.coef, f32[2,4,8,128]{3,2,1,0:T(8,128)S(1)} %collective-permute-done.packed, f32[8,32,16,128]{3,2,1,0:T(8,128)S(1)} %get-tuple-element.21.tiled, f32[2,8,1024]{2,1,0:T(8,128)S(1)} %get-tuple-element.27.after.m0), custom_call_target="tpu_custom_call" | custom-call | flops 41943040 | bytes 4194304 | tf_op jit(solution)/shard_map/local1/pallas_call | solution.py:540
  26.9 0.6 %collective-permute-done.7.m3 = f32[2,8,1024]{2,1,0:T(8,128)S(1)} collective-permute-done((f32[2,8,1024]{2,1,0:T(8,128)S(1)}, f32[2,8,1024]{2,1,0:T(8,128)S(1)}, u32[]{:S(2)}, u32[]{:S(2)}) %collective-permute-start.7) | collective-permute-done | bytes 65568 | tf_op jit(solution)/shard_map/ppermute | solution.py:409
  27.6 0.0 collective-permute-start.8
  27.6 0.7 %spread.1.own = f32[2,2,16,1024]{3,2,1,0:T(8,128)S(1)} custom-call(f32[2,8,1024]{2,1,0:T(8,128)S(1)} %get-tuple-element.27.after.m0, f32[2,8,1024]{2,1,0:T(8,128)S(1)} %collective-permute-done.5.m1, f32[2,8,1024]{2,1,0:T(8,128)S(1)} %collective-permute-done.6.m2, f32[2,8,1024]{2,1,0:T(8,128)S(1)} %collective-permute-done.7.m3, f32[4,2,8,128]{3,2,1,0:T(8,128)S(1)} %edges.1.after), custom_call_target="tpu_custom_call" | custom-call | flops 4194304 | bytes 1048576 | tf_op jit(solution)/shard_map/spread/pallas_call | solution.py:558
  28.3 0.5 %collective-permute-done.8.halo = f32[4,2,8,128]{3,2,1,0:T(8,128)S(1)} collective-permute-done((f32[4,2,8,128]{3,2,1,0:T(8,128)S(1)}, f32[4,2,8,128]{3,2,1,0:T(8,128)S(1)}, u32[]{:S(2)}, u32[]{:S(2)}) %collective-permute-start.8) | collective-permute-done | bytes 32800 | tf_op jit(solution)/shard_map/ppermute | solution.py:409
  28.8 3.2 %finish.1 = (f32[32,2,16,1024]{3,2,1,0:T(8,128)}, f32[32,16,1024]{2,1,0:T(8,128)}) custom-call(f32[32,16,1024]{2,1,0:T(8,128)S(1)} %get-tuple-element.20.after.g0, f32[32,16,1024]{2,1,0:T(8,128)S(1)} %local1.1.after.g1, f32[2,2,32,128]{3,2,1,0:T(8,128)S(1)} %get-tuple-element.26.after.reach, f32[16,1024]{1,0:T(8,128)S(1)} %get-tuple-element.28.bias, ...), custom_call_target="tpu_custom_call" | custom-call | tf_op jit(solution)/shard_map/finish/pallas_call | solution.py:573
  (13 shorter events, 0.1 us)
Async XLA Ops:
  3.6 10.1 %collective-permute-start.1 = (f32[2,8,1152]{2,1,0:T(8,128)S(1)}, f32[2,8,1152]{2,1,0:T(8,128)S(1)}, u32[]{:S(2)}, u32[]{:S(2)}) collective-permute-start(f32[2,8,1152]{2,1,0:T(8,128)S(1)} %get-tuple-element.23), channel_id=1, source_target_pairs={{0,2},{2,0},{4,6},{6,4},{8,10},{10,8},{12,14},{14,12},{1,3},{3,1},... | collective-permute-start | bytes 221192 | tf_op jit(solution)/shard_map/ppermute | solution.py:409
  6.6 7.1 %collective-permute-start.2 = (f32[2,8,1152]{2,1,0:T(8,128)S(1)}, f32[2,8,1152]{2,1,0:T(8,128)S(1)}, u32[]{:S(2)}, u32[]{:S(2)}) collective-permute-start(f32[2,8,1152]{2,1,0:T(8,128)S(1)} %get-tuple-element.24), channel_id=1, source_target_pairs={{0,4},{2,6},{4,0},{6,2},{8,12},{10,14},{12,8},{14,10},{1,5},{3,7},... | collective-permute-start | bytes 221192 | tf_op jit(solution)/shard_map/ppermute | solution.py:409
  8.2 5.5 %collective-permute-start.3 = (f32[2,8,1152]{2,1,0:T(8,128)S(1)}, f32[2,8,1152]{2,1,0:T(8,128)S(1)}, u32[]{:S(2)}, u32[]{:S(2)}) collective-permute-start(f32[2,8,1152]{2,1,0:T(8,128)S(1)} %get-tuple-element.25), channel_id=1, source_target_pairs={{0,6},{2,4},{4,2},{6,0},{8,14},{10,12},{12,10},{14,8},{1,7},{3,5},... | collective-permute-start | bytes 221192 | tf_op jit(solution)/shard_map/ppermute | solution.py:409
  8.2 1.2 %collective-permute-start = (f32[2,4,8,128]{3,2,1,0:T(8,128)S(1)}, f32[2,4,8,128]{3,2,1,0:T(8,128)S(1)}, u32[]{:S(2)}, u32[]{:S(2)}) collective-permute-start(f32[2,4,8,128]{3,2,1,0:T(8,128)S(1)} %get-tuple-element.18), channel_id=1, source_target_pairs={{0,1},{1,0},{2,3},{3,2},{4,5},{5,4},{6,7},{7,6},{8,9},{9,8},{10,11... | collective-permute-start | bytes 98312 | tf_op jit(solution)/shard_map/ppermute | solution.py:409
  13.7 3.2 %copy-start = (s32[16,1024]{1,0:T(8,128)S(1)}, s32[16,1024]{1,0:T(8,128)}, u32[]{:S(2)}) copy-start(s32[16,1024]{1,0:T(8,128)} %codes.1) | copy-start | bytes 196612
  13.7 3.2 %copy-start.1 = (f32[8]{0:T(128)S(1)}, f32[8]{0:T(128)}, u32[]{:S(2)}) copy-start(f32[8]{0:T(128)} %thresholds.1) | copy-start | bytes 100
  13.8 5.0 %collective-permute-start.4 = (f32[8,1152]{1,0:T(8,128)S(1)}, f32[8,1152]{1,0:T(8,128)S(1)}, u32[]{:S(2)}, u32[]{:S(2)}) collective-permute-start(f32[8,1152]{1,0:T(8,128)S(1)} %fusion), channel_id=1, source_target_pairs={{0,8},{2,10},{4,12},{6,14},{8,0},{10,2},{12,4},{14,6},{1,9},{3,11}... | collective-permute-start | bytes 110600 | tf_op jit(solution)/shard_map/ppermute | solution.py:409
  18.9 8.0 %collective-permute-start.5 = (f32[2,8,1024]{2,1,0:T(8,128)S(1)}, f32[2,8,1024]{2,1,0:T(8,128)S(1)}, u32[]{:S(2)}, u32[]{:S(2)}) collective-permute-start(f32[2,8,1024]{2,1,0:T(8,128)S(1)} %get-tuple-element.29), channel_id=1, source_target_pairs={{0,2},{2,0},{4,6},{6,4},{8,10},{10,8},{12,14},{14,12},{1,3},{3,1},... | collective-permute-start | bytes 196616 | tf_op jit(solution)/shard_map/ppermute | solution.py:409
  21.2 5.7 %collective-permute-start.6 = (f32[2,8,1024]{2,1,0:T(8,128)S(1)}, f32[2,8,1024]{2,1,0:T(8,128)S(1)}, u32[]{:S(2)}, u32[]{:S(2)}) collective-permute-start(f32[2,8,1024]{2,1,0:T(8,128)S(1)} %get-tuple-element.30), channel_id=1, source_target_pairs={{0,4},{2,6},{4,0},{6,2},{8,12},{10,14},{12,8},{14,10},{1,5},{3,7},... | collective-permute-start | bytes 196616 | tf_op jit(solution)/shard_map/ppermute | solution.py:409
  22.4 5.2 %collective-permute-start.7 = (f32[2,8,1024]{2,1,0:T(8,128)S(1)}, f32[2,8,1024]{2,1,0:T(8,128)S(1)}, u32[]{:S(2)}, u32[]{:S(2)}) collective-permute-start(f32[2,8,1024]{2,1,0:T(8,128)S(1)} %get-tuple-element.31), channel_id=1, source_target_pairs={{0,6},{2,4},{4,2},{6,0},{8,14},{10,12},{12,10},{14,8},{1,7},{3,5},... | collective-permute-start | bytes 196616 | tf_op jit(solution)/shard_map/ppermute | solution.py:409
  27.6 1.2 %collective-permute-start.8 = (f32[4,2,8,128]{3,2,1,0:T(8,128)S(1)}, f32[4,2,8,128]{3,2,1,0:T(8,128)S(1)}, u32[]{:S(2)}, u32[]{:S(2)}) collective-permute-start(f32[4,2,8,128]{3,2,1,0:T(8,128)S(1)} %edges.1.after), channel_id=1, source_target_pairs={{0,1},{1,0},{2,3},{3,2},{4,5},{5,4},{6,7},{7,6},{8,9},{9,8},{10,11... | collective-permute-start | bytes 98312 | tf_op jit(solution)/shard_map/ppermute | solution.py:409

commit v5 on v4

--- a/solution.py
+++ b/solution.py
@@ -215,19 +215,19 @@
     bias[...] = value
 
 
-def local_first(coef, packed, tiled, noise_hbm, out, tiled_next, buf, work, sems):
+def sweep_first(packed, tiled, noise_hbm, buf, tiled_next, work, sems):
     copies = [
         pltpu.make_async_copy(noise_hbm.at[:, 1, :, pl.ds(t * TILE, TILE)], tiled_next.at[t], sems.at[t])
         for t in range(tiled.shape[0])
     ]
     for copy in copies:
         copy.start()
-    local_field(0, coef, packed, tiled, None, out, buf, work)
+    sweep_field(0, packed, tiled, buf, work)
     for copy in copies:
         copy.wait()
 
 
-def local_field(field, coef, packed, tiled, after, out, buf, work):
+def sweep_field(field, packed, tiled, buf, work):
     tiles, levels, ys, _ = tiled.shape
     columns = tiles * TILE
     ranges = TILE // levels
@@ -289,6 +289,19 @@
             turned = work[SWEEPS % 2, y, main + b * TILE : main + (b + 1) * TILE, :].T
             for i, (c, g, at) in enumerate(pieces(y)):
                 flat[c * blocks + b, at, :] = turned[8 * i : 8 * i + 8]
+
+
+def filter_first(coef, mixed, after, out, buf):
+    filter_field(0, coef, mixed, buf, out)
+
+
+def local_field(field, coef, packed, tiled, after, out, buf, work):
+    sweep_field(field, packed, tiled, buf, work)
+    filter_field(field, coef, buf, buf, out)
+
+
+def filter_field(field, coef, mixed, buf, out):
+    tiles, levels, ys, _ = mixed.shape
     scale = 0.2**SWEEPS
     spots = [(t, top) for t in range(tiles) for top in range(ys // 8)]
 
@@ -296,7 +309,7 @@
         alpha, gain = row(coef, 0, field, level), row(coef, 1, field, level) * scale
         new = []
         for (t, top), old in zip(spots, state):
-            value = alpha * old + gain * buf[t, level, 8 * top : 8 * top + 8, :]
+            value = alpha * old + gain * mixed[t, level, 8 * top : 8 * top + 8, :]
             buf[t, level, 8 * top : 8 * top + 8, :] = value
             new.append(value)
         return tuple(new)
@@ -492,16 +505,16 @@
         pltpu.VMEM((tiles, levels, ys, TILE), F32),
         pltpu.VMEM((2, ys, columns * levels // TILE + 32, TILE), F32),
     ]
-    local0, tiled1 = pl.pallas_call(
-        local_first,
-        out_shape=[field_out, field_tiled],
-        in_specs=[VMEM, VMEM, VMEM, HBM],
+    mixed, tiled1 = pl.pallas_call(
+        sweep_first,
+        out_shape=[field_tiled] * 2,
+        in_specs=[VMEM, VMEM, HBM],
         out_specs=[VMEM] * 2,
-        scratch_shapes=[*scratch, pltpu.SemaphoreType.DMA((tiles,))],
+        scratch_shapes=[scratch[1], pltpu.SemaphoreType.DMA((tiles,))],
         compiler_params=params(45),
         cost_estimate=cost(40 * noise.size, 4 * noise.size),
-        name="local0",
-    )(coef, halo, tiled0, noise)
+        name="sweep0",
+    )(halo, tiled0, in_hbm(noise))
     held = pltpu.VMEM((GROUP, 2, 8, columns + TILE), F32)
     total = pl.pallas_call(
         group_total,
@@ -511,7 +524,17 @@
         scratch_shapes=[held],
         compiler_params=params(8),
         name="group_total",
-    )(*got, local0)
+    )(*got, mixed)
+    local0 = pl.pallas_call(
+        filter_first,
+        out_shape=field_out,
+        in_specs=[VMEM, VMEM, ANY],
+        out_specs=VMEM,
+        scratch_shapes=[scratch[0]],
+        compiler_params=params(16),
+        cost_estimate=cost(8 * noise.size, noise.size),
+        name="filter0",
+    )(coef, mixed, total)
     reach, bias = pl.pallas_call(
         prepare,
         out_shape=[
@@ -524,7 +547,7 @@
         compiler_params=params(4),
         cost_estimate=cost(noise.size, noise.size),
         name="prepare",
-    )(coef, facies_code, thresholds, total)
+    )(coef, facies_code, thresholds, local0)
     entering = entering_states(total, groups)
     state = jax.ShapeDtypeStruct((2, 8, columns), F32)
     own = pl.pallas_call(

time: 32.2 us -> 31.4 us (0.975)
  starting transfers between devices: 11.5 us -> 10.9 us
    ppermute x9, starting transfers between devices: 11.5 us -> 10.9 us  [xor_permute(): lax.ppermute(value, axis, [(i, i ^ by) for i in range(lax.axis_size(axis))])]
    pallas_call x1 -> x2, Pallas kernels: 4.24 us -> 4.01 us  [the longest x1 3.41 us: shards(): pl.pallas_call(sweep_first, out_shape=[field_tiled] * 2, in_specs=[VMEM,...]
where the time goes in v5:
time: 31.4 us; the launch traced here: 31.3 us
  Pallas kernels  15.9 us (51%)
  starting transfers between devices  10.9 us (35%)
  waiting for transfers between devices  3.46 us (11%)
  between operations  0.74 us (2%)
    ppermute x9, starting transfers between devices, xor_permute(): lax.ppermute(value, axis, [(i, i ^ by) for i in range(lax.axis_size(axis))])  10.9 us
    pallas_call x1, Pallas kernels, shards(): pl.pallas_call(functools.partial(local_field, 1), out_shape=field_out, in...  4.14 us
    ppermute x9, waiting for transfers between devices, xor_permute(): lax.ppermute(value, axis, [(i, i ^ by) for i in range(lax.axis_size(axis))])  3.46 us
    pallas_call x1, Pallas kernels, shards(): pl.pallas_call(sweep_first, out_shape=[field_tiled] * 2, in_specs=[VMEM,...  3.41 us
    pallas_call x1, Pallas kernels, shards(): pl.pallas_call(finish, out_shape=out, in_specs=[VMEM] * 6, out_specs=[ANY...  3.25 us
    pallas_call x1, Pallas kernels, shards(): pl.pallas_call(carries, out_shape=[message] * GROUP + [jax.ShapeDtypeStru...  2.94 us
    pallas_call x1, Pallas kernels, shards(): pl.pallas_call(spread, out_shape=jax.ShapeDtypeStruct((2, 2, ys, columns)...  0.72 us
    pallas_call x1, Pallas kernels, shards(): pl.pallas_call(prepare, out_shape=[jax.ShapeDtypeStruct((2, 2, levels, TI...  0.66 us
  transfers between devices with their start and end apart: 9, of which 4 were waited for; matrix products, arithmetic and copies ran while one was open for 0% of the time, Pallas kernels for 30%

profile of v5, /device:TPU:0, one launch (start us, length us, event | category | flops | bytes accessed | tf_op | source)
XLA Modules:
  0.0 31.3 jit_solution(2730083498785171813)
XLA Ops:
  0.6 2.9 %carries.1 = (f32[2,8,1152]{2,1,0:T(8,128)S(1)}, f32[2,8,1152]{2,1,0:T(8,128)S(1)}, f32[2,8,1152]{2,1,0:T(8,128)S(1)}, f32[2,8,1152]{2,1,0:T(8,128)S(1)}, f32[2,...) custom-call(s32[2,32]{1,0:T(2,128)} %bitcast.23, f32[16]{0:T(128)} %rates_hbm.1, ...), custom_call_target="tpu_custom_call" | custom-call | flops 4194304 | bytes 4194304 | tf_op jit(solution)/shard_map/carries/pallas_call | solution.py:475
  3.6 3.0 %collective-permute-start.1 = (f32[2,8,1152]{2,1,0:T(8,128)S(1)}, f32[2,8,1152]{2,1,0:T(8,128)S(1)}, u32[]{:S(2)}, u32[]{:S(2)}) collective-permute-start(f32[2,8,1152]{2,1,0:T(8,128)S(1)} %get-tuple-element.22), channel_id=1, source_target_pairs={{0,2},{2,0},{4,6},{6,4},{8,10},{10,8},{12,14},{14,12},{1,3},{3,1},... | collective-permute-start | bytes 221192 | tf_op jit(solution)/shard_map/ppermute | solution.py:422
  6.6 1.6 %collective-permute-start.2 = (f32[2,8,1152]{2,1,0:T(8,128)S(1)}, f32[2,8,1152]{2,1,0:T(8,128)S(1)}, u32[]{:S(2)}, u32[]{:S(2)}) collective-permute-start(f32[2,8,1152]{2,1,0:T(8,128)S(1)} %get-tuple-element.23), channel_id=1, source_target_pairs={{0,4},{2,6},{4,0},{6,2},{8,12},{10,14},{12,8},{14,10},{1,5},{3,7},... | collective-permute-start | bytes 221192 | tf_op jit(solution)/shard_map/ppermute | solution.py:422
  8.2 0.0 collective-permute-start.3
  8.2 0.0 collective-permute-start
  8.2 1.2 %collective-permute-done.packed = f32[2,4,8,128]{3,2,1,0:T(8,128)S(1)} collective-permute-done((f32[2,4,8,128]{3,2,1,0:T(8,128)S(1)}, f32[2,4,8,128]{3,2,1,0:T(8,128)S(1)}, u32[]{:S(2)}, u32[]{:S(2)}) %collective-permute-start) | collective-permute-done | bytes 32800 | tf_op jit(solution)/shard_map/ppermute | solution.py:422
  9.4 3.4 %sweep0.1 = (f32[8,32,16,128]{3,2,1,0:T(8,128)S(1)}, f32[8,32,16,128]{3,2,1,0:T(8,128)S(1)}) custom-call(f32[2,4,8,128]{3,2,1,0:T(8,128)S(1)} %collective-permute-done.packed, f32[8,32,16,128]{3,2,1,0:T(8,128)S(1)} %get-tuple-element.19.tiled, f32[32,2,16,1024]{3,2,1,0:T(8,128)} %noise_hbm.3), custom_call_target="tpu_custom_call" | custom-call | flops 41943040 | bytes 4194304 | tf_op jit(solution)/shard_map/sweep0/pallas_call | solution.py:508
  12.8 0.6 %collective-permute-done.3.m3 = f32[2,8,1152]{2,1,0:T(8,128)S(1)} collective-permute-done((f32[2,8,1152]{2,1,0:T(8,128)S(1)}, f32[2,8,1152]{2,1,0:T(8,128)S(1)}, u32[]{:S(2)}, u32[]{:S(2)}) %collective-permute-start.3) | collective-permute-done | bytes 73760 | tf_op jit(solution)/shard_map/ppermute | solution.py:422
  13.4 0.1 group_total.1.after
  13.6 2.7 %collective-permute-start.4 = (f32[8,1152]{1,0:T(8,128)S(1)}, f32[8,1152]{1,0:T(8,128)S(1)}, u32[]{:S(2)}, u32[]{:S(2)}) collective-permute-start(f32[8,1152]{1,0:T(8,128)S(1)} %fusion), channel_id=1, source_target_pairs={{0,8},{2,10},{4,12},{6,14},{8,0},{10,2},{12,4},{14,6},{1,9},{3,11}... | collective-permute-start | bytes 110600 | tf_op jit(solution)/shard_map/ppermute | solution.py:422
  16.2 0.6 %filter0.1.after.g0 = f32[32,16,1024]{2,1,0:T(8,128)S(1)} custom-call(f32[2,2,32,128]{3,2,1,0:T(8,128)S(1)} %get-tuple-element.17.coef, f32[8,32,16,128]{3,2,1,0:T(8,128)S(1)} %get-tuple-element.20.after.mixed, f32[2,8,1152]{2,1,0:T(8,128)S(1)} %group_total.1.after), custom_call_target="tpu_custom_call" | custom-call | flops 8388608 | bytes 1048576 | tf_op jit(solution)/shard_map/filter0/pallas_call | solution.py:528
  16.8 0.2 copy-done
  17.1 0.7 %prepare.1 = (f32[2,2,32,128]{3,2,1,0:T(8,128)S(1)}, f32[16,1024]{1,0:T(8,128)S(1)}) custom-call(f32[2,2,32,128]{3,2,1,0:T(8,128)S(1)} %get-tuple-element.17.coef, s32[16,1024]{1,0:T(8,128)S(1)} %copy-done, f32[8]{0:T(128)S(1)} %copy-done.1, f32[32,16,1024]{2,1,0:T(8,128)S(1)} %filter0.1.after.g0), custom_call_target="tpu_custom_call" | custom-call | flops 1048576 | bytes 1048576 | tf_op jit(solution)/shard_map/prepare/pallas_call | solution.py:538
  17.7 1.1 %collective-permute-done.4 = f32[8,1152]{1,0:T(8,128)S(1)} collective-permute-done((f32[8,1152]{1,0:T(8,128)S(1)}, f32[8,1152]{1,0:T(8,128)S(1)}, u32[]{:S(2)}, u32[]{:S(2)}) %collective-permute-start.4) | collective-permute-done | bytes 36896 | tf_op jit(solution)/shard_map/ppermute | solution.py:422
  18.9 0.1 enter_group.1
  19.0 1.4 %collective-permute-start.5 = (f32[2,8,1024]{2,1,0:T(8,128)S(1)}, f32[2,8,1024]{2,1,0:T(8,128)S(1)}, u32[]{:S(2)}, u32[]{:S(2)}) collective-permute-start(f32[2,8,1024]{2,1,0:T(8,128)S(1)} %get-tuple-element.29), channel_id=1, source_target_pairs={{0,2},{2,0},{4,6},{6,4},{8,10},{10,8},{12,14},{14,12},{1,3},{3,1},... | collective-permute-start | bytes 196616 | tf_op jit(solution)/shard_map/ppermute | solution.py:422
  20.4 1.2 %collective-permute-start.6 = (f32[2,8,1024]{2,1,0:T(8,128)S(1)}, f32[2,8,1024]{2,1,0:T(8,128)S(1)}, u32[]{:S(2)}, u32[]{:S(2)}) collective-permute-start(f32[2,8,1024]{2,1,0:T(8,128)S(1)} %get-tuple-element.30), channel_id=1, source_target_pairs={{0,4},{2,6},{4,0},{6,2},{8,12},{10,14},{12,8},{14,10},{1,5},{3,7},... | collective-permute-start | bytes 196616 | tf_op jit(solution)/shard_map/ppermute | solution.py:422
  21.6 1.0 %collective-permute-start.7 = (f32[2,8,1024]{2,1,0:T(8,128)S(1)}, f32[2,8,1024]{2,1,0:T(8,128)S(1)}, u32[]{:S(2)}, u32[]{:S(2)}) collective-permute-start(f32[2,8,1024]{2,1,0:T(8,128)S(1)} %get-tuple-element.31), channel_id=1, source_target_pairs={{0,6},{2,4},{4,2},{6,0},{8,14},{10,12},{12,10},{14,8},{1,7},{3,5},... | collective-permute-start | bytes 196616 | tf_op jit(solution)/shard_map/ppermute | solution.py:422
  22.6 4.1 %local1.1.after.g1 = f32[32,16,1024]{2,1,0:T(8,128)S(1)} custom-call(f32[2,2,32,128]{3,2,1,0:T(8,128)S(1)} %get-tuple-element.17.coef, f32[2,4,8,128]{3,2,1,0:T(8,128)S(1)} %collective-permute-done.packed, f32[8,32,16,128]{3,2,1,0:T(8,128)S(1)} %get-tuple-element.25.tiled, f32[2,8,1024]{2,1,0:T(8,128)S(1)} %get-tuple-element.27.after.m0), custom_call_target="tpu_custom_call" | custom-call | flops 41943040 | bytes 4194304 | tf_op jit(solution)/shard_map/local1/pallas_call | solution.py:563
  26.7 0.0 collective-permute-done.7.m3
  26.7 0.1 collective-permute-start.8
  26.8 0.7 %spread.1.own = f32[2,2,16,1024]{3,2,1,0:T(8,128)S(1)} custom-call(f32[2,8,1024]{2,1,0:T(8,128)S(1)} %get-tuple-element.27.after.m0, f32[2,8,1024]{2,1,0:T(8,128)S(1)} %collective-permute-done.5.m1, f32[2,8,1024]{2,1,0:T(8,128)S(1)} %collective-permute-done.6.m2, f32[2,8,1024]{2,1,0:T(8,128)S(1)} %collective-permute-done.7.m3, f32[4,2,8,128]{3,2,1,0:T(8,128)S(1)} %edges.1.after), custom_call_target="tpu_custom_call" | custom-call | flops 4194304 | bytes 1048576 | tf_op jit(solution)/shard_map/spread/pallas_call | solution.py:581
  27.6 0.5 %collective-permute-done.8.halo = f32[4,2,8,128]{3,2,1,0:T(8,128)S(1)} collective-permute-done((f32[4,2,8,128]{3,2,1,0:T(8,128)S(1)}, f32[4,2,8,128]{3,2,1,0:T(8,128)S(1)}, u32[]{:S(2)}, u32[]{:S(2)}) %collective-permute-start.8) | collective-permute-done | bytes 32800 | tf_op jit(solution)/shard_map/ppermute | solution.py:422
  28.0 3.2 %finish.1 = (f32[32,2,16,1024]{3,2,1,0:T(8,128)}, f32[32,16,1024]{2,1,0:T(8,128)}) custom-call(f32[32,16,1024]{2,1,0:T(8,128)S(1)} %filter0.1.after.g0, f32[32,16,1024]{2,1,0:T(8,128)S(1)} %local1.1.after.g1, f32[2,2,32,128]{3,2,1,0:T(8,128)S(1)} %get-tuple-element.26.after.reach, f32[16,1024]{1,0:T(8,128)S(1)} %get-tuple-element.28.bias, ...), custom_call_target="tpu_custom_call" | custom-call | tf_op jit(solution)/shard_map/finish/pallas_call | solution.py:596
  (14 shorter events, 0.1 us)
Async XLA Ops:
  3.6 9.2 %collective-permute-start.1 = (f32[2,8,1152]{2,1,0:T(8,128)S(1)}, f32[2,8,1152]{2,1,0:T(8,128)S(1)}, u32[]{:S(2)}, u32[]{:S(2)}) collective-permute-start(f32[2,8,1152]{2,1,0:T(8,128)S(1)} %get-tuple-element.22), channel_id=1, source_target_pairs={{0,2},{2,0},{4,6},{6,4},{8,10},{10,8},{12,14},{14,12},{1,3},{3,1},... | collective-permute-start | bytes 221192 | tf_op jit(solution)/shard_map/ppermute | solution.py:422
  6.6 6.2 %collective-permute-start.2 = (f32[2,8,1152]{2,1,0:T(8,128)S(1)}, f32[2,8,1152]{2,1,0:T(8,128)S(1)}, u32[]{:S(2)}, u32[]{:S(2)}) collective-permute-start(f32[2,8,1152]{2,1,0:T(8,128)S(1)} %get-tuple-element.23), channel_id=1, source_target_pairs={{0,4},{2,6},{4,0},{6,2},{8,12},{10,14},{12,8},{14,10},{1,5},{3,7},... | collective-permute-start | bytes 221192 | tf_op jit(solution)/shard_map/ppermute | solution.py:422
  8.2 5.3 %collective-permute-start.3 = (f32[2,8,1152]{2,1,0:T(8,128)S(1)}, f32[2,8,1152]{2,1,0:T(8,128)S(1)}, u32[]{:S(2)}, u32[]{:S(2)}) collective-permute-start(f32[2,8,1152]{2,1,0:T(8,128)S(1)} %get-tuple-element.24), channel_id=1, source_target_pairs={{0,6},{2,4},{4,2},{6,0},{8,14},{10,12},{12,10},{14,8},{1,7},{3,5},... | collective-permute-start | bytes 221192 | tf_op jit(solution)/shard_map/ppermute | solution.py:422
  8.2 1.2 %collective-permute-start = (f32[2,4,8,128]{3,2,1,0:T(8,128)S(1)}, f32[2,4,8,128]{3,2,1,0:T(8,128)S(1)}, u32[]{:S(2)}, u32[]{:S(2)}) collective-permute-start(f32[2,4,8,128]{3,2,1,0:T(8,128)S(1)} %get-tuple-element.18), channel_id=1, source_target_pairs={{0,1},{1,0},{2,3},{3,2},{4,5},{5,4},{6,7},{7,6},{8,9},{9,8},{10,11... | collective-permute-start | bytes 98312 | tf_op jit(solution)/shard_map/ppermute | solution.py:422
  13.6 5.3 %collective-permute-start.4 = (f32[8,1152]{1,0:T(8,128)S(1)}, f32[8,1152]{1,0:T(8,128)S(1)}, u32[]{:S(2)}, u32[]{:S(2)}) collective-permute-start(f32[8,1152]{1,0:T(8,128)S(1)} %fusion), channel_id=1, source_target_pairs={{0,8},{2,10},{4,12},{6,14},{8,0},{10,2},{12,4},{14,6},{1,9},{3,11}... | collective-permute-start | bytes 110600 | tf_op jit(solution)/shard_map/ppermute | solution.py:422
  16.2 0.8 %copy-start = (s32[16,1024]{1,0:T(8,128)S(1)}, s32[16,1024]{1,0:T(8,128)}, u32[]{:S(2)}) copy-start(s32[16,1024]{1,0:T(8,128)} %codes.1) | copy-start | bytes 196612
  16.2 0.8 %copy-start.1 = (f32[8]{0:T(128)S(1)}, f32[8]{0:T(128)}, u32[]{:S(2)}) copy-start(f32[8]{0:T(128)} %thresholds.1) | copy-start | bytes 100
  19.0 7.7 %collective-permute-start.5 = (f32[2,8,1024]{2,1,0:T(8,128)S(1)}, f32[2,8,1024]{2,1,0:T(8,128)S(1)}, u32[]{:S(2)}, u32[]{:S(2)}) collective-permute-start(f32[2,8,1024]{2,1,0:T(8,128)S(1)} %get-tuple-element.29), channel_id=1, source_target_pairs={{0,2},{2,0},{4,6},{6,4},{8,10},{10,8},{12,14},{14,12},{1,3},{3,1},... | collective-permute-start | bytes 196616 | tf_op jit(solution)/shard_map/ppermute | solution.py:422
  20.4 6.3 %collective-permute-start.6 = (f32[2,8,1024]{2,1,0:T(8,128)S(1)}, f32[2,8,1024]{2,1,0:T(8,128)S(1)}, u32[]{:S(2)}, u32[]{:S(2)}) collective-permute-start(f32[2,8,1024]{2,1,0:T(8,128)S(1)} %get-tuple-element.30), channel_id=1, source_target_pairs={{0,4},{2,6},{4,0},{6,2},{8,12},{10,14},{12,8},{14,10},{1,5},{3,7},... | collective-permute-start | bytes 196616 | tf_op jit(solution)/shard_map/ppermute | solution.py:422
  21.6 5.2 %collective-permute-start.7 = (f32[2,8,1024]{2,1,0:T(8,128)S(1)}, f32[2,8,1024]{2,1,0:T(8,128)S(1)}, u32[]{:S(2)}, u32[]{:S(2)}) collective-permute-start(f32[2,8,1024]{2,1,0:T(8,128)S(1)} %get-tuple-element.31), channel_id=1, source_target_pairs={{0,6},{2,4},{4,2},{6,0},{8,14},{10,12},{12,10},{14,8},{1,7},{3,5},... | collective-permute-start | bytes 196616 | tf_op jit(solution)/shard_map/ppermute | solution.py:422
  26.7 1.3 %collective-permute-start.8 = (f32[4,2,8,128]{3,2,1,0:T(8,128)S(1)}, f32[4,2,8,128]{3,2,1,0:T(8,128)S(1)}, u32[]{:S(2)}, u32[]{:S(2)}) collective-permute-start(f32[4,2,8,128]{3,2,1,0:T(8,128)S(1)} %edges.1.after), channel_id=1, source_target_pairs={{0,1},{1,0},{2,3},{3,2},{4,5},{5,4},{6,7},{7,6},{8,9},{9,8},{10,11... | collective-permute-start | bytes 98312 | tf_op jit(solution)/shard_map/ppermute | solution.py:422

commit v6 on v5

--- a/solution.py
+++ b/solution.py
@@ -295,9 +295,12 @@
     filter_field(0, coef, mixed, buf, out)
 
 
-def local_field(field, coef, packed, tiled, after, out, buf, work):
-    sweep_field(field, packed, tiled, buf, work)
-    filter_field(field, coef, buf, buf, out)
+def sweep_second(packed, tiled, after, buf, work):
+    sweep_field(1, packed, tiled, buf, work)
+
+
+def filter_second(coef, mixed, after, out, buf):
+    filter_field(1, coef, mixed, buf, out)
 
 
 def filter_field(field, coef, mixed, buf, out):
@@ -560,16 +563,16 @@
         name="enter_group",
     )(*got, entering, reach)
     states = [own[0]] + [xor_permute(own[k], "gz", k) for k in range(1, GROUP)]
-    local1 = pl.pallas_call(
-        functools.partial(local_field, 1),
-        out_shape=field_out,
-        in_specs=[VMEM, VMEM, VMEM, ANY],
+    mixed1 = pl.pallas_call(
+        sweep_second,
+        out_shape=field_tiled,
+        in_specs=[VMEM, VMEM, ANY],
         out_specs=VMEM,
-        scratch_shapes=scratch,
+        scratch_shapes=[scratch[1]],
         compiler_params=params(16),
         cost_estimate=cost(40 * noise.size, 4 * noise.size),
-        name="local1",
-    )(coef, halo, tiled1, own[0])
+        name="sweep1",
+    )(halo, tiled1, own[0])
     near = pl.pallas_call(
         edges,
         out_shape=jax.ShapeDtypeStruct((GROUP, 2, 8, TILE), F32),
@@ -577,7 +580,7 @@
         out_specs=VMEM,
         compiler_params=params(4),
         name="edges",
-    )(*states, local1)
+    )(*states, mixed1)
     spread_out = pl.pallas_call(
         spread,
         out_shape=jax.ShapeDtypeStruct((2, 2, ys, columns), F32),
@@ -588,6 +591,16 @@
         cost_estimate=cost(4 * noise.size, noise.size),
         name="spread",
     )(*states, near)
+    local1 = pl.pallas_call(
+        filter_second,
+        out_shape=field_out,
+        in_specs=[VMEM, VMEM, ANY],
+        out_specs=VMEM,
+        scratch_shapes=[scratch[0]],
+        compiler_params=params(16),
+        cost_estimate=cost(8 * noise.size, noise.size),
+        name="filter1",
+    )(coef, mixed1, near)
     near = xor_permute(near, "gx", 1)
     out = [
         jax.ShapeDtypeStruct(noise.shape, F32),

time: 31.4 us -> 31.6 us (level)
  waiting for transfers between devices: 3.46 us -> 3.81 us
    ppermute x9, waiting for transfers between devices: 3.46 us -> 3.81 us  [xor_permute(): lax.ppermute(value, axis, [(i, i ^ by) for i in range(lax.axis_size(axis))])]
    pallas_call x1 -> x2, Pallas kernels: 4.14 us -> 3.9 us  [the longest x1 3.31 us: shards(): pl.pallas_call(sweep_second, out_shape=field_tiled, in_specs=[VMEM, VMEM,...]
where the time goes in v6:
time: 31.6 us; the launch traced here: 31.4 us
  Pallas kernels  15.7 us (50%)
  starting transfers between devices  10.8 us (34%)
  waiting for transfers between devices  3.81 us (12%)
  between operations  0.76 us (2%)
    ppermute x9, starting transfers between devices, xor_permute(): lax.ppermute(value, axis, [(i, i ^ by) for i in range(lax.axis_size(axis))])  10.8 us
    ppermute x9, waiting for transfers between devices, xor_permute(): lax.ppermute(value, axis, [(i, i ^ by) for i in range(lax.axis_size(axis))])  3.81 us
    pallas_call x1, Pallas kernels, shards(): pl.pallas_call(sweep_first, out_shape=[field_tiled] * 2, in_specs=[VMEM,...  3.41 us
    pallas_call x1, Pallas kernels, shards(): pl.pallas_call(sweep_second, out_shape=field_tiled, in_specs=[VMEM, VMEM,...  3.31 us
    pallas_call x1, Pallas kernels, shards(): pl.pallas_call(finish, out_shape=out, in_specs=[VMEM] * 6, out_specs=[ANY...  3.27 us
    pallas_call x1, Pallas kernels, shards(): pl.pallas_call(carries, out_shape=[message] * GROUP + [jax.ShapeDtypeStru...  2.94 us
    pallas_call x1, Pallas kernels, shards(): pl.pallas_call(spread, out_shape=jax.ShapeDtypeStruct((2, 2, ys, columns)...  0.72 us
    pallas_call x1, Pallas kernels, shards(): pl.pallas_call(prepare, out_shape=[jax.ShapeDtypeStruct((2, 2, levels, TI...  0.66 us
  transfers between devices with their start and end apart: 9, of which 4 were waited for; matrix products, arithmetic and copies ran while one was open for 0% of the time, Pallas kernels for 30%

profile of v6, /device:TPU:0, one launch (start us, length us, event | category | flops | bytes accessed | tf_op | source)
XLA Modules:
  0.0 31.4 jit_solution(13386409646408383659)
XLA Ops:
  0.6 2.9 %carries.1 = (f32[2,8,1152]{2,1,0:T(8,128)S(1)}, f32[2,8,1152]{2,1,0:T(8,128)S(1)}, f32[2,8,1152]{2,1,0:T(8,128)S(1)}, f32[2,8,1152]{2,1,0:T(8,128)S(1)}, f32[2,...) custom-call(s32[2,32]{1,0:T(2,128)} %bitcast.23, f32[16]{0:T(128)} %rates_hbm.1, ...), custom_call_target="tpu_custom_call" | custom-call | flops 4194304 | bytes 4194304 | tf_op jit(solution)/shard_map/carries/pallas_call | solution.py:478
  3.6 3.0 %collective-permute-start.1 = (f32[2,8,1152]{2,1,0:T(8,128)S(1)}, f32[2,8,1152]{2,1,0:T(8,128)S(1)}, u32[]{:S(2)}, u32[]{:S(2)}) collective-permute-start(f32[2,8,1152]{2,1,0:T(8,128)S(1)} %get-tuple-element.22), channel_id=1, source_target_pairs={{0,2},{2,0},{4,6},{6,4},{8,10},{10,8},{12,14},{14,12},{1,3},{3,1},... | collective-permute-start | bytes 221192 | tf_op jit(solution)/shard_map/ppermute | solution.py:425
  6.6 1.6 %collective-permute-start.2 = (f32[2,8,1152]{2,1,0:T(8,128)S(1)}, f32[2,8,1152]{2,1,0:T(8,128)S(1)}, u32[]{:S(2)}, u32[]{:S(2)}) collective-permute-start(f32[2,8,1152]{2,1,0:T(8,128)S(1)} %get-tuple-element.23), channel_id=1, source_target_pairs={{0,4},{2,6},{4,0},{6,2},{8,12},{10,14},{12,8},{14,10},{1,5},{3,7},... | collective-permute-start | bytes 221192 | tf_op jit(solution)/shard_map/ppermute | solution.py:425
  8.2 0.0 collective-permute-start.3
  8.2 0.0 collective-permute-start
  8.2 1.2 %collective-permute-done.packed = f32[2,4,8,128]{3,2,1,0:T(8,128)S(1)} collective-permute-done((f32[2,4,8,128]{3,2,1,0:T(8,128)S(1)}, f32[2,4,8,128]{3,2,1,0:T(8,128)S(1)}, u32[]{:S(2)}, u32[]{:S(2)}) %collective-permute-start) | collective-permute-done | bytes 32800 | tf_op jit(solution)/shard_map/ppermute | solution.py:425
  9.4 3.4 %sweep0.1 = (f32[8,32,16,128]{3,2,1,0:T(8,128)S(1)}, f32[8,32,16,128]{3,2,1,0:T(8,128)S(1)}) custom-call(f32[2,4,8,128]{3,2,1,0:T(8,128)S(1)} %collective-permute-done.packed, f32[8,32,16,128]{3,2,1,0:T(8,128)S(1)} %get-tuple-element.19.tiled, f32[32,2,16,1024]{3,2,1,0:T(8,128)} %noise_hbm.3), custom_call_target="tpu_custom_call" | custom-call | flops 41943040 | bytes 4194304 | tf_op jit(solution)/shard_map/sweep0/pallas_call | solution.py:511
  12.8 0.6 %collective-permute-done.3.m3 = f32[2,8,1152]{2,1,0:T(8,128)S(1)} collective-permute-done((f32[2,8,1152]{2,1,0:T(8,128)S(1)}, f32[2,8,1152]{2,1,0:T(8,128)S(1)}, u32[]{:S(2)}, u32[]{:S(2)}) %collective-permute-start.3) | collective-permute-done | bytes 73760 | tf_op jit(solution)/shard_map/ppermute | solution.py:425
  13.4 0.1 group_total.1.after
  13.6 2.7 %collective-permute-start.4 = (f32[8,1152]{1,0:T(8,128)S(1)}, f32[8,1152]{1,0:T(8,128)S(1)}, u32[]{:S(2)}, u32[]{:S(2)}) collective-permute-start(f32[8,1152]{1,0:T(8,128)S(1)} %fusion), channel_id=1, source_target_pairs={{0,8},{2,10},{4,12},{6,14},{8,0},{10,2},{12,4},{14,6},{1,9},{3,11}... | collective-permute-start | bytes 110600 | tf_op jit(solution)/shard_map/ppermute | solution.py:425
  16.2 0.6 %filter0.1.after.g0 = f32[32,16,1024]{2,1,0:T(8,128)S(1)} custom-call(f32[2,2,32,128]{3,2,1,0:T(8,128)S(1)} %get-tuple-element.17.coef, f32[8,32,16,128]{3,2,1,0:T(8,128)S(1)} %get-tuple-element.20.after.mixed, f32[2,8,1152]{2,1,0:T(8,128)S(1)} %group_total.1.after), custom_call_target="tpu_custom_call" | custom-call | flops 8388608 | bytes 1048576 | tf_op jit(solution)/shard_map/filter0/pallas_call | solution.py:531
  16.8 0.2 copy-done
  17.1 0.7 %prepare.1 = (f32[2,2,32,128]{3,2,1,0:T(8,128)S(1)}, f32[16,1024]{1,0:T(8,128)S(1)}) custom-call(f32[2,2,32,128]{3,2,1,0:T(8,128)S(1)} %get-tuple-element.17.coef, s32[16,1024]{1,0:T(8,128)S(1)} %copy-done, f32[8]{0:T(128)S(1)} %copy-done.1, f32[32,16,1024]{2,1,0:T(8,128)S(1)} %filter0.1.after.g0), custom_call_target="tpu_custom_call" | custom-call | flops 1048576 | bytes 1048576 | tf_op jit(solution)/shard_map/prepare/pallas_call | solution.py:541
  17.7 1.1 %collective-permute-done.4 = f32[8,1152]{1,0:T(8,128)S(1)} collective-permute-done((f32[8,1152]{1,0:T(8,128)S(1)}, f32[8,1152]{1,0:T(8,128)S(1)}, u32[]{:S(2)}, u32[]{:S(2)}) %collective-permute-start.4) | collective-permute-done | bytes 36896 | tf_op jit(solution)/shard_map/ppermute | solution.py:425
  18.9 0.1 enter_group.1
  19.0 1.4 %collective-permute-start.5 = (f32[2,8,1024]{2,1,0:T(8,128)S(1)}, f32[2,8,1024]{2,1,0:T(8,128)S(1)}, u32[]{:S(2)}, u32[]{:S(2)}) collective-permute-start(f32[2,8,1024]{2,1,0:T(8,128)S(1)} %get-tuple-element.28), channel_id=1, source_target_pairs={{0,2},{2,0},{4,6},{6,4},{8,10},{10,8},{12,14},{14,12},{1,3},{3,1},... | collective-permute-start | bytes 196616 | tf_op jit(solution)/shard_map/ppermute | solution.py:425
  20.4 1.2 %collective-permute-start.6 = (f32[2,8,1024]{2,1,0:T(8,128)S(1)}, f32[2,8,1024]{2,1,0:T(8,128)S(1)}, u32[]{:S(2)}, u32[]{:S(2)}) collective-permute-start(f32[2,8,1024]{2,1,0:T(8,128)S(1)} %get-tuple-element.29), channel_id=1, source_target_pairs={{0,4},{2,6},{4,0},{6,2},{8,12},{10,14},{12,8},{14,10},{1,5},{3,7},... | collective-permute-start | bytes 196616 | tf_op jit(solution)/shard_map/ppermute | solution.py:425
  21.6 1.0 %collective-permute-start.7 = (f32[2,8,1024]{2,1,0:T(8,128)S(1)}, f32[2,8,1024]{2,1,0:T(8,128)S(1)}, u32[]{:S(2)}, u32[]{:S(2)}) collective-permute-start(f32[2,8,1024]{2,1,0:T(8,128)S(1)} %get-tuple-element.30), channel_id=1, source_target_pairs={{0,6},{2,4},{4,2},{6,0},{8,14},{10,12},{12,10},{14,8},{1,7},{3,5},... | collective-permute-start | bytes 196616 | tf_op jit(solution)/shard_map/ppermute | solution.py:425
  22.6 3.3 %sweep1.1.after.mixed = f32[8,32,16,128]{3,2,1,0:T(8,128)S(1)} custom-call(f32[2,4,8,128]{3,2,1,0:T(8,128)S(1)} %collective-permute-done.packed, f32[8,32,16,128]{3,2,1,0:T(8,128)S(1)} %get-tuple-element.25.tiled, f32[2,8,1024]{2,1,0:T(8,128)S(1)} %get-tuple-element.27.after.m0), custom_call_target="tpu_custom_call" | custom-call | flops 41943040 | bytes 4194304 | tf_op jit(solution)/shard_map/sweep1/pallas_call | solution.py:566
  25.9 0.0 collective-permute-done.6.m2
  25.9 0.8 %collective-permute-done.7.m3 = f32[2,8,1024]{2,1,0:T(8,128)S(1)} collective-permute-done((f32[2,8,1024]{2,1,0:T(8,128)S(1)}, f32[2,8,1024]{2,1,0:T(8,128)S(1)}, u32[]{:S(2)}, u32[]{:S(2)}) %collective-permute-start.7) | collective-permute-done | bytes 65568 | tf_op jit(solution)/shard_map/ppermute | solution.py:425
  26.8 0.7 %spread.1.own = f32[2,2,16,1024]{3,2,1,0:T(8,128)S(1)} custom-call(f32[2,8,1024]{2,1,0:T(8,128)S(1)} %get-tuple-element.27.after.m0, f32[2,8,1024]{2,1,0:T(8,128)S(1)} %collective-permute-done.5.m1, f32[2,8,1024]{2,1,0:T(8,128)S(1)} %collective-permute-done.6.m2, f32[2,8,1024]{2,1,0:T(8,128)S(1)} %collective-permute-done.7.m3, f32[4,2,8,128]{3,2,1,0:T(8,128)S(1)} %edges.1.after), custom_call_target="tpu_custom_call" | custom-call | flops 4194304 | bytes 1048576 | tf_op jit(solution)/shard_map/spread/pallas_call | solution.py:584
  27.5 0.6 %filter1.1.g1 = f32[32,16,1024]{2,1,0:T(8,128)S(1)} custom-call(f32[2,2,32,128]{3,2,1,0:T(8,128)S(1)} %get-tuple-element.17.coef, f32[8,32,16,128]{3,2,1,0:T(8,128)S(1)} %sweep1.1.after.mixed, f32[4,2,8,128]{3,2,1,0:T(8,128)S(1)} %edges.1.after), custom_call_target="tpu_custom_call" | custom-call | flops 8388608 | bytes 1048576 | tf_op jit(solution)/shard_map/filter1/pallas_call | solution.py:594
  28.1 3.3 %finish.1 = (f32[32,2,16,1024]{3,2,1,0:T(8,128)}, f32[32,16,1024]{2,1,0:T(8,128)}) custom-call(f32[32,16,1024]{2,1,0:T(8,128)S(1)} %filter0.1.after.g0, f32[32,16,1024]{2,1,0:T(8,128)S(1)} %filter1.1.g1, f32[2,2,32,128]{3,2,1,0:T(8,128)S(1)} %get-tuple-element.26.after.reach, f32[16,1024]{1,0:T(8,128)S(1)} %get-tuple-element.31.bias, ...), custom_call_target="tpu_custom_call" | custom-call | tf_op jit(solution)/shard_map/finish/pallas_call | solution.py:609
  (15 shorter events, 0.1 us)
Async XLA Ops:
  3.6 9.2 %collective-permute-start.1 = (f32[2,8,1152]{2,1,0:T(8,128)S(1)}, f32[2,8,1152]{2,1,0:T(8,128)S(1)}, u32[]{:S(2)}, u32[]{:S(2)}) collective-permute-start(f32[2,8,1152]{2,1,0:T(8,128)S(1)} %get-tuple-element.22), channel_id=1, source_target_pairs={{0,2},{2,0},{4,6},{6,4},{8,10},{10,8},{12,14},{14,12},{1,3},{3,1},... | collective-permute-start | bytes 221192 | tf_op jit(solution)/shard_map/ppermute | solution.py:425
  6.6 6.2 %collective-permute-start.2 = (f32[2,8,1152]{2,1,0:T(8,128)S(1)}, f32[2,8,1152]{2,1,0:T(8,128)S(1)}, u32[]{:S(2)}, u32[]{:S(2)}) collective-permute-start(f32[2,8,1152]{2,1,0:T(8,128)S(1)} %get-tuple-element.23), channel_id=1, source_target_pairs={{0,4},{2,6},{4,0},{6,2},{8,12},{10,14},{12,8},{14,10},{1,5},{3,7},... | collective-permute-start | bytes 221192 | tf_op jit(solution)/shard_map/ppermute | solution.py:425
  8.2 5.3 %collective-permute-start.3 = (f32[2,8,1152]{2,1,0:T(8,128)S(1)}, f32[2,8,1152]{2,1,0:T(8,128)S(1)}, u32[]{:S(2)}, u32[]{:S(2)}) collective-permute-start(f32[2,8,1152]{2,1,0:T(8,128)S(1)} %get-tuple-element.24), channel_id=1, source_target_pairs={{0,6},{2,4},{4,2},{6,0},{8,14},{10,12},{12,10},{14,8},{1,7},{3,5},... | collective-permute-start | bytes 221192 | tf_op jit(solution)/shard_map/ppermute | solution.py:425
  8.2 1.2 %collective-permute-start = (f32[2,4,8,128]{3,2,1,0:T(8,128)S(1)}, f32[2,4,8,128]{3,2,1,0:T(8,128)S(1)}, u32[]{:S(2)}, u32[]{:S(2)}) collective-permute-start(f32[2,4,8,128]{3,2,1,0:T(8,128)S(1)} %get-tuple-element.18), channel_id=1, source_target_pairs={{0,1},{1,0},{2,3},{3,2},{4,5},{5,4},{6,7},{7,6},{8,9},{9,8},{10,11... | collective-permute-start | bytes 98312 | tf_op jit(solution)/shard_map/ppermute | solution.py:425
  13.6 5.3 %collective-permute-start.4 = (f32[8,1152]{1,0:T(8,128)S(1)}, f32[8,1152]{1,0:T(8,128)S(1)}, u32[]{:S(2)}, u32[]{:S(2)}) collective-permute-start(f32[8,1152]{1,0:T(8,128)S(1)} %fusion), channel_id=1, source_target_pairs={{0,8},{2,10},{4,12},{6,14},{8,0},{10,2},{12,4},{14,6},{1,9},{3,11}... | collective-permute-start | bytes 110600 | tf_op jit(solution)/shard_map/ppermute | solution.py:425
  16.2 0.8 %copy-start = (s32[16,1024]{1,0:T(8,128)S(1)}, s32[16,1024]{1,0:T(8,128)}, u32[]{:S(2)}) copy-start(s32[16,1024]{1,0:T(8,128)} %codes.1) | copy-start | bytes 196612
  16.2 0.8 %copy-start.1 = (f32[8]{0:T(128)S(1)}, f32[8]{0:T(128)}, u32[]{:S(2)}) copy-start(f32[8]{0:T(128)} %thresholds.1) | copy-start | bytes 100
  19.0 6.9 %collective-permute-start.5 = (f32[2,8,1024]{2,1,0:T(8,128)S(1)}, f32[2,8,1024]{2,1,0:T(8,128)S(1)}, u32[]{:S(2)}, u32[]{:S(2)}) collective-permute-start(f32[2,8,1024]{2,1,0:T(8,128)S(1)} %get-tuple-element.28), channel_id=1, source_target_pairs={{0,2},{2,0},{4,6},{6,4},{8,10},{10,8},{12,14},{14,12},{1,3},{3,1},... | collective-permute-start | bytes 196616 | tf_op jit(solution)/shard_map/ppermute | solution.py:425
  20.4 5.5 %collective-permute-start.6 = (f32[2,8,1024]{2,1,0:T(8,128)S(1)}, f32[2,8,1024]{2,1,0:T(8,128)S(1)}, u32[]{:S(2)}, u32[]{:S(2)}) collective-permute-start(f32[2,8,1024]{2,1,0:T(8,128)S(1)} %get-tuple-element.29), channel_id=1, source_target_pairs={{0,4},{2,6},{4,0},{6,2},{8,12},{10,14},{12,8},{14,10},{1,5},{3,7},... | collective-permute-start | bytes 196616 | tf_op jit(solution)/shard_map/ppermute | solution.py:425
  21.6 5.2 %collective-permute-start.7 = (f32[2,8,1024]{2,1,0:T(8,128)S(1)}, f32[2,8,1024]{2,1,0:T(8,128)S(1)}, u32[]{:S(2)}, u32[]{:S(2)}) collective-permute-start(f32[2,8,1024]{2,1,0:T(8,128)S(1)} %get-tuple-element.30), channel_id=1, source_target_pairs={{0,6},{2,4},{4,2},{6,0},{8,14},{10,12},{12,10},{14,8},{1,7},{3,5},... | collective-permute-start | bytes 196616 | tf_op jit(solution)/shard_map/ppermute | solution.py:425
  26.7 1.3 %collective-permute-start.8 = (f32[4,2,8,128]{3,2,1,0:T(8,128)S(1)}, f32[4,2,8,128]{3,2,1,0:T(8,128)S(1)}, u32[]{:S(2)}, u32[]{:S(2)}) collective-permute-start(f32[4,2,8,128]{3,2,1,0:T(8,128)S(1)} %edges.1.after), channel_id=1, source_target_pairs={{0,1},{1,0},{2,3},{3,2},{4,5},{5,4},{6,7},{7,6},{8,9},{9,8},{10,11... | collective-permute-start | bytes 98312 | tf_op jit(solution)/shard_map/ppermute | solution.py:425
